TPU v7x, 256 devices: a whole 4x4x8 slice. The times are simulated.
256 devices in a mesh: facet: 32 (over x, z), uv: 8 (over y, core).
Axes of the slice: x: 4, y: 4, z: 8, core: 2. Of those that a mesh axis runs over, the one named last changes fastest.
Arguments:
- sky_image: bfloat16 [256, 65536], P('uv', 'facet'), may hold values from -6 to 6
- subgrid_offsets: int32 [32], replicated, may hold values from 0 to 2047
- owner_order: int32 [32], replicated, may hold values from 0 to 31, each once
- visibility_count: int32 [32], P('facet'), may hold values from 1 to 512, 8192 in all
- visibility_cell: int32 [32, 512], P('facet'), may hold values from 0 to 255
- observed: bfloat16 [32, 2, 256, 512], P('facet', None, 'uv'), may hold values from -6 to 6
- visibility_weight: float32 [32, 256, 512], P('facet', 'uv'), may hold values from 0.3 to 3
- row_kernel: float32 [7], replicated, may hold values from 0.3 to 1
- column_kernel: float32 [7], replicated, may hold values from 0.3 to 1
Outputs:
- weighted_residual: float32 [32, 2, 256, 512], P('facet', None, 'uv')
- dirty_image: float32 [256, 65536], P('uv', 'facet')
Inputs may be any that keep to these rules, and one draw needn't show every extreme that they name: `owner_order`: a permutation of the 32 subgrids over the slots. `visibility_count`: the counts sum to 8192, and some slot has exactly 512 live visibilities in every draw.
All inputs are finite; a program needn't handle non-finite values. No bound on the sum of `visibility_count` on one device may be relied on, other than what follows from the above.
Results may differ from a plain program's by a relative error of at most 0.022.
Values may be sent and summed in bfloat16 or wider, within the bound.
No kernel may reach another device: no remote copies, remote signals or barrier semaphores. Data moves between devices by JAX's collectives and lax.ppermute only.
A program may use at most 64 MiB of HBM per device.

v0:
```python
import math

import jax
import jax.numpy as jnp
from jax import lax
from jax.sharding import PartitionSpec as P

XC = 128
SG = 256


def padded_2(value, sides, width):
    for axis, dim in sides:
        count, length = (lax.axis_size(axis), value.shape[dim])
        up = [(i, (i + 1) % count) for i in range(count - 1)]
        down = [(j, i) for i, j in up]
        last = lax.slice_in_dim(value, length - width, length, axis=dim)
        first = lax.slice_in_dim(value, 0, width, axis=dim)
        before = lax.ppermute(last, axis, up)
        after = lax.ppermute(first, axis, down)
        value = jnp.concatenate([before, value, after], axis=dim)
    return value


def taper_values(strip_rows):
    position = jnp.arange(strip_rows, dtype=jnp.float32)
    return jnp.sin((position + 0.5) * (math.pi / strip_rows)) / math.sqrt(strip_rows)


def shift_values(slot_offsets, strip_rows):
    position = jnp.arange(strip_rows, dtype=jnp.int32)
    shifted = jnp.bitwise_and(slot_offsets[:, None] * position[None, :], strip_rows - 1)
    angle_shift = shifted.astype(jnp.float32) * (2.0 * math.pi / strip_rows)
    return jnp.stack([jnp.cos(angle_shift), -jnp.sin(angle_shift)], axis=1)


def base_tables(coarse, strip_rows):
    position = jnp.arange(strip_rows, dtype=jnp.int32)
    base = jnp.bitwise_and(
        jnp.arange(coarse, dtype=jnp.int32)[:, None] * position[None, :], strip_rows - 1
    )
    angle_base = base.astype(jnp.float32) * (2.0 * math.pi / strip_rows)
    cosine = jnp.cos(angle_base)
    sine_part = jnp.sin(angle_base)
    upper = jnp.stack([cosine, sine_part])
    lower = jnp.stack([-sine_part, cosine])
    return jnp.stack([upper, lower]).astype(jnp.bfloat16)


def expand_tables(facet, coarse, strip_rows, facet_count):
    grid_width = 2 * coarse
    image_rows = strip_rows * facet_count
    fine_index = jnp.arange(grid_width, dtype=jnp.int32)[:, None]
    coarse_index = jnp.arange(coarse, dtype=jnp.int32)[None, :]
    centre = (facet * strip_rows + strip_rows // 2)[..., None, None]
    product = jnp.bitwise_and(
        jnp.bitwise_and(fine_index * coarse_index, grid_width - 1) * (image_rows // grid_width)
        + (fine_index - 2 * coarse_index) * centre,
        image_rows - 1,
    )
    radians = product.astype(jnp.float32) * (2.0 * math.pi / image_rows)
    factor = 1.0 / math.sqrt(facet_count * coarse)
    cosine = jnp.cos(radians) * factor
    sine_part = jnp.sin(radians) * factor
    upper = jnp.stack([cosine, -sine_part], axis=-3)
    lower = jnp.stack([sine_part, cosine], axis=-3)
    return jnp.stack([upper, lower], axis=-4).astype(jnp.bfloat16)


def degrid_matrix(positions, kernel, grid_width):
    margin = (kernel.shape[0] - 1) // 2
    distance = jnp.arange(grid_width, dtype=jnp.int32)[None, :] - positions[:, None] + margin
    matrix = jnp.zeros(distance.shape, jnp.float32)
    for tap_index in range(kernel.shape[0]):
        matrix = matrix + jnp.where(distance == tap_index, kernel[tap_index], 0.0)
    return matrix.astype(jnp.bfloat16)


def convolve(padded, kernel, columns, flipped):
    tap_count = kernel.shape[0]
    result = jnp.zeros(padded.shape[:-2] + (columns, padded.shape[-1]), jnp.float32)
    for tap_index in range(tap_count):
        first_column = tap_count - 1 - tap_index if flipped else tap_index
        result = result + kernel[tap_index] * padded[..., first_column : first_column + columns, :]
    return result


def visibility_rows(degrid_table, grid_values, observed_slot, weights, live_count):
    model_rows = jnp.einsum(
        "vj,pcj->pcv", degrid_table, grid_values, preferred_element_type=jnp.float32
    )
    row_index = jnp.arange(degrid_table.shape[0], dtype=jnp.int32)
    live_rows = (row_index < live_count).astype(jnp.float32)
    residual = (
        live_rows[None, None, :]
        * weights[None, :, :]
        * (observed_slot.astype(jnp.float32) - model_rows)
    )
    gridded = jnp.einsum(
        "vj,pcv->pcj",
        degrid_table,
        residual.astype(jnp.bfloat16),
        preferred_element_type=jnp.float32,
    )
    return (residual, gridded)


def local(
    sky_image,
    subgrid_offsets,
    owner_order,
    visibility_count,
    visibility_cell,
    observed,
    visibility_weight,
    row_kernel,
    column_kernel,
):
    facet_count = lax.axis_size("facet")
    columns, strip_rows = sky_image.shape
    owned_slots = visibility_count.shape[0]
    slot_count = owned_slots * facet_count
    margin = (column_kernel.shape[0] - 1) // 2
    window_taper = taper_values(strip_rows)
    windowed = (sky_image.astype(jnp.float32) * window_taper[None, :]).astype(jnp.bfloat16)
    slot_offset = subgrid_offsets[owner_order]
    shift_table = shift_values(slot_offset, strip_rows)
    base_table = base_tables(XC, strip_rows)
    modulated = (
        shift_table[:, :, None, :] * windowed.astype(jnp.float32)[None, None, :, :]
    ).astype(jnp.bfloat16)
    contribution = jnp.einsum(
        "pqkr,iqcr->ipck", base_table, modulated, preferred_element_type=jnp.float32
    ).astype(jnp.bfloat16)
    all_tables = expand_tables(
        jnp.arange(facet_count, dtype=jnp.int32), XC, strip_rows, facet_count
    )
    arrived = lax.all_to_all(contribution, "facet", split_axis=0, concat_axis=0, tiled=True)
    arrived = arrived.reshape(facet_count, owned_slots, 2, columns, XC)
    subgrid = jnp.einsum(
        "fpqjk,fsqck->spcj", all_tables, arrived, preferred_element_type=jnp.float32
    )
    padded = padded_2(subgrid.astype(jnp.bfloat16), (("uv", 2),), margin).astype(subgrid.dtype)
    grid_values = convolve(padded, column_kernel, columns, False).astype(jnp.bfloat16)
    degrid_table = degrid_matrix(visibility_cell[0], row_kernel, SG)
    live_count = visibility_count[0]
    observed_slot = observed[0]
    weights = visibility_weight[0]
    target = grid_values[0]
    residual, gridded = visibility_rows(degrid_table, target, observed_slot, weights, live_count)
    residual_parts = [residual]
    gridded_parts = [gridded]
    residuals = jnp.stack(residual_parts)
    gridded = jnp.stack(gridded_parts)
    padded_back = padded_2(gridded.astype(jnp.bfloat16), (("uv", 2),), margin).astype(gridded.dtype)
    back_grid = convolve(padded_back, column_kernel, columns, True).astype(jnp.bfloat16)
    every_table = expand_tables(
        jnp.arange(facet_count, dtype=jnp.int32), XC, strip_rows, facet_count
    )
    outgoing = jnp.einsum(
        "fqpjk,sqcj->fspck", every_table, back_grid, preferred_element_type=jnp.float32
    ).astype(jnp.bfloat16)
    back_pieces = lax.all_to_all(
        outgoing.reshape(slot_count, 2, columns, XC),
        "facet",
        split_axis=0,
        concat_axis=0,
        tiled=True,
    )
    back_rows = jnp.einsum(
        "pqkr,ipck->iqcr", base_table, back_pieces, preferred_element_type=jnp.float32
    )
    dirty_sum = jnp.einsum("iqr,iqcr->cr", shift_table, back_rows)
    return (residuals, dirty_sum * window_taper[None, :])


def solution(mesh):
    in_specs = (
        P("uv", "facet"),
        P(),
        P(),
        P("facet"),
        P("facet", None),
        P("facet", None, "uv", None),
        P("facet", "uv", None),
        P(),
        P(),
    )
    out_specs = (P("facet", None, "uv", None), P("uv", "facet"))
    return jax.shard_map(local, mesh=mesh, in_specs=in_specs, out_specs=out_specs, check_vma=False)
```

profile of v0, /device:TPU:48, one launch (start us, length us, event | category | flops | bytes accessed | tf_op | source)
XLA Modules:
  0.0 121.2 jit_solution(11928801770138537708)
XLA Ops:
  0.7 3.9 %negate_convert_fusion.1 = (bf16[1,128,2048]{2,1,0:T(8,128)(2,1)S(1)}, bf16[1,128,2048]{2,1,0:T(8,128)(2,1)S(1)}) fusion(), kind=kLoop, calls=%fused_computation.37 | loop fusion | flops 1835008 | bytes 1048576 | tf_op jit(solution)/shard_map/convert.12
  4.6 3.6 %fusion.36 = bf16[1,128,2048]{2,1,0:T(8,128)(2,1)S(1)} fusion(), kind=kLoop, calls=%fused_computation.41 | loop fusion | flops 1310720 | bytes 524288 | tf_op jit(solution)/shard_map/convert.16
  8.9 0.7 gather_fusion
  9.6 1.0 fusion.55
  11.4 1.1 copy-done.3
  12.4 3.2 %fusion.24 = bf16[32,2,32,128]{3,2,1,0:T(8,128)(2,1)} fusion(f32[32,2048]{1,0:T(8,128)S(1)} %fusion.56, f32[32,2,2048]{2,1,0:T(2,128)S(1)} %copy.13, bf16[1,2,128,2048]{3,2,1,0:T(8,128)(2,1)S(1)} %get-tuple-element.7, bf16[1,2,128,2048]{3,2,1,0:T(8,128)(2,1)S(1)} %get-tuple-element.6), kind=kOutput, calls=%fused_computation.26 | convolution fusion | flops 2160328704 | bytes 3407872 | tf_op jit(solution)/shard_map/pqkr,iqcr->ipck/dot_general | solution.py:132
  15.6 11.2 %all-to-all-start = ((bf16[32,2,32,128]{3,2,1,0:T(8,128)(2,1)}), bf16[32,2,32,128]{3,2,1,0:T(8,128)(2,1)S(1)}, u32[]{:S(2)}, u32[]{:S(2)}) async-start(bf16[32,2,32,128]{3,2,1,0:T(8,128)(2,1)} %fusion.24), calls=%async_computation | async-start | bytes 1048576 | tf_op jit(solution)/shard_map/all_to_all | solution.py:138
  28.2 16.2 %negate_convert_fusion = (bf16[32,1,256,128]{3,2,1,0:T(8,128)(2,1)S(1)}, bf16[32,1,256,128]{3,2,1,0:T(8,128)(2,1)S(1)}, bf16[32,1,256,128]{3,2,1,0:T(8,128)(2,1)S(1)}) fusion(s32[32]{0:T(128)S(1)} %multiply_add_fusion, s32[256,128]{1,0:T(8,128)S(1)} %get-tuple-element.31, s32[256,128]{1,0:T(8,128)S(1)} %get-tuple-element.32), kind=kLoop, calls=%fused_computation.13 | loop fusion | flops 11534336 | bytes 6553728 | tf_op jit(solution)/shard_map/convert.8
  44.4 3.6 %maximum_bitcast_fusion = (bf16[32,1,2,256,128]{4,3,2,1,0:T(8,128)(2,1)}, bf16[32,1,2,256,128]{4,3,2,1,0:T(8,128)(2,1)}) fusion(bf16[32,1,256,128]{3,2,1,0:T(8,128)(2,1)S(1)} %get-tuple-element.8, bf16[32,1,256,128]{3,2,1,0:T(8,128)(2,1)S(1)} %get-tuple-element.10, bf16[32,1,256,128]{3,2,1,0:T(8,128)(2,1)S(1)} %get-tuple-element.9), kind=kLoop, calls=%fused_computation.11 | loop fusion | flops 4194304 | bytes 14680064 | tf_op jit(solution)/shard_map/stack | solution.py:67
  48.1 5.0 %fusion.34 = bf16[1,2,32,256]{3,2,1,0:T(8,128)(2,1)S(1)} fusion(bf16[32,1,2,256,128]{4,3,2,1,0:T(8,128)(2,1)} %get-tuple-element.3, bf16[32,1,2,256,128]{4,3,2,1,0:T(8,128)(2,1)} %get-tuple-element.2, bf16[32,2,32,128]{3,2,1,0:T(8,128)(2,1)S(1)} %all-to-all-done), kind=kOutput, calls=%fused_computation.34 | convolution fusion | flops 285229056 | bytes 8945664 | tf_op jit(solution)/shard_map/fpqjk,fsqck->spcj/dot_general | solution.py:140
  53.0 1.9 %collective-permute-start = (bf16[1,2,3,256]{3,2,1,0:T(4,128)(2,1)S(1)}, bf16[1,2,3,256]{3,2,1,0:T(4,128)(2,1)S(1)}, u32[]{:S(2)}, u32[]{:S(2)}) collective-permute-start(bf16[1,2,3,256]{3,2,1,0:T(4,128)(2,1)S(1)} %get-tuple-element.13), channel_id=1, source_target_pairs={{0,1},{1,2},{2,3},{3,4},{4,5},{5,6},{6,7},{8,9},{9,10},{10,11},{11... | collective-permute-start | bytes 9224 | tf_op jit(solution)/shard_map/ppermute | solution.py:19
  55.0 3.9 %collective-permute-start.1 = (bf16[1,2,3,256]{3,2,1,0:T(4,128)(2,1)S(1)}, bf16[1,2,3,256]{3,2,1,0:T(4,128)(2,1)S(1)}, u32[]{:S(2)}, u32[]{:S(2)}) collective-permute-start(bf16[1,2,3,256]{3,2,1,0:T(4,128)(2,1)S(1)} %get-tuple-element.14), channel_id=1, source_target_pairs={{1,0},{2,1},{3,2},{4,3},{5,4},{6,5},{7,6},{9,8},{10,9},{11,10},{12... | collective-permute-start | bytes 9224 | tf_op jit(solution)/shard_map/ppermute | solution.py:20
  58.9 0.7 fusion.111
  60.2 9.4 %fusion.30 = f32[2,32,512]{2,1,0:T(8,128)S(1)} fusion(f32[]{:T(128)} %bitcast.38, f32[]{:T(128)} %bitcast.37, f32[]{:T(128)} %bitcast.36, f32[]{:T(128)} %bitcast.35, f32[]{:T(128)} %bitcast.34, f32[]{:T(128)} %bitcast.33, f32[]{:T(128)} %bitcast.32, s32[512]{0:T(512)S(1)} %bitcast.133, bf16[1,2,32,512]{3,2,1,0:T(8,128)(2,1)S(1)} %copy-done.9, ...), kind=kOutput, calls=%fused_computation.29 | convolution fusion | flops 20119552 | bytes 723000 | tf_op jit(solution)/shard_map/vj,pcj->pcv/dot_general | solution.py:89
  69.7 5.0 %fusion.33 = bf16[1,2,32,256]{3,2,1,0:T(8,128)(2,1)S(1)} fusion(f32[]{:T(128)} %bitcast.38, f32[]{:T(128)} %bitcast.37, f32[]{:T(128)} %bitcast.36, f32[]{:T(128)} %bitcast.35, f32[]{:T(128)} %bitcast.34, f32[]{:T(128)} %bitcast.33, f32[]{:T(128)} %bitcast.32, s32[512]{0:T(512)S(1)} %bitcast.134, f32[2,32,512]{2,1,0:T(8,128)S(1)} %fusion.30), kind=kOutput, calls=%fused_computation.33 | convolution fusion | flops 19841024 | bytes 165916 | tf_op jit(solution)/shard_map/vj,pcv->pcj/dot_general | solution.py:99
  74.7 3.3 %collective-permute-start.2 = (bf16[1,2,3,256]{3,2,1,0:T(4,128)(2,1)S(1)}, bf16[1,2,3,256]{3,2,1,0:T(4,128)(2,1)S(1)}, u32[]{:S(2)}, u32[]{:S(2)}) collective-permute-start(bf16[1,2,3,256]{3,2,1,0:T(4,128)(2,1)S(1)} %get-tuple-element.11), channel_id=1, source_target_pairs={{0,1},{1,2},{2,3},{3,4},{4,5},{5,6},{6,7},{8,9},{9,10},{10,11},{11... | collective-permute-start | bytes 9224 | tf_op jit(solution)/shard_map/ppermute | solution.py:19
  77.9 2.3 %collective-permute-start.3 = (bf16[1,2,3,256]{3,2,1,0:T(4,128)(2,1)S(1)}, bf16[1,2,3,256]{3,2,1,0:T(4,128)(2,1)S(1)}, u32[]{:S(2)}, u32[]{:S(2)}) collective-permute-start(bf16[1,2,3,256]{3,2,1,0:T(4,128)(2,1)S(1)} %get-tuple-element.12), channel_id=1, source_target_pairs={{1,0},{2,1},{3,2},{4,3},{5,4},{6,5},{7,6},{9,8},{10,9},{11,10},{12... | collective-permute-start | bytes 9224 | tf_op jit(solution)/shard_map/ppermute | solution.py:20
  80.3 1.3 %collective-permute-done.3 = bf16[1,2,3,256]{3,2,1,0:T(4,128)(2,1)S(1)} collective-permute-done((bf16[1,2,3,256]{3,2,1,0:T(4,128)(2,1)S(1)}, bf16[1,2,3,256]{3,2,1,0:T(4,128)(2,1)S(1)}, u32[]{:S(2)}, u32[]{:S(2)}) %collective-permute-start.3) | collective-permute-done | bytes 3104 | tf_op jit(solution)/shard_map/ppermute | solution.py:20
  81.6 6.8 %fusion.29 = bf16[32,2,32,128]{3,2,1,0:T(8,128)(2,1)} fusion(bf16[32,1,2,256,128]{4,3,2,1,0:T(8,128)(2,1)S(1)} %copy-done.2, bf16[32,1,2,256,128]{4,3,2,1,0:T(8,128)(2,1)S(1)} %copy-done.1, f32[1,2,38,256]{3,2,1,0:T(8,128)S(1)} %maximum_convert_fusion.1, f32[]{:T(128)} %bitcast.29, f32[]{:T(128)} %bitcast.28, f32[]{:T(128)} %bitcast.27, f32[]{:T(128)} %bitcast.26, ...), kind=kOutput, calls=%fused_computation.27 | convolution fusion | flops 285704192 | bytes 9371676 | tf_op jit(solution)/shard_map/fqpjk,sqcj->fspck/dot_general | solution.py:160
  88.4 9.8 %all-to-all-start.1 = ((bf16[32,2,32,128]{3,2,1,0:T(8,128)(2,1)}), bf16[32,2,32,128]{3,2,1,0:T(8,128)(2,1)S(1)}, u32[]{:S(2)}, u32[]{:S(2)}) async-start(bf16[32,2,32,128]{3,2,1,0:T(8,128)(2,1)} %fusion.29), calls=%async_computation.1 | async-start | bytes 1048576 | tf_op jit(solution)/shard_map/all_to_all | solution.py:163
  98.2 1.2 %copy.31 = f32[2048,32,2]{0,2,1:T(2,128)} copy(f32[2048,32,2]{0,1,2:T(8,128)S(1)} %get-tuple-element.4) | data formatting | bytes 1048576
  99.5 17.4 %all-to-all-done.1 = bf16[32,2,32,128]{3,2,1,0:T(8,128)(2,1)S(1)} async-done(((bf16[32,2,32,128]{3,2,1,0:T(8,128)(2,1)}), bf16[32,2,32,128]{3,2,1,0:T(8,128)(2,1)S(1)}, u32[]{:S(2)}, u32[]{:S(2)}) %all-to-all-start.1) | async-done | bytes 524320 | tf_op jit(solution)/shard_map/all_to_all | solution.py:163
  116.9 3.6 %fusion = f32[2048,32]{0,1:T(8,128)S(1)} fusion(f32[2048,32,2]{0,2,1:T(2,128)} %copy.31, bf16[32,2,32,128]{3,2,1,0:T(8,128)(2,1)S(1)} %all-to-all-done.1, bf16[1,2,128,2048]{3,2,1,0:T(8,128)(2,1)S(1)} %copy-done.4, bf16[1,2,128,2048]{3,2,1,0:T(8,128)(2,1)S(1)} %get-tuple-element.6), kind=kOutput, calls=%fused_computation.2 | convolution fusion | flops 2156855296 | bytes 3407872 | tf_op jit(solution)/shard_map/pqkr,ipck->iqcr/dot_general | solution.py:170
  120.4 0.7 multiply_bitcast_fusion
  (44 shorter events, 2.9 us)
Async XLA Ops:
  0.6 8.2 %copy-start = (s32[32]{0:T(128)S(1)}, s32[32]{0:T(128)}, u32[]{:S(2)}) copy-start(s32[32]{0:T(128)} %param.10) | copy-start | bytes 388
  0.6 10.5 %copy-start.5 = (bf16[32,2048]{1,0:T(8,128)(2,1)S(1)}, bf16[32,2048]{1,0:T(8,128)(2,1)}, u32[]{:S(2)}) copy-start(bf16[32,2048]{1,0:T(8,128)(2,1)} %param.9) | copy-start | bytes 393220
  11.3 1.1 copy-start.3
  12.4 14.4 %copy-start.7 = (f32[7]{0:T(128)S(1)}, f32[7]{0:T(128)}, u32[]{:S(2)}) copy-start(f32[7]{0:T(128)} %param.17) | copy-start | bytes 88
  12.4 15.7 %copy-start.6 = (f32[1,32,512]{2,1,0:T(8,128)S(1)}, f32[1,32,512]{2,1,0:T(8,128)}, u32[]{:S(2)}) copy-start(f32[1,32,512]{2,1,0:T(8,128)} %param.15) | copy-start | bytes 196612
  15.6 32.5 %all-to-all-start = ((bf16[32,2,32,128]{3,2,1,0:T(8,128)(2,1)}), bf16[32,2,32,128]{3,2,1,0:T(8,128)(2,1)S(1)}, u32[]{:S(2)}, u32[]{:S(2)}) async-start(bf16[32,2,32,128]{3,2,1,0:T(8,128)(2,1)} %fusion.24), calls=%async_computation | async-start | bytes 1048576 | tf_op jit(solution)/shard_map/all_to_all | solution.py:138
  48.0 10.9 %copy-start.8 = (f32[7]{0:T(128)S(1)}, f32[7]{0:T(128)}, u32[]{:S(2)}) copy-start(f32[7]{0:T(128)} %param.16) | copy-start | bytes 88
  48.0 12.2 %copy-start.9 = (bf16[1,2,32,512]{3,2,1,0:T(8,128)(2,1)S(1)}, bf16[1,2,32,512]{3,2,1,0:T(8,128)(2,1)}, u32[]{:S(2)}) copy-start(bf16[1,2,32,512]{3,2,1,0:T(8,128)(2,1)} %param.14) | copy-start | bytes 196612
  48.1 12.2 %copy-start.10 = (s32[1,512]{1,0:T(1,128)S(1)}, s32[1,512]{1,0:T(1,128)}, u32[]{:S(2)}) copy-start(s32[1,512]{1,0:T(1,128)} %param.13) | copy-start | bytes 6148
  53.0 6.6 %collective-permute-start = (bf16[1,2,3,256]{3,2,1,0:T(4,128)(2,1)S(1)}, bf16[1,2,3,256]{3,2,1,0:T(4,128)(2,1)S(1)}, u32[]{:S(2)}, u32[]{:S(2)}) collective-permute-start(bf16[1,2,3,256]{3,2,1,0:T(4,128)(2,1)S(1)} %get-tuple-element.13), channel_id=1, source_target_pairs={{0,1},{1,2},{2,3},{3,4},{4,5},{5,6},{6,7},{8,9},{9,10},{10,11},{11... | collective-permute-start | bytes 9224 | tf_op jit(solution)/shard_map/ppermute | solution.py:19
  55.0 26.6 %copy-start.1 = (bf16[32,1,2,256,128]{4,3,2,1,0:T(8,128)(2,1)S(1)}, bf16[32,1,2,256,128]{4,3,2,1,0:T(8,128)(2,1)}, u32[]{:S(2)}) copy-start(bf16[32,1,2,256,128]{4,3,2,1,0:T(8,128)(2,1)} %get-tuple-element.2) | copy-start | bytes 12582916
  55.0 26.6 %copy-start.2 = (bf16[32,1,2,256,128]{4,3,2,1,0:T(8,128)(2,1)S(1)}, bf16[32,1,2,256,128]{4,3,2,1,0:T(8,128)(2,1)}, u32[]{:S(2)}) copy-start(bf16[32,1,2,256,128]{4,3,2,1,0:T(8,128)(2,1)} %get-tuple-element.3) | copy-start | bytes 12582916
  55.0 5.2 %collective-permute-start.1 = (bf16[1,2,3,256]{3,2,1,0:T(4,128)(2,1)S(1)}, bf16[1,2,3,256]{3,2,1,0:T(4,128)(2,1)S(1)}, u32[]{:S(2)}, u32[]{:S(2)}) collective-permute-start(bf16[1,2,3,256]{3,2,1,0:T(4,128)(2,1)S(1)} %get-tuple-element.14), channel_id=1, source_target_pairs={{1,0},{2,1},{3,2},{4,3},{5,4},{6,5},{7,6},{9,8},{10,9},{11,10},{12... | collective-permute-start | bytes 9224 | tf_op jit(solution)/shard_map/ppermute | solution.py:20
  69.7 18.8 %copy-start.11 = (f32[2,32,512]{2,1,0:T(8,128)}, f32[2,32,512]{2,1,0:T(8,128)S(1)}, u32[]{:S(2)}) copy-start(f32[2,32,512]{2,1,0:T(8,128)S(1)} %fusion.30) | copy-start | bytes 393220
  74.7 5.6 %collective-permute-start.2 = (bf16[1,2,3,256]{3,2,1,0:T(4,128)(2,1)S(1)}, bf16[1,2,3,256]{3,2,1,0:T(4,128)(2,1)S(1)}, u32[]{:S(2)}, u32[]{:S(2)}) collective-permute-start(bf16[1,2,3,256]{3,2,1,0:T(4,128)(2,1)S(1)} %get-tuple-element.11), channel_id=1, source_target_pairs={{0,1},{1,2},{2,3},{3,4},{4,5},{5,6},{6,7},{8,9},{9,10},{10,11},{11... | collective-permute-start | bytes 9224 | tf_op jit(solution)/shard_map/ppermute | solution.py:19
  77.9 3.6 %collective-permute-start.3 = (bf16[1,2,3,256]{3,2,1,0:T(4,128)(2,1)S(1)}, bf16[1,2,3,256]{3,2,1,0:T(4,128)(2,1)S(1)}, u32[]{:S(2)}, u32[]{:S(2)}) collective-permute-start(bf16[1,2,3,256]{3,2,1,0:T(4,128)(2,1)S(1)} %get-tuple-element.12), channel_id=1, source_target_pairs={{1,0},{2,1},{3,2},{4,3},{5,4},{6,5},{7,6},{9,8},{10,9},{11,10},{12... | collective-permute-start | bytes 9224 | tf_op jit(solution)/shard_map/ppermute | solution.py:20
  81.6 35.3 %copy-start.4 = (bf16[1,2,128,2048]{3,2,1,0:T(8,128)(2,1)S(1)}, bf16[1,2,128,2048]{3,2,1,0:T(8,128)(2,1)}, u32[]{:S(2)}) copy-start(bf16[1,2,128,2048]{3,2,1,0:T(8,128)(2,1)} %copy-done.3) | copy-start | bytes 3145732
  88.4 28.4 %all-to-all-start.1 = ((bf16[32,2,32,128]{3,2,1,0:T(8,128)(2,1)}), bf16[32,2,32,128]{3,2,1,0:T(8,128)(2,1)S(1)}, u32[]{:S(2)}, u32[]{:S(2)}) async-start(bf16[32,2,32,128]{3,2,1,0:T(8,128)(2,1)} %fusion.29), calls=%async_computation.1 | async-start | bytes 1048576 | tf_op jit(solution)/shard_map/all_to_all | solution.py:163
where the time goes:
time: 122 us; the launch traced here: 121 us
  matrix products  32.9 us (27%)
  starting transfers between devices  32.4 us (27%)
  other arithmetic  30.1 us (25%)
  waiting for transfers between devices  19.3 us (16%)
  local copies, waits for them, and re-layouts  4.81 us (4%)
  between operations  1.61 us (1%)
    another operation x3, other arithmetic  23.6 us
    all_to_all x1, waiting for transfers between devices, local(): lax.all_to_all(outgoing.reshape(slot_count, 2, columns, XC), 'facet', spl...  17.4 us
    all_to_all x1, starting transfers between devices, local(): lax.all_to_all(contribution, 'facet', split_axis=0, concat_axis=0, tiled=...  11.2 us
    all_to_all x1, starting transfers between devices, local(): lax.all_to_all(outgoing.reshape(slot_count, 2, columns, XC), 'facet', spl...  9.78 us
    dot_general x1, matrix products, visibility_rows(): jnp.einsum('vj,pcj->pcv', degrid_table, grid_values, preferred_element_ty...  9.42 us
    dot_general x1, matrix products, local(): jnp.einsum('fqpjk,sqcj->fspck', every_table, back_grid, preferred_element...  6.84 us
    ppermute x2, starting transfers between devices, padded_2(): after = lax.ppermute(first, axis, down)  6.2 us
    ppermute x2, starting transfers between devices, padded_2(): before = lax.ppermute(last, axis, up)  5.18 us
  transfers between devices with their start and end apart: 6, of which 3 were waited for; matrix products, arithmetic and copies ran while one was open for 19% of the time, Pallas kernels for 0%

commit v1 on v0

v1 whole, which is shorter than its diff:
```python
import functools
import math

import jax
import jax.numpy as jnp
import numpy as np
from jax import lax
from jax.experimental import pallas as pl
from jax.experimental.pallas import tpu as pltpu
from jax.sharding import PartitionSpec as P

FR = 2048
XC = 128
SG = 256
NF = 32
CB = 32
CE = 40
TAPS = 7
VM = 512
EXT = 3968
BF = jnp.bfloat16
F32 = jnp.float32


def facet_table():
    s = np.arange(EXT)[:, None] + 64
    k = np.arange(XC)[None, :]
    a = 2.0 * np.pi * ((s * k) % FR) / FR
    return np.concatenate([np.cos(a), -np.sin(a)], axis=1).astype(np.float32)


def subgrid_table():
    j = np.arange(SG)[None, :]
    k = np.arange(XC)[:, None]
    a = 2.0 * np.pi * ((j * k) % SG) / SG
    c, s = np.cos(a) / 64.0, np.sin(a) / 64.0
    return np.block([[c, s], [-s, c]]).astype(np.float32)


def facet_phase():
    f = np.arange(NF)[:, None]
    j = np.arange(SG)[None, :]
    a = 2.0 * np.pi * ((j * (2 * f + 1)) % 64) / 64
    return np.stack([np.cos(a), np.sin(a)]).astype(np.float32)


def window():
    r = np.arange(FR)
    return (np.sin((r + 0.5) * np.pi / FR) / math.sqrt(FR)).astype(np.float32)[None, :]


def turn(n):
    q = (n + 256) >> 9
    x = (n - (q << 9)).astype(F32) * (math.pi / 1024.0)
    y = x * x
    c = 1.0 + y * (-0.5 + y * (1.0 / 24 + y * (-1.0 / 720 + y * (1.0 / 40320))))
    s = x * (1.0 + y * (-1.0 / 6 + y * (1.0 / 120 + y * (-1.0 / 5040 + y * (1.0 / 362880)))))
    odd = (q & 1) == 1
    cos = jnp.where(odd, s, c)
    sin = jnp.where(odd, c, s)
    cos = jnp.where(((q + 1) & 2) == 2, -cos, cos)
    sin = jnp.where((q & 2) == 2, -sin, sin)
    return cos, sin


def shifts(offs_ref, order_ref, sh_ref):
    row = lax.broadcasted_iota(jnp.int32, (NF, 128), 0)
    off = jnp.zeros((NF, 128), jnp.int32)
    for i in range(NF):
        off = jnp.where(row == i, offs_ref[order_ref[i]], off)
    for b in range(FR // 128):
        r = lax.broadcasted_iota(jnp.int32, (NF, 128), 1) + 128 * b
        c, s = turn((off * r) & (FR - 1))
        sh_ref[0, :, 128 * b : 128 * (b + 1)] = c
        sh_ref[1, :, 128 * b : 128 * (b + 1)] = s


def halo_rows(after, before, axis):
    row = lax.broadcasted_iota(jnp.int32, after.shape, axis)
    return jnp.where(row < 3, after, jnp.where(row >= 5, before, jnp.zeros_like(after)))


def k1_body(
    offs_ref, order_ref, ck_ref, fm_ref, sky_ref, before_ref, after_ref, win_ref, tab_hbm,
    out_ref, tab_ref, ext_ref, conv_ref, sh_ref, lhs_ref, sem,
):
    start = pl.multiple_of(fm_ref[0] * 128, 128)
    copy = pltpu.make_async_copy(tab_hbm.at[pl.ds(start, FR), :], tab_ref, sem)
    copy.start()
    shifts(offs_ref, order_ref, sh_ref)
    win = win_ref[...]
    ext_ref[8:16, :] = before_ref[...].astype(F32) * win
    ext_ref[16:48, :] = sky_ref[...].astype(F32) * win
    ext_ref[48:56, :] = after_ref[...].astype(F32) * win
    own = jnp.zeros((CB, FR), F32)
    lo = jnp.zeros((8, FR), F32)
    hi = jnp.zeros((8, FR), F32)
    for t in range(TAPS):
        k = ck_ref[t]
        own = own + k * ext_ref[13 + t : 45 + t, :]
        lo = lo + k * ext_ref[5 + t : 13 + t, :]
        hi = hi + k * ext_ref[45 + t : 53 + t, :]
    conv_ref[0:CB, :] = own
    conv_ref[CB:CE, :] = halo_rows(hi, lo, 0)
    copy.wait()

    def chunk(g, _):
        for h in range(4):
            i = g * 8 + 2 * h
            for q in range(2):
                for b in range(4):
                    lanes = slice(512 * b, 512 * (b + 1))
                    w = conv_ref[:, lanes]
                    x = w * sh_ref[q, pl.ds(i, 1), lanes]
                    y = w * sh_ref[q, pl.ds(i + 1, 1), lanes]
                    lhs_ref[q * 320 + 80 * h : q * 320 + 80 * (h + 1), lanes] = jnp.concatenate(
                        [x, y], axis=0
                    ).astype(BF)
        u = jnp.dot(lhs_ref[...], tab_ref[...], preferred_element_type=F32)
        re = u[:320, :XC] + u[320:, XC:]
        im = u[:320, XC:] - u[320:, :XC]
        for s in range(8):
            out_ref[g * 8 + s, 0] = re[s * CE : (s + 1) * CE].astype(BF)
            out_ref[g * 8 + s, 1] = im[s * CE : (s + 1) * CE].astype(BF)
        return 0

    lax.fori_loop(0, 4, chunk, 0)


SMEM = pl.BlockSpec(memory_space=pltpu.SMEM)
VMEM = pl.BlockSpec(memory_space=pltpu.VMEM)
ANY = pl.BlockSpec(memory_space=pl.ANY)


def k1(offs, order, ck, fm, sky, before, after):
    return pl.pallas_call(
        k1_body,
        out_shape=jax.ShapeDtypeStruct((NF, 2, CE, XC), BF),
        in_specs=[SMEM, SMEM, SMEM, SMEM, VMEM, VMEM, VMEM, VMEM, ANY],
        out_specs=VMEM,
        scratch_shapes=[
            pltpu.VMEM((FR, 2 * XC), BF),
            pltpu.VMEM((64, FR), F32),
            pltpu.VMEM((CE, FR), F32),
            pltpu.VMEM((2, NF, FR), F32),
            pltpu.VMEM((640, FR), BF),
            pltpu.SemaphoreType.DMA,
        ],
        name="facet_to_slots",
    )(offs, order, ck, fm, sky, before, after, window(), jnp.asarray(facet_table(), BF))


def k2_body(
    count_ref, rk_ref, ck_ref, arr_ref, cell_ref, obs_ref, obs_b_ref, obs_a_ref,
    wt_ref, wt_b_ref, wt_a_ref, w_ref, wt_tab_ref, ph_ref,
    res_ref, out_ref, u_ref, dt_ref, ext_ref, y_ref,
):
    cell = cell_ref[...]
    d = lax.broadcasted_iota(jnp.int32, (SG, VM), 0) - cell + 3
    m = jnp.zeros((SG, VM), F32)
    for t in range(TAPS):
        m = jnp.where(d == t, rk_ref[t], m)
    dt_ref[...] = m.astype(BF)

    re = jnp.zeros((CE, SG), F32)
    im = jnp.zeros((CE, SG), F32)
    for g in range(8):
        lhs = jnp.concatenate(
            [
                jnp.concatenate([arr_ref[4 * g + h, 0], arr_ref[4 * g + h, 1]], axis=1)
                for h in range(4)
            ],
            axis=0,
        )
        u = jnp.dot(lhs, w_ref[...], preferred_element_type=F32)
        for h in range(4):
            ur = u[h * CE : (h + 1) * CE, :SG]
            ui = u[h * CE : (h + 1) * CE, SG:]
            pc = ph_ref[0, 4 * g + h : 4 * g + h + 1, :]
            ps = ph_ref[1, 4 * g + h : 4 * g + h + 1, :]
            re = re + (ur * pc - ui * ps)
            im = im + (ur * ps + ui * pc)
    grid = jnp.concatenate([re, im], axis=0).astype(BF)
    model = jnp.dot(grid, dt_ref[...], preferred_element_type=F32)

    live = (lax.broadcasted_iota(jnp.int32, (1, VM), 1) < count_ref[0]).astype(F32)
    wt = wt_ref[...] * live
    wt_h = halo_rows(wt_a_ref[...], wt_b_ref[...], 0) * live
    parts = []
    for p in range(2):
        own = wt * (obs_ref[p].astype(F32) - model[p * CE : p * CE + CB])
        res_ref[p] = own
        obs_h = halo_rows(obs_a_ref[p].astype(F32), obs_b_ref[p].astype(F32), 0)
        parts += [own, wt_h * (obs_h - model[p * CE + CB : (p + 1) * CE])]
    rr = jnp.concatenate(parts, axis=0).astype(BF)
    gridded = lax.dot_general(
        rr, dt_ref[...], (((1,), (1,)), ((), ())), preferred_element_type=F32
    )
    backs = []
    for p in range(2):
        halo = gridded[p * CE + CB : (p + 1) * CE]
        ext_ref[p, 0:8, :] = halo
        ext_ref[p, 8:40, :] = gridded[p * CE : p * CE + CB]
        ext_ref[p, 40:48, :] = halo
        b = jnp.zeros((CB, SG), F32)
        for t in range(TAPS):
            b = b + ck_ref[t] * ext_ref[p, 11 - t : 43 - t, :]
        backs.append(b)
    br, bi = backs
    for g in range(8):
        for h in range(4):
            pc = ph_ref[0, 4 * g + h : 4 * g + h + 1, :]
            ps = ph_ref[1, 4 * g + h : 4 * g + h + 1, :]
            y_ref[h * CB : (h + 1) * CB, :SG] = (br * pc + bi * ps).astype(BF)
            y_ref[h * CB : (h + 1) * CB, SG:] = (bi * pc - br * ps).astype(BF)
        z = jnp.dot(y_ref[...], wt_tab_ref[...], preferred_element_type=F32)
        for h in range(4):
            out_ref[4 * g + h, 0] = z[h * CB : (h + 1) * CB, :XC].astype(BF)
            out_ref[4 * g + h, 1] = z[h * CB : (h + 1) * CB, XC:].astype(BF)


def k2(count, rk, ck, arrived, cell, obs, obs_b, obs_a, wt, wt_b, wt_a):
    tab = subgrid_table()
    return pl.pallas_call(
        k2_body,
        out_shape=(
            jax.ShapeDtypeStruct((2, CB, VM), F32),
            jax.ShapeDtypeStruct((NF, 2, CB, XC), BF),
        ),
        in_specs=[SMEM, SMEM, SMEM] + [VMEM] * 11,
        out_specs=(VMEM, VMEM),
        scratch_shapes=[
            pltpu.VMEM((8, 128), F32),
            pltpu.VMEM((SG, VM), BF),
            pltpu.VMEM((2, 48, SG), F32),
            pltpu.VMEM((4 * CB, 2 * SG), BF),
        ],
        name="slot_round_trip",
    )(
        count, rk, ck, arrived, cell, obs, obs_b, obs_a, wt, wt_b, wt_a,
        jnp.asarray(tab, BF), jnp.asarray(tab.T, BF), facet_phase(),
    )


def k3_body(
    offs_ref, order_ref, fm_ref, bp_ref, win_ref, tab_hbm, out_ref, tab_ref, sh_ref, lhs_ref, sem
):
    start = pl.multiple_of(fm_ref[0] * 128, 128)
    copy = pltpu.make_async_copy(tab_hbm.at[:, pl.ds(start, FR)], tab_ref, sem)
    copy.start()
    shifts(offs_ref, order_ref, sh_ref)
    for i in range(NF):
        a = bp_ref[i, 0]
        b = bp_ref[i, 1]
        lhs_ref[i * CB : (i + 1) * CB, :] = jnp.concatenate([a, b], axis=1)
        lhs_ref[1024 + i * CB : 1024 + (i + 1) * CB, :] = jnp.concatenate([b, -a], axis=1)
    copy.wait()

    def tile(n, _):
        lanes = pl.ds(pl.multiple_of(n * 256, 256), 256)
        z = jnp.dot(lhs_ref[...], tab_ref[:, lanes], preferred_element_type=F32)
        acc = jnp.zeros((CB, 256), F32)
        for i in range(NF):
            c = sh_ref[0, i : i + 1, lanes]
            s = sh_ref[1, i : i + 1, lanes]
            acc = acc + (c * z[i * CB : (i + 1) * CB] - s * z[1024 + i * CB : 1024 + (i + 1) * CB])
        out_ref[:, lanes] = acc * win_ref[:, lanes]
        return 0

    lax.fori_loop(0, FR // 256, tile, 0)


def k3(offs, order, fm, bp):
    return pl.pallas_call(
        k3_body,
        out_shape=jax.ShapeDtypeStruct((CB, FR), F32),
        in_specs=[SMEM, SMEM, SMEM, VMEM, VMEM, ANY],
        out_specs=VMEM,
        scratch_shapes=[
            pltpu.VMEM((2 * XC, FR), BF),
            pltpu.VMEM((2, NF, FR), F32),
            pltpu.VMEM((2048, 2 * XC), BF),
            pltpu.SemaphoreType.DMA,
        ],
        name="slots_to_facet",
    )(offs, order, fm, bp, window(), jnp.asarray(facet_table().T, BF))


def neighbours(first, last):
    n = lax.axis_size("uv")
    up = [(i, i + 1) for i in range(n - 1)]
    down = [(i + 1, i) for i in range(n - 1)]
    return lax.ppermute(last, "uv", up), lax.ppermute(first, "uv", down)


def local(
    sky_image, subgrid_offsets, owner_order, visibility_count, visibility_cell, observed,
    visibility_weight, row_kernel, column_kernel,
):
    fm = (lax.axis_index("facet") % 16).astype(jnp.int32).reshape(1)
    obs = observed[0]
    wt = visibility_weight[0]
    sky_b, sky_a = neighbours(sky_image[:8], sky_image[24:])
    obs_b, obs_a = neighbours(obs[:, :8], obs[:, 24:])
    wt_b, wt_a = neighbours(wt[:8], wt[24:])
    out = k1(subgrid_offsets, owner_order, column_kernel, fm, sky_image, sky_b, sky_a)
    arrived = lax.all_to_all(out, "facet", split_axis=0, concat_axis=0, tiled=True)
    res, outgoing = k2(
        visibility_count, row_kernel, column_kernel, arrived, visibility_cell,
        obs, obs_b, obs_a, wt, wt_b, wt_a,
    )
    back = lax.all_to_all(outgoing, "facet", split_axis=0, concat_axis=0, tiled=True)
    dirty = k3(subgrid_offsets, owner_order, fm, back)
    return (res[None], dirty)


def solution(mesh):
    in_specs = (
        P("uv", "facet"),
        P(),
        P(),
        P("facet"),
        P("facet", None),
        P("facet", None, "uv", None),
        P("facet", "uv", None),
        P(),
        P(),
    )
    out_specs = (P("facet", None, "uv", None), P("uv", "facet"))
    return jax.shard_map(local, mesh=mesh, in_specs=in_specs, out_specs=out_specs, check_vma=False)
```

time: 122 us -> 83.7 us (0.69)
  matrix products: 32.9 us -> 0 us
  other arithmetic: 30.1 us -> 0 us
  blocking collectives: 0 us -> 23.4 us
  Pallas kernels: 0 us -> 17.2 us
  waiting for transfers between devices: 19.3 us -> 10.9 us
  starting transfers between devices: 32.4 us -> 27.9 us
  local copies, waits for them, and re-layouts: 4.81 us -> 2.26 us
    dot_general x6 -> x0, matrix products: 32.9 us -> none  [the longest x1 9.42 us: visibility_rows(): jnp.einsum('vj,pcj->pcv', degrid_table, grid_values, preferred_element_ty...]
    another operation x5 -> x0, other arithmetic: 27.5 us -> none
    all_to_all x0 -> x1, blocking collectives: none -> 23.4 us  [local(): lax.all_to_all(outgoing, 'facet', split_axis=0, concat_axis=0, tiled=True)]
    pallas_call x0 -> x3, Pallas kernels: none -> 17.2 us  [the longest x1 6.55 us: k3(): pl.pallas_call(k3_body, out_shape=jax.ShapeDtypeStruct((CB, FR), F32), in...]
    all_to_all x2 -> x1, starting transfers between devices: 21 us -> 11.2 us  [local(): lax.all_to_all(out, 'facet', split_axis=0, concat_axis=0, tiled=True)]
    all_to_all x2 -> x1, waiting for transfers between devices: 17.4 us -> 8.65 us  [local(): lax.all_to_all(out, 'facet', split_axis=0, concat_axis=0, tiled=True)]
    ppermute x4 -> x6, starting transfers between devices: 11.4 us -> 16.7 us  [neighbours(): return (lax.ppermute(last, 'uv', up), lax.ppermute(first, 'uv', down))]
  transfers between devices with their start and end apart: 6 -> 7, of which waited for: 3 -> 3; matrix products, arithmetic and copies ran while one was open for 19% -> 0% of each run, Pallas kernels for 0% -> 0%
where the time goes in v1:
time: 83.7 us; the launch traced here: 83.1 us
  starting transfers between devices  27.9 us (33%)
  blocking collectives  23.4 us (28%)
  Pallas kernels  17.2 us (21%)
  waiting for transfers between devices  10.9 us (13%)
  local copies, waits for them, and re-layouts  2.26 us (3%)
  between operations  1.47 us (2%)
    all_to_all x1, blocking collectives, local(): lax.all_to_all(outgoing, 'facet', split_axis=0, concat_axis=0, tiled=True)  23.4 us
    ppermute x6, starting transfers between devices, neighbours(): return (lax.ppermute(last, 'uv', up), lax.ppermute(first, 'uv', down))  16.7 us
    all_to_all x1, starting transfers between devices, local(): lax.all_to_all(out, 'facet', split_axis=0, concat_axis=0, tiled=True)  11.2 us
    all_to_all x1, waiting for transfers between devices, local(): lax.all_to_all(out, 'facet', split_axis=0, concat_axis=0, tiled=True)  8.65 us
    pallas_call x1, Pallas kernels, k3(): pl.pallas_call(k3_body, out_shape=jax.ShapeDtypeStruct((CB, FR), F32), in...  6.55 us
    pallas_call x1, Pallas kernels, k1(): pl.pallas_call(k1_body, out_shape=jax.ShapeDtypeStruct((NF, 2, CE, XC), B...  6.44 us
    pallas_call x1, Pallas kernels, k2(): pl.pallas_call(k2_body, out_shape=(jax.ShapeDtypeStruct((2, CB, VM), F32)...  4.2 us
    ppermute x6, waiting for transfers between devices, neighbours(): return (lax.ppermute(last, 'uv', up), lax.ppermute(first, 'uv', down))  2.26 us
  transfers between devices with their start and end apart: 7, of which 3 were waited for; matrix products, arithmetic and copies ran while one was open for 0% of the time, Pallas kernels for 0%

profile of v1, /device:TPU:48, one launch (start us, length us, event | category | flops | bytes accessed | tf_op | source)
XLA Modules:
  0.0 83.1 jit_solution(5776844780633532327)
XLA Ops:
  0.6 0.8 fusion
  1.4 1.9 %collective-permute-start = (bf16[8,2048]{1,0:T(8,128)(2,1)S(1)}, bf16[8,2048]{1,0:T(8,128)(2,1)S(1)}, u32[]{:S(2)}, u32[]{:S(2)}) collective-permute-start(bf16[8,2048]{1,0:T(8,128)(2,1)S(1)} %get-tuple-element.7), channel_id=1, source_target_pairs={{0,1},{1,2},{2,3},{3,4},{4,5},{5,6},{6,7},{8,9},{9,10},{10,11},{11... | collective-permute-start | bytes 98312 | tf_op jit(solution)/shard_map/ppermute | solution.py:293
  3.3 3.6 %collective-permute-start.1 = (bf16[8,2048]{1,0:T(8,128)(2,1)S(1)}, bf16[8,2048]{1,0:T(8,128)(2,1)S(1)}, u32[]{:S(2)}, u32[]{:S(2)}) collective-permute-start(bf16[8,2048]{1,0:T(8,128)(2,1)S(1)} %get-tuple-element.6), channel_id=1, source_target_pairs={{1,0},{2,1},{3,2},{4,3},{5,4},{6,5},{7,6},{9,8},{10,9},{11,10},{12... | collective-permute-start | bytes 98312 | tf_op jit(solution)/shard_map/ppermute | solution.py:293
  7.0 0.0 collective-permute-done.before_ref
  7.0 0.0 copy-start.3
  7.0 1.5 %collective-permute-done.1.after_ref = bf16[8,2048]{1,0:T(8,128)(2,1)S(1)} collective-permute-done((bf16[8,2048]{1,0:T(8,128)(2,1)S(1)}, bf16[8,2048]{1,0:T(8,128)(2,1)S(1)}, u32[]{:S(2)}, u32[]{:S(2)}) %collective-permute-start.1) | collective-permute-done | bytes 32800 | tf_op jit(solution)/shard_map/ppermute | solution.py:293
  8.6 0.6 copy-done.4
  9.2 6.4 %facet_to_slots.1 = bf16[32,2,40,128]{3,2,1,0:T(8,128)(2,1)} custom-call(s32[32]{0:T(128)} %offs_ref.3, s32[32]{0:T(128)} %order_ref.3, f32[7]{0:T(128)} %ck_ref.3, s32[1]{0:T(128)} %bitcast.fm_ref, bf16[32,2048]{1,0:T(8,128)(2,1)} %sky_ref.1, bf16[8,2048]{1,0:T(8,128)(2,1)} %copy-done.3, bf16[8,2048]{1,0:T(8,128)(2,1)} %copy-done.4, ...), custom_call_target="tpu_custom_call" | custom-call | tf_op jit(solution)/shard_map/facet_to_slots/pallas_call | solution.py:136
  15.6 11.2 %all-to-all-start = ((bf16[32,2,40,128]{3,2,1,0:T(8,128)(2,1)}), bf16[32,2,40,128]{3,2,1,0:T(8,128)(2,1)S(1)}, u32[]{:S(2)}, u32[]{:S(2)}) async-start(bf16[32,2,40,128]{3,2,1,0:T(8,128)(2,1)} %facet_to_slots.1), calls=%async_computation | async-start | bytes 1310720 | tf_op jit(solution)/shard_map/all_to_all | solution.py:307
  26.9 2.7 %collective-permute-start.2 = (bf16[2,8,512]{2,1,0:T(8,128)(2,1)S(1)}, bf16[2,8,512]{2,1,0:T(8,128)(2,1)S(1)}, u32[]{:S(2)}, u32[]{:S(2)}) collective-permute-start(bf16[2,8,512]{2,1,0:T(8,128)(2,1)S(1)} %get-tuple-element.11), channel_id=1, source_target_pairs={{0,1},{1,2},{2,3},{3,4},{4,5},{5,6},{6,7},{8,9},{9,10},{10,11},{11... | collective-permute-start | bytes 49160 | tf_op jit(solution)/shard_map/ppermute | solution.py:293
  29.6 2.8 %collective-permute-start.3 = (bf16[2,8,512]{2,1,0:T(8,128)(2,1)S(1)}, bf16[2,8,512]{2,1,0:T(8,128)(2,1)S(1)}, u32[]{:S(2)}, u32[]{:S(2)}) collective-permute-start(bf16[2,8,512]{2,1,0:T(8,128)(2,1)S(1)} %get-tuple-element.10), channel_id=1, source_target_pairs={{1,0},{2,1},{3,2},{4,3},{5,4},{6,5},{7,6},{9,8},{10,9},{11,10},{12... | collective-permute-start | bytes 49160 | tf_op jit(solution)/shard_map/ppermute | solution.py:293
  32.5 1.9 %collective-permute-start.4 = (f32[8,512]{1,0:T(8,128)S(1)}, f32[8,512]{1,0:T(8,128)S(1)}, u32[]{:S(2)}, u32[]{:S(2)}) collective-permute-start(f32[8,512]{1,0:T(8,128)S(1)} %get-tuple-element.9), channel_id=1, source_target_pairs={{0,1},{1,2},{2,3},{3,4},{4,5},{5,6},{6,7},{8,9},{9,10},{10,11},{11... | collective-permute-start | bytes 49160 | tf_op jit(solution)/shard_map/ppermute | solution.py:293
  34.4 3.6 %collective-permute-start.5 = (f32[8,512]{1,0:T(8,128)S(1)}, f32[8,512]{1,0:T(8,128)S(1)}, u32[]{:S(2)}, u32[]{:S(2)}) collective-permute-start(f32[8,512]{1,0:T(8,128)S(1)} %get-tuple-element.8), channel_id=1, source_target_pairs={{1,0},{2,1},{3,2},{4,3},{5,4},{6,5},{7,6},{9,8},{10,9},{11,10},{12... | collective-permute-start | bytes 49160 | tf_op jit(solution)/shard_map/ppermute | solution.py:293
  38.7 0.0 collective-permute-done.2.obs_b_ref
  38.7 0.0 copy-start.5
  38.7 0.0 collective-permute-done.3.obs_a_ref
  38.7 0.0 collective-permute-done.4.wt_b_ref
  38.7 0.7 collective-permute-done.5.wt_a_ref
  39.5 8.6 %all-to-all-done.arr_ref = bf16[32,2,40,128]{3,2,1,0:T(8,128)(2,1)S(1)} async-done(((bf16[32,2,40,128]{3,2,1,0:T(8,128)(2,1)}), bf16[32,2,40,128]{3,2,1,0:T(8,128)(2,1)S(1)}, u32[]{:S(2)}, u32[]{:S(2)}) %all-to-all-start) | async-done | bytes 655392 | tf_op jit(solution)/shard_map/all_to_all | solution.py:307
  48.1 0.0 copy-done.6
  48.1 0.8 copy-done
  49.0 4.2 %slot_round_trip.1 = (f32[2,32,512]{2,1,0:T(8,128)}, bf16[32,2,32,128]{3,2,1,0:T(8,128)(2,1)}) custom-call(s32[1]{0:T(128)S(6)} %copy.18.count_ref, f32[7]{0:T(128)} %rk_ref.1, f32[7]{0:T(128)} %ck_ref.3, bf16[32,2,40,128]{3,2,1,0:T(8,128)(2,1)} %copy-done, s32[1,512]{1,0:T(1,128)} %cell_ref.1, bf16[2,32,512]{2,1,0:T(8,128)(2,1)} %bitcast.8, ...), custom_call_target="tpu_custom_call" | custom-call | tf_op jit(solution)/shard_map/slot_round_trip/pallas_call | solution.py:224
  53.1 23.4 %all_to_all.10.bp_ref = bf16[32,2,32,128]{3,2,1,0:T(8,128)(2,1)} all-to-all(bf16[32,2,32,128]{3,2,1,0:T(8,128)(2,1)} %get-tuple-element.5), channel_id=1, replica_groups=mesh['facet'=32,'uv'=8] {'facet'}, dimensions={0} | all-to-all | bytes 1048576 | tf_op jit(solution)/shard_map/all_to_all | solution.py:312
  76.5 6.5 %slots_to_facet.1 = f32[32,2048]{1,0:T(8,128)} custom-call(s32[32]{0:T(128)} %offs_ref.3, s32[32]{0:T(128)} %order_ref.3, s32[1]{0:T(128)} %bitcast.fm_ref, bf16[32,2,32,128]{3,2,1,0:T(8,128)(2,1)} %all_to_all.10.bp_ref, f32[1,2048]{1,0:T(1,128)} %constant.32.clone.win_ref, bf16[256,3968]{1,0:T(8,128)(2,1)} %constant.36.clone.tab_hbm), custom_call_target="tpu_custom_call" | custom-call | tf_op jit(solution)/shard_map/slots_to_facet/pallas_call | solution.py:274
  (15 shorter events, 0.0 us)
Async XLA Ops:
  1.4 5.6 %collective-permute-start = (bf16[8,2048]{1,0:T(8,128)(2,1)S(1)}, bf16[8,2048]{1,0:T(8,128)(2,1)S(1)}, u32[]{:S(2)}, u32[]{:S(2)}) collective-permute-start(bf16[8,2048]{1,0:T(8,128)(2,1)S(1)} %get-tuple-element.7), channel_id=1, source_target_pairs={{0,1},{1,2},{2,3},{3,4},{4,5},{5,6},{6,7},{8,9},{9,10},{10,11},{11... | collective-permute-start | bytes 98312 | tf_op jit(solution)/shard_map/ppermute | solution.py:293
  3.3 5.2 %collective-permute-start.1 = (bf16[8,2048]{1,0:T(8,128)(2,1)S(1)}, bf16[8,2048]{1,0:T(8,128)(2,1)S(1)}, u32[]{:S(2)}, u32[]{:S(2)}) collective-permute-start(bf16[8,2048]{1,0:T(8,128)(2,1)S(1)} %get-tuple-element.6), channel_id=1, source_target_pairs={{1,0},{2,1},{3,2},{4,3},{5,4},{6,5},{7,6},{9,8},{10,9},{11,10},{12... | collective-permute-start | bytes 98312 | tf_op jit(solution)/shard_map/ppermute | solution.py:293
  7.0 1.6 %copy-start.3 = (bf16[8,2048]{1,0:T(8,128)(2,1)}, bf16[8,2048]{1,0:T(8,128)(2,1)S(1)}, u32[]{:S(2)}) copy-start(bf16[8,2048]{1,0:T(8,128)(2,1)S(1)} %collective-permute-done.before_ref) | copy-start | bytes 98308
  8.6 0.6 copy-start.4
  9.2 17.7 %copy-start.1 = (bf16[1,2,32,512]{3,2,1,0:T(8,128)(2,1)S(1)}, bf16[1,2,32,512]{3,2,1,0:T(8,128)(2,1)}, u32[]{:S(2)}) copy-start(bf16[1,2,32,512]{3,2,1,0:T(8,128)(2,1)} %param.21) | copy-start | bytes 196612
  9.2 23.3 %copy-start.2 = (f32[1,32,512]{2,1,0:T(8,128)S(1)}, f32[1,32,512]{2,1,0:T(8,128)}, u32[]{:S(2)}) copy-start(f32[1,32,512]{2,1,0:T(8,128)} %param.22) | copy-start | bytes 196612
  15.6 32.5 %all-to-all-start = ((bf16[32,2,40,128]{3,2,1,0:T(8,128)(2,1)}), bf16[32,2,40,128]{3,2,1,0:T(8,128)(2,1)S(1)}, u32[]{:S(2)}, u32[]{:S(2)}) async-start(bf16[32,2,40,128]{3,2,1,0:T(8,128)(2,1)} %facet_to_slots.1), calls=%async_computation | async-start | bytes 1310720 | tf_op jit(solution)/shard_map/all_to_all | solution.py:307
  26.9 11.8 %collective-permute-start.2 = (bf16[2,8,512]{2,1,0:T(8,128)(2,1)S(1)}, bf16[2,8,512]{2,1,0:T(8,128)(2,1)S(1)}, u32[]{:S(2)}, u32[]{:S(2)}) collective-permute-start(bf16[2,8,512]{2,1,0:T(8,128)(2,1)S(1)} %get-tuple-element.11), channel_id=1, source_target_pairs={{0,1},{1,2},{2,3},{3,4},{4,5},{5,6},{6,7},{8,9},{9,10},{10,11},{11... | collective-permute-start | bytes 49160 | tf_op jit(solution)/shard_map/ppermute | solution.py:293
  29.6 9.1 %collective-permute-start.3 = (bf16[2,8,512]{2,1,0:T(8,128)(2,1)S(1)}, bf16[2,8,512]{2,1,0:T(8,128)(2,1)S(1)}, u32[]{:S(2)}, u32[]{:S(2)}) collective-permute-start(bf16[2,8,512]{2,1,0:T(8,128)(2,1)S(1)} %get-tuple-element.10), channel_id=1, source_target_pairs={{1,0},{2,1},{3,2},{4,3},{5,4},{6,5},{7,6},{9,8},{10,9},{11,10},{12... | collective-permute-start | bytes 49160 | tf_op jit(solution)/shard_map/ppermute | solution.py:293
  32.5 6.3 %collective-permute-start.4 = (f32[8,512]{1,0:T(8,128)S(1)}, f32[8,512]{1,0:T(8,128)S(1)}, u32[]{:S(2)}, u32[]{:S(2)}) collective-permute-start(f32[8,512]{1,0:T(8,128)S(1)} %get-tuple-element.9), channel_id=1, source_target_pairs={{0,1},{1,2},{2,3},{3,4},{4,5},{5,6},{6,7},{8,9},{9,10},{10,11},{11... | collective-permute-start | bytes 49160 | tf_op jit(solution)/shard_map/ppermute | solution.py:293
  34.4 5.1 %collective-permute-start.5 = (f32[8,512]{1,0:T(8,128)S(1)}, f32[8,512]{1,0:T(8,128)S(1)}, u32[]{:S(2)}, u32[]{:S(2)}) collective-permute-start(f32[8,512]{1,0:T(8,128)S(1)} %get-tuple-element.8), channel_id=1, source_target_pairs={{1,0},{2,1},{3,2},{4,3},{5,4},{6,5},{7,6},{9,8},{10,9},{11,10},{12... | collective-permute-start | bytes 49160 | tf_op jit(solution)/shard_map/ppermute | solution.py:293
  38.7 9.4 %copy-start.5 = (bf16[2,8,512]{2,1,0:T(8,128)(2,1)}, bf16[2,8,512]{2,1,0:T(8,128)(2,1)S(1)}, u32[]{:S(2)}) copy-start(bf16[2,8,512]{2,1,0:T(8,128)(2,1)S(1)} %collective-permute-done.2.obs_b_ref) | copy-start | bytes 49156
  38.7 9.4 %copy-start.6 = (bf16[2,8,512]{2,1,0:T(8,128)(2,1)}, bf16[2,8,512]{2,1,0:T(8,128)(2,1)S(1)}, u32[]{:S(2)}) copy-start(bf16[2,8,512]{2,1,0:T(8,128)(2,1)S(1)} %collective-permute-done.3.obs_a_ref) | copy-start | bytes 49156
  38.7 9.4 %copy-start.7 = (f32[8,512]{1,0:T(8,128)}, f32[8,512]{1,0:T(8,128)S(1)}, u32[]{:S(2)}) copy-start(f32[8,512]{1,0:T(8,128)S(1)} %collective-permute-done.4.wt_b_ref) | copy-start | bytes 49156
  39.5 8.7 %copy-start.8 = (f32[8,512]{1,0:T(8,128)}, f32[8,512]{1,0:T(8,128)S(1)}, u32[]{:S(2)}) copy-start(f32[8,512]{1,0:T(8,128)S(1)} %collective-permute-done.5.wt_a_ref) | copy-start | bytes 49156
  48.1 0.8 %copy-start = (bf16[32,2,40,128]{3,2,1,0:T(8,128)(2,1)}, bf16[32,2,40,128]{3,2,1,0:T(8,128)(2,1)S(1)}, u32[]{:S(2)}) copy-start(bf16[32,2,40,128]{3,2,1,0:T(8,128)(2,1)S(1)} %all-to-all-done.arr_ref) | copy-start | bytes 1966084

commit v2 on v1

v2 whole, which is shorter than its diff:
```python
import math

import jax
import jax.numpy as jnp
import numpy as np
from jax import lax
from jax.experimental import pallas as pl
from jax.experimental.pallas import tpu as pltpu
from jax.sharding import PartitionSpec as P

FR = 2048
XC = 128
SG = 256
NF = 32
CB = 32
CE = 40
TAPS = 7
VM = 512
BF = jnp.bfloat16
F32 = jnp.float32


def block_table():
    lane = np.arange(128)[None, :]
    g = 8 * (lane % 16) + lane // 16
    row = np.arange(128)[:, None] + 64
    a = 2.0 * np.pi * ((g * row) % 128) / 128
    c, s = np.cos(a), np.sin(a)
    return np.block([[c, -s], [s, c]]).astype(np.float32)


def subgrid_table():
    j = np.arange(SG)[None, :]
    k = np.arange(XC)[:, None]
    a = 2.0 * np.pi * ((j * k) % SG) / SG
    c, s = np.cos(a) / 64.0, np.sin(a) / 64.0
    return np.block([[c, s], [-s, c]]).astype(np.float32)


def facet_phase():
    f = np.arange(NF)[:, None]
    j = np.arange(128)[None, :]
    a = 2.0 * np.pi * ((j * (2 * f + 1)) % 64) / 64
    return np.stack([np.cos(a), np.sin(a)]).astype(np.float32)


def window():
    r = np.arange(FR)
    return (np.sin((r + 0.5) * np.pi / FR) / math.sqrt(FR)).astype(np.float32)[None, :]


def turn(n):
    q = (n + 256) >> 9
    x = (n - (q << 9)).astype(F32) * (math.pi / 1024.0)
    y = x * x
    c = 1.0 + y * (-0.5 + y * (1.0 / 24 + y * (-1.0 / 720 + y * (1.0 / 40320))))
    s = x * (1.0 + y * (-1.0 / 6 + y * (1.0 / 120 + y * (-1.0 / 5040 + y * (1.0 / 362880)))))
    odd = (q & 1) == 1
    cos = jnp.where(odd, s, c)
    sin = jnp.where(odd, c, s)
    cos = jnp.where(((q + 1) & 2) == 2, -cos, cos)
    sin = jnp.where((q & 2) == 2, -sin, sin)
    return cos, sin


def twiddles(facet):
    m = lax.broadcasted_iota(jnp.int32, (16, 128), 0)
    lane = lax.broadcasted_iota(jnp.int32, (16, 128), 1)
    return turn((m * (lane + 64 + 128 * facet)) & (FR - 1))


def cmul(a, w):
    wr, wi = w
    if abs(wi) < 1e-12:
        return a if abs(wr - 1) < 1e-12 else (a[0] * wr, a[1] * wr)
    if abs(wr) < 1e-12:
        return (-a[1], a[0]) if wi > 0 else (a[1], -a[0])
    return (a[0] * wr - a[1] * wi, a[0] * wi + a[1] * wr)


def real_transform(x):
    n = len(x)
    if n == 2:
        zero = jnp.zeros_like(x[0])
        return [(x[0] + x[1], zero), (x[0] - x[1], zero)]
    even, odd = real_transform(x[::2]), real_transform(x[1::2])
    out = [None] * (n // 2 + 1)
    for k in range(n // 4 + 1):
        a = 2.0 * math.pi * k / n
        o = cmul(odd[k], (math.cos(a), -math.sin(a)))
        e = even[k]
        out[k] = (e[0] + o[0], e[1] + o[1])
        if k != n // 2 - k:
            out[n // 2 - k] = (e[0] - o[0], o[1] - e[1])
    return out


def real_inverse(h):
    n = 2 * (len(h) - 1)
    if n == 2:
        return [h[0][0] + h[1][0], h[0][0] - h[1][0]]
    even, odd = [], []
    for k in range(n // 4 + 1):
        a, b = h[k], h[n // 2 - k]
        t = 2.0 * math.pi * k / n
        even.append((a[0] + b[0], a[1] - b[1]))
        odd.append(cmul((a[0] - b[0], a[1] + b[1]), (math.cos(t), math.sin(t))))
    even, odd = real_inverse(even), real_inverse(odd)
    return [v for pair in zip(even, odd) for v in pair]


def swap_index(x, lane):
    for bit in (1, 2, 4, 8):
        high = (lane & bit) != 0
        y = list(x)
        for i in range(16):
            if i & bit:
                continue
            y[i] = jnp.where(high, pltpu.roll(x[i + bit], bit, 1), x[i])
            y[i + bit] = jnp.where(high, x[i + bit], pltpu.roll(x[i], 128 - bit, 1))
        x = y
    return x


def halo_rows(after, before, axis):
    row = lax.broadcasted_iota(jnp.int32, after.shape, axis)
    return jnp.where(row < 3, after, jnp.where(row >= 5, before, jnp.zeros_like(after)))


def k1_body(
    offs_ref, order_ref, ck_ref, facet_ref, sky_ref, before_ref, after_ref, win_ref, tab_ref,
    out_ref, ext_ref, conv_ref, tw_ref, lhs_ref, u_ref, nat_ref,
):
    tw_ref[0], tw_ref[1] = twiddles(facet_ref[0])
    for b in range(16):
        lanes = slice(128 * b, 128 * (b + 1))
        win = win_ref[:, lanes]
        ext_ref[8:16, lanes] = before_ref[:, lanes].astype(F32) * win
        ext_ref[16:48, lanes] = sky_ref[:, lanes].astype(F32) * win
        ext_ref[48:56, lanes] = after_ref[:, lanes].astype(F32) * win
    for b in range(16):
        lanes = slice(128 * b, 128 * (b + 1))
        own = jnp.zeros((CB, 128), F32)
        lo = jnp.zeros((8, 128), F32)
        hi = jnp.zeros((8, 128), F32)
        for t in range(TAPS):
            k = ck_ref[t]
            own = own + k * ext_ref[13 + t : 45 + t, lanes]
            lo = lo + k * ext_ref[5 + t : 13 + t, lanes]
            hi = hi + k * ext_ref[45 + t : 53 + t, lanes]
        conv_ref[0:CB, lanes] = own
        conv_ref[CB:CE, lanes] = halo_rows(hi, lo, 0)
        conv_ref[CE : CE + 8, lanes] = jnp.zeros((8, 128), F32)

    for g in range(3):
        rows = slice(16 * g, 16 * (g + 1))
        a = real_transform([conv_ref[rows, 128 * b : 128 * (b + 1)] for b in range(16)])
        for m in range(16):
            ar, ai = a[m] if m <= 8 else (a[16 - m][0], -a[16 - m][1])
            c, s = tw_ref[0, m : m + 1, :], tw_ref[1, m : m + 1, :]
            lhs_ref[m, rows, 0:128] = (ar * c + ai * s).astype(BF)
            lhs_ref[m, rows, 128:256] = (ai * c - ar * s).astype(BF)
    u = jnp.dot(lhs_ref[...].reshape(16 * 48, 256), tab_ref[...], preferred_element_type=F32)
    u_ref[...] = u.reshape(16, 48, 256)

    lane = lax.broadcasted_iota(jnp.int32, (8, 128), 1)
    for g in range(5):
        rows = slice(8 * g, 8 * (g + 1))
        for p in range(2):
            x = swap_index([u_ref[m, rows, 128 * p : 128 * (p + 1)] for m in range(16)], lane)
            for b in range(16):
                nat_ref[b, rows, 128 * p : 128 * (p + 1)] = x[b]
            nat_ref[16, rows, 128 * p : 128 * (p + 1)] = x[0]

    lane = lax.broadcasted_iota(jnp.int32, (CE, 128), 1)
    for i in range(NF):
        off = offs_ref[order_ref[i]]
        b, s = off >> 7, off & 127
        back = (128 - s) & 127
        keep = lane >= s
        for p in range(2):
            cols = slice(128 * p, 128 * (p + 1))
            x = jnp.where(keep, nat_ref[b, :, cols], nat_ref[b + 1, :, cols])
            out_ref[i, :, cols] = pltpu.roll(x, back, 1).astype(BF)


SMEM = pl.BlockSpec(memory_space=pltpu.SMEM)
VMEM = pl.BlockSpec(memory_space=pltpu.VMEM)
PARAMS = pltpu.CompilerParams(vmem_limit_bytes=24 * 1024 * 1024)


def k1(offs, order, ck, facet, sky, before, after):
    return pl.pallas_call(
        k1_body,
        out_shape=jax.ShapeDtypeStruct((NF, CE, 2 * XC), BF),
        in_specs=[SMEM, SMEM, SMEM, SMEM] + [VMEM] * 5,
        out_specs=VMEM,
        scratch_shapes=[
            pltpu.VMEM((64, FR), F32),
            pltpu.VMEM((48, FR), F32),
            pltpu.VMEM((2, 16, 128), F32),
            pltpu.VMEM((16, 48, 256), BF),
            pltpu.VMEM((16, 48, 256), F32),
            pltpu.VMEM((17, CE, 256), F32),
        ],
        compiler_params=PARAMS,
        name="facet_to_slots",
    )(offs, order, ck, facet, sky, before, after, window(), jnp.asarray(block_table(), BF))


def k2_body(
    offs_ref, order_ref, facet_ref, count_ref, rk_ref, ck_ref, arr_ref, cell_ref, obs_ref, wt_ref,
    before_ref, after_ref, w_ref, wt_tab_ref, ph_ref,
    res_ref, out_ref, lhs_ref, u_ref, dt_ref, ext_ref, y_ref, pho_ref,
):
    for f in range(NF):
        lhs_ref[f, 0:CE, :] = arr_ref[f]
    off = offs_ref[order_ref[facet_ref[0]]]
    back = (128 - 2 * off) & 127
    pho_ref[0] = pltpu.roll(ph_ref[0], back, 1)
    pho_ref[1] = pltpu.roll(ph_ref[1], back, 1)

    cell = cell_ref[...]
    d = lax.broadcasted_iota(jnp.int32, (SG, VM), 0) - cell + 3
    m = jnp.zeros((SG, VM), F32)
    for t in range(TAPS):
        m = jnp.where(d == t, rk_ref[t], m)
    dt_ref[...] = m.astype(BF)

    u = jnp.dot(lhs_ref[...].reshape(NF * 48, 256), w_ref[...], preferred_element_type=F32)
    u_ref[...] = u.reshape(NF, 48, 2 * SG)
    res = []
    ims = []
    for h in range(2):
        re = jnp.zeros((CE, 128), F32)
        im = jnp.zeros((CE, 128), F32)
        for f in range(NF):
            ur = u_ref[f, 0:CE, 128 * h : 128 * (h + 1)]
            ui = u_ref[f, 0:CE, SG + 128 * h : SG + 128 * (h + 1)]
            pc = pho_ref[0, f : f + 1, :]
            ps = pho_ref[1, f : f + 1, :]
            re = re + (ur * pc - ui * ps)
            im = im + (ur * ps + ui * pc)
        res.append(re)
        ims.append(im)
    grid = jnp.concatenate(
        [jnp.concatenate(res, axis=1), jnp.concatenate(ims, axis=1)], axis=0
    ).astype(BF)
    model = jnp.dot(grid, dt_ref[...], preferred_element_type=F32)

    live = (lax.broadcasted_iota(jnp.int32, (1, VM), 1) < count_ref[0]).astype(F32)
    wt = wt_ref[...] * live
    wt_h = halo_rows(after_ref[:, FR + 2 * VM :], before_ref[:, FR + 2 * VM :], 0).astype(F32) * live
    parts = []
    for p in range(2):
        own = wt * (obs_ref[p].astype(F32) - model[p * CE : p * CE + CB])
        res_ref[p] = own
        cols = slice(FR + p * VM, FR + (p + 1) * VM)
        obs_h = halo_rows(after_ref[:, cols], before_ref[:, cols], 0).astype(F32)
        parts += [own, wt_h * (obs_h - model[p * CE + CB : (p + 1) * CE])]
    rr = jnp.concatenate(parts, axis=0).astype(BF)
    gridded = lax.dot_general(
        rr, dt_ref[...], (((1,), (1,)), ((), ())), preferred_element_type=F32
    )
    backs = []
    for p in range(2):
        halo = gridded[p * CE + CB : (p + 1) * CE]
        ext_ref[p, 0:8, :] = halo
        ext_ref[p, 8:40, :] = gridded[p * CE : p * CE + CB]
        ext_ref[p, 40:48, :] = halo
        b = jnp.zeros((CB, SG), F32)
        for t in range(TAPS):
            b = b + ck_ref[t] * ext_ref[p, 11 - t : 43 - t, :]
        backs.append(b)
    br, bi = backs
    for h in range(2):
        lanes = slice(128 * h, 128 * (h + 1))
        xr, xi = br[:, lanes], bi[:, lanes]
        for f in range(NF):
            pc = pho_ref[0, f : f + 1, :]
            ps = pho_ref[1, f : f + 1, :]
            y_ref[f, :, lanes] = (xr * pc + xi * ps).astype(BF)
            y_ref[f, :, SG + 128 * h : SG + 128 * (h + 1)] = (xi * pc - xr * ps).astype(BF)
    z = jnp.dot(y_ref[...].reshape(NF * CB, 2 * SG), wt_tab_ref[...], preferred_element_type=F32)
    out_ref[...] = z.astype(BF).reshape(NF, CB, 2 * XC)


def k2(offs, order, facet, count, rk, ck, arrived, cell, obs, wt, before, after):
    tab = subgrid_table()
    return pl.pallas_call(
        k2_body,
        out_shape=(
            jax.ShapeDtypeStruct((2, CB, VM), F32),
            jax.ShapeDtypeStruct((NF, CB, 2 * XC), BF),
        ),
        in_specs=[SMEM] * 6 + [VMEM] * 9,
        out_specs=(VMEM, VMEM),
        scratch_shapes=[
            pltpu.VMEM((NF, 48, 256), BF),
            pltpu.VMEM((NF, 48, 2 * SG), F32),
            pltpu.VMEM((SG, VM), BF),
            pltpu.VMEM((2, 48, SG), F32),
            pltpu.VMEM((NF, CB, 2 * SG), BF),
            pltpu.VMEM((2, NF, 128), F32),
        ],
        compiler_params=PARAMS,
        name="slot_round_trip",
    )(
        offs, order, facet, count, rk, ck, arrived, cell, obs, wt, before, after,
        jnp.asarray(tab, BF), jnp.asarray(tab.T, BF), facet_phase(),
    )


def k3_body(
    offs_ref, order_ref, facet_ref, bp_ref, win_ref, tab_ref,
    out_ref, nat_ref, tw_ref, lhs_ref, v_ref,
):
    tw_ref[0], tw_ref[1] = twiddles(facet_ref[0])
    nat_ref[...] = jnp.zeros_like(nat_ref)
    lane = lax.broadcasted_iota(jnp.int32, (CB, 128), 1)
    for i in range(NF):
        off = offs_ref[order_ref[i]]
        b, s = off >> 7, off & 127
        keep = lane >= s
        for p in range(2):
            cols = slice(128 * p, 128 * (p + 1))
            x = pltpu.roll(bp_ref[i, :, cols].astype(F32), s, 1)
            nat_ref[b, :, cols] += jnp.where(keep, x, 0.0)
            nat_ref[b + 1, :, cols] += jnp.where(keep, 0.0, x)
    nat_ref[0] += nat_ref[16]

    lane = lax.broadcasted_iota(jnp.int32, (16, 128), 1)
    for g in range(2):
        rows = slice(16 * g, 16 * (g + 1))
        for p in range(2):
            cols = slice(128 * p, 128 * (p + 1))
            x = swap_index([nat_ref[b, rows, cols] for b in range(16)], lane)
            for m in range(16):
                lhs_ref[m, rows, cols] = x[m].astype(BF)
    v = jnp.dot(lhs_ref[...].reshape(16 * CB, 256), tab_ref[...], preferred_element_type=F32)
    v_ref[...] = v.reshape(16, CB, 256)
    for g in range(4):
        rows = slice(8 * g, 8 * (g + 1))
        t = []
        for m in range(16):
            vr, vi = v_ref[m, rows, 0:128], v_ref[m, rows, 128:256]
            c, s = tw_ref[0, m : m + 1, :], tw_ref[1, m : m + 1, :]
            t.append((vr * c - vi * s, vr * s + vi * c))
        h = [(t[m][0] + t[-m % 16][0], t[m][1] - t[-m % 16][1]) for m in range(9)]
        x = real_inverse(h)
        for b in range(16):
            lanes = slice(128 * b, 128 * (b + 1))
            out_ref[rows, lanes] = x[b] * (0.5 * win_ref[:, lanes])


def k3(offs, order, facet, bp):
    return pl.pallas_call(
        k3_body,
        out_shape=jax.ShapeDtypeStruct((CB, FR), F32),
        in_specs=[SMEM, SMEM, SMEM, VMEM, VMEM, VMEM],
        out_specs=VMEM,
        scratch_shapes=[
            pltpu.VMEM((17, CB, 256), F32),
            pltpu.VMEM((2, 16, 128), F32),
            pltpu.VMEM((16, CB, 256), BF),
            pltpu.VMEM((16, CB, 256), F32),
        ],
        compiler_params=PARAMS,
        name="slots_to_facet",
    )(offs, order, facet, bp, window(), jnp.asarray(block_table().T, BF))


def neighbours(first, last):
    n = lax.axis_size("uv")
    up = [(i, i + 1) for i in range(n - 1)]
    down = [(i + 1, i) for i in range(n - 1)]
    return lax.ppermute(last, "uv", up), lax.ppermute(first, "uv", down)


def local(
    sky_image, subgrid_offsets, owner_order, visibility_count, visibility_cell, observed,
    visibility_weight, row_kernel, column_kernel,
):
    facet = lax.axis_index("facet").astype(jnp.int32).reshape(1)
    obs = observed[0]
    wt = visibility_weight[0]

    def edge(rows):
        return jnp.concatenate(
            [sky_image[rows], obs[0, rows], obs[1, rows], wt[rows].astype(BF)], axis=1
        )

    before, after = neighbours(edge(slice(0, 8)), edge(slice(24, 32)))
    out = k1(subgrid_offsets, owner_order, column_kernel, facet, sky_image, before, after)
    arrived = lax.all_to_all(out, "facet", split_axis=0, concat_axis=0, tiled=True)
    res, outgoing = k2(
        subgrid_offsets, owner_order, facet, visibility_count, row_kernel, column_kernel,
        arrived, visibility_cell, obs, wt, before, after,
    )
    back = lax.all_to_all(outgoing, "facet", split_axis=0, concat_axis=0, tiled=True)
    dirty = k3(subgrid_offsets, owner_order, facet, back)
    return (res[None], dirty)


def solution(mesh):
    in_specs = (
        P("uv", "facet"),
        P(),
        P(),
        P("facet"),
        P("facet", None),
        P("facet", None, "uv", None),
        P("facet", "uv", None),
        P(),
        P(),
    )
    out_specs = (P("facet", None, "uv", None), P("uv", "facet"))
    return jax.shard_map(local, mesh=mesh, in_specs=in_specs, out_specs=out_specs, check_vma=False)
```

time: 83.7 us -> 73.3 us (0.88)
  starting transfers between devices: 27.9 us -> 15.8 us
  waiting for transfers between devices: 10.9 us -> 22 us
  Pallas kernels: 17.2 us -> 9.3 us
  blocking collectives: 23.4 us -> 21.7 us
  local copies, waits for them, and re-layouts: 2.26 us -> 0.91 us
  other arithmetic: 0 us -> 0.86 us
    ppermute x6 -> x2, starting transfers between devices: 16.7 us -> 4.46 us  [neighbours(): return (lax.ppermute(last, 'uv', up), lax.ppermute(first, 'uv', down))]
    all_to_all x1, waiting for transfers between devices: 8.65 us -> 19 us  [local(): lax.all_to_all(out, 'facet', split_axis=0, concat_axis=0, tiled=True)]
    pallas_call x1, Pallas kernels: 6.55 us -> 2.18 us  [k3(): pl.pallas_call(k3_body, out_shape=jax.ShapeDtypeStruct((CB, FR), F32), in...]
    pallas_call x1, Pallas kernels: 6.44 us -> 3.73 us  [k1(): pl.pallas_call(k1_body, out_shape=jax.ShapeDtypeStruct((NF, CE, 2 * XC),...]
    all_to_all x1, blocking collectives: 23.4 us -> 21.7 us  [local(): lax.all_to_all(outgoing, 'facet', split_axis=0, concat_axis=0, tiled=True)]
    unnamed x18 -> x28, local copies, waits for them, and re-layouts: 1.47 us -> 0.09 us
    another operation x0 -> x1, other arithmetic: none -> 0.85 us
    ppermute x6 -> x2, waiting for transfers between devices: 2.26 us -> 3.05 us  [neighbours(): return (lax.ppermute(last, 'uv', up), lax.ppermute(first, 'uv', down))]
  transfers between devices with their start and end apart: 7 -> 3, of which waited for: 3 -> 2; matrix products, arithmetic and copies ran while one was open for 0% -> 0% of each run, Pallas kernels for 0% -> 0%
where the time goes in v2:
time: 73.3 us; the launch traced here: 72.1 us
  waiting for transfers between devices  22 us (30%)
  blocking collectives  21.7 us (30%)
  starting transfers between devices  15.8 us (22%)
  Pallas kernels  9.3 us (13%)
  between operations  1.48 us (2%)
  local copies, waits for them, and re-layouts  0.91 us (1%)
  other arithmetic  0.86 us (1%)
    all_to_all x1, blocking collectives, local(): lax.all_to_all(outgoing, 'facet', split_axis=0, concat_axis=0, tiled=True)  21.7 us
    all_to_all x1, waiting for transfers between devices, local(): lax.all_to_all(out, 'facet', split_axis=0, concat_axis=0, tiled=True)  19 us
    all_to_all x1, starting transfers between devices, local(): lax.all_to_all(out, 'facet', split_axis=0, concat_axis=0, tiled=True)  11.3 us
    ppermute x2, starting transfers between devices, neighbours(): return (lax.ppermute(last, 'uv', up), lax.ppermute(first, 'uv', down))  4.46 us
    pallas_call x1, Pallas kernels, k1(): pl.pallas_call(k1_body, out_shape=jax.ShapeDtypeStruct((NF, CE, 2 * XC),...  3.73 us
    pallas_call x1, Pallas kernels, k2(): pl.pallas_call(k2_body, out_shape=(jax.ShapeDtypeStruct((2, CB, VM), F32)...  3.39 us
    ppermute x2, waiting for transfers between devices, neighbours(): return (lax.ppermute(last, 'uv', up), lax.ppermute(first, 'uv', down))  3.05 us
    pallas_call x1, Pallas kernels, k3(): pl.pallas_call(k3_body, out_shape=jax.ShapeDtypeStruct((CB, FR), F32), in...  2.18 us
  transfers between devices with their start and end apart: 3, of which 2 were waited for; matrix products, arithmetic and copies ran while one was open for 0% of the time, Pallas kernels for 0%

profile of v2, /device:TPU:48, one launch (start us, length us, event | category | flops | bytes accessed | tf_op | source)
XLA Modules:
  0.0 72.1 jit_solution(12709671807929571382)
XLA Ops:
  0.6 0.8 %convert.4 = bf16[1,32,512]{2,1,0:T(8,128)(2,1)S(1)} convert(f32[1,32,512]{2,1,0:T(8,128)} %param.22) | non-fusion elementwise | flops 16384 | bytes 98304 | tf_op jit(solution)/shard_map/convert.1
  1.5 0.8 %fusion = (bf16[8,2048]{1,0:T(8,128)(2,1)S(1)}, bf16[8,2048]{1,0:T(8,128)(2,1)S(1)}) fusion(bf16[32,2048]{1,0:T(8,128)(2,1)} %sky_ref.1), kind=kLoop, calls=%fused_computation.8 | loop fusion | bytes 131072 | tf_op jit(solution)/shard_map/slice | solution.py:390
  2.3 0.0 copy-done.4
  2.3 2.1 %collective-permute-start.1 = (bf16[8,3584]{1,0:T(8,128)(2,1)S(1)}, bf16[8,3584]{1,0:T(8,128)(2,1)S(1)}, u32[]{:S(2)}, u32[]{:S(2)}) collective-permute-start(bf16[8,3584]{1,0:T(8,128)(2,1)S(1)} %pad_maximum_fusion.1), channel_id=1, source_target_pairs={{1,0},{2,1},{3,2},{4,3},{5,4},{6,5},{7,6},{9,8},{10,9},{11,10},{12... | collective-permute-start | bytes 172040 | tf_op jit(solution)/shard_map/ppermute | solution.py:377
  4.4 0.0 copy-start.11
  4.4 0.0 copy-start.7
  4.4 2.4 %collective-permute-start = (bf16[8,3584]{1,0:T(8,128)(2,1)S(1)}, bf16[8,3584]{1,0:T(8,128)(2,1)S(1)}, u32[]{:S(2)}, u32[]{:S(2)}) collective-permute-start(bf16[8,3584]{1,0:T(8,128)(2,1)S(1)} %pad_maximum_fusion), channel_id=1, source_target_pairs={{0,1},{1,2},{2,3},{3,4},{4,5},{5,6},{6,7},{8,9},{9,10},{10,11},{11... | collective-permute-start | bytes 172040 | tf_op jit(solution)/shard_map/ppermute | solution.py:377
  6.9 0.0 copy-start.9
  6.9 0.0 copy-start.10
  6.9 0.0 collective-permute-done.1.after_ref
  6.9 3.0 %collective-permute-done.before_ref = bf16[8,3584]{1,0:T(8,128)(2,1)S(1)} collective-permute-done((bf16[8,3584]{1,0:T(8,128)(2,1)S(1)}, bf16[8,3584]{1,0:T(8,128)(2,1)S(1)}, u32[]{:S(2)}, u32[]{:S(2)}) %collective-permute-start) | collective-permute-done | bytes 57376 | tf_op jit(solution)/shard_map/ppermute | solution.py:377
  9.9 0.0 copy-done
  10.0 3.7 %facet_to_slots.1 = bf16[32,40,256]{2,1,0:T(8,128)(2,1)} custom-call(s32[32]{0:T(128)S(1)} %copy-done.9, s32[32]{0:T(128)S(1)} %copy-done.10, f32[7]{0:T(128)S(1)} %copy-done.11, s32[1]{0:T(128)} %bitcast.facet_ref, bf16[32,2048]{1,0:T(8,128)(2,1)S(1)} %copy-done, bf16[8,3584]{1,0:T(8,128)(2,1)S(1)} %collective-permute-done.before_ref, ...), custom_call_target="tpu_custom_call" | custom-call | tf_op jit(solution)/shard_map/facet_to_slots/pallas_call | solution.py:193
  13.7 11.3 %all-to-all-start = ((bf16[32,40,256]{2,1,0:T(8,128)(2,1)}), bf16[32,40,256]{2,1,0:T(8,128)(2,1)S(1)}, u32[]{:S(2)}, u32[]{:S(2)}) async-start(bf16[32,40,256]{2,1,0:T(8,128)(2,1)} %facet_to_slots.1), calls=%async_computation | async-start | bytes 1310720 | tf_op jit(solution)/shard_map/all_to_all | solution.py:395
  25.1 0.0 copy-start.12
  25.7 0.0 copy-start.13
  25.7 19.0 %all-to-all-done.arr_ref = bf16[32,40,256]{2,1,0:T(8,128)(2,1)S(1)} async-done(((bf16[32,40,256]{2,1,0:T(8,128)(2,1)}), bf16[32,40,256]{2,1,0:T(8,128)(2,1)S(1)}, u32[]{:S(2)}, u32[]{:S(2)}) %all-to-all-start) | async-done | bytes 655392 | tf_op jit(solution)/shard_map/all_to_all | solution.py:395
  44.7 0.0 copy-done.8
  44.7 0.0 copy-done.12
  44.7 0.0 copy-done.13
  44.7 3.4 %slot_round_trip.1 = (f32[2,32,512]{2,1,0:T(8,128)}, bf16[32,32,256]{2,1,0:T(8,128)(2,1)S(1)}) custom-call(s32[32]{0:T(128)S(1)} %copy-done.9, s32[32]{0:T(128)S(1)} %copy-done.10, s32[1]{0:T(128)} %bitcast.facet_ref, s32[1]{0:T(128)S(6)} %copy.18.count_ref, f32[7]{0:T(128)S(1)} %copy-done.13, f32[7]{0:T(128)S(1)} %copy-done.11, ...), custom_call_target="tpu_custom_call" | custom-call | tf_op jit(solution)/shard_map/slot_round_trip/pallas_call | solution.py:290
  48.1 0.0 copy-start.5
  48.2 21.7 %all_to_all.10.bp_ref = bf16[32,32,256]{2,1,0:T(8,128)(2,1)S(1)} all-to-all(bf16[32,32,256]{2,1,0:T(8,128)(2,1)S(1)} %get-tuple-element.5), channel_id=1, replica_groups=mesh['facet'=32,'uv'=8] {'facet'}, dimensions={0} | all-to-all | bytes 1048576 | tf_op jit(solution)/shard_map/all_to_all | solution.py:400
  69.9 2.2 %slots_to_facet.1 = f32[32,2048]{1,0:T(8,128)} custom-call(s32[32]{0:T(128)S(1)} %copy-done.9, s32[32]{0:T(128)S(1)} %copy-done.10, s32[1]{0:T(128)} %bitcast.facet_ref, bf16[32,32,256]{2,1,0:T(8,128)(2,1)S(1)} %all_to_all.10.bp_ref, f32[1,2048]{1,0:T(1,128)S(1)} %copy-done.7, bf16[256,256]{1,0:T(8,128)(2,1)S(1)} %copy-done.5), custom_call_target="tpu_custom_call" | custom-call | tf_op jit(solution)/shard_map/slots_to_facet/pallas_call | solution.py:357
  (19 shorter events, 0.0 us)
Async XLA Ops:
  1.5 0.8 %copy-start.4 = (bf16[1,2,32,512]{3,2,1,0:T(8,128)(2,1)S(1)}, bf16[1,2,32,512]{3,2,1,0:T(8,128)(2,1)}, u32[]{:S(2)}) copy-start(bf16[1,2,32,512]{3,2,1,0:T(8,128)(2,1)} %param.21) | copy-start | bytes 196612
  2.3 7.6 %copy-start.6 = (bf16[256,256]{1,0:T(8,128)(2,1)S(1)}, bf16[256,256]{1,0:T(8,128)(2,1)}, u32[]{:S(2)}) copy-start(bf16[256,256]{1,0:T(8,128)(2,1)} %constant.18.clone.tab_ref) | copy-start | bytes 393220
  2.3 7.6 %copy-start = (bf16[32,2048]{1,0:T(8,128)(2,1)S(1)}, bf16[32,2048]{1,0:T(8,128)(2,1)}, u32[]{:S(2)}) copy-start(bf16[32,2048]{1,0:T(8,128)(2,1)} %sky_ref.1) | copy-start | bytes 393220
  2.3 4.5 %collective-permute-start.1 = (bf16[8,3584]{1,0:T(8,128)(2,1)S(1)}, bf16[8,3584]{1,0:T(8,128)(2,1)S(1)}, u32[]{:S(2)}, u32[]{:S(2)}) collective-permute-start(bf16[8,3584]{1,0:T(8,128)(2,1)S(1)} %pad_maximum_fusion.1), channel_id=1, source_target_pairs={{1,0},{2,1},{3,2},{4,3},{5,4},{6,5},{7,6},{9,8},{10,9},{11,10},{12... | collective-permute-start | bytes 172040 | tf_op jit(solution)/shard_map/ppermute | solution.py:377
  4.4 5.5 %copy-start.11 = (f32[7]{0:T(128)S(1)}, f32[7]{0:T(128)}, u32[]{:S(2)}) copy-start(f32[7]{0:T(128)} %ck_ref.3) | copy-start | bytes 88
  4.4 5.5 %copy-start.7 = (f32[1,2048]{1,0:T(1,128)S(1)}, f32[1,2048]{1,0:T(1,128)}, u32[]{:S(2)}) copy-start(f32[1,2048]{1,0:T(1,128)} %constant.19.clone.win_ref) | copy-start | bytes 24580
  4.4 5.5 %collective-permute-start = (bf16[8,3584]{1,0:T(8,128)(2,1)S(1)}, bf16[8,3584]{1,0:T(8,128)(2,1)S(1)}, u32[]{:S(2)}, u32[]{:S(2)}) collective-permute-start(bf16[8,3584]{1,0:T(8,128)(2,1)S(1)} %pad_maximum_fusion), channel_id=1, source_target_pairs={{0,1},{1,2},{2,3},{3,4},{4,5},{5,6},{6,7},{8,9},{9,10},{10,11},{11... | collective-permute-start | bytes 172040 | tf_op jit(solution)/shard_map/ppermute | solution.py:377
  6.9 3.1 %copy-start.9 = (s32[32]{0:T(128)S(1)}, s32[32]{0:T(128)}, u32[]{:S(2)}) copy-start(s32[32]{0:T(128)} %offs_ref.5) | copy-start | bytes 388
  6.9 3.1 %copy-start.10 = (s32[32]{0:T(128)S(1)}, s32[32]{0:T(128)}, u32[]{:S(2)}) copy-start(s32[32]{0:T(128)} %order_ref.5) | copy-start | bytes 388
  13.7 31.0 %copy-start.1 = (bf16[256,512]{1,0:T(8,128)(2,1)S(1)}, bf16[256,512]{1,0:T(8,128)(2,1)}, u32[]{:S(2)}) copy-start(bf16[256,512]{1,0:T(8,128)(2,1)} %constant.20.clone.w_ref) | copy-start | bytes 786436
  13.7 31.0 %copy-start.2 = (bf16[512,256]{1,0:T(8,128)(2,1)S(1)}, bf16[512,256]{1,0:T(8,128)(2,1)}, u32[]{:S(2)}) copy-start(bf16[512,256]{1,0:T(8,128)(2,1)} %constant.21.clone.wt_tab_ref) | copy-start | bytes 786436
  13.7 31.0 %copy-start.3 = (f32[1,32,512]{2,1,0:T(8,128)S(1)}, f32[1,32,512]{2,1,0:T(8,128)}, u32[]{:S(2)}) copy-start(f32[1,32,512]{2,1,0:T(8,128)} %param.22) | copy-start | bytes 196612
  13.7 31.0 %copy-start.8 = (f32[2,32,128]{2,1,0:T(8,128)S(1)}, f32[2,32,128]{2,1,0:T(8,128)}, u32[]{:S(2)}) copy-start(f32[2,32,128]{2,1,0:T(8,128)} %constant.22.clone.ph_ref) | copy-start | bytes 98308
  13.7 31.0 %all-to-all-start = ((bf16[32,40,256]{2,1,0:T(8,128)(2,1)}), bf16[32,40,256]{2,1,0:T(8,128)(2,1)S(1)}, u32[]{:S(2)}, u32[]{:S(2)}) async-start(bf16[32,40,256]{2,1,0:T(8,128)(2,1)} %facet_to_slots.1), calls=%async_computation | async-start | bytes 1310720 | tf_op jit(solution)/shard_map/all_to_all | solution.py:395
  25.1 19.7 %copy-start.12 = (s32[1,512]{1,0:T(1,128)S(1)}, s32[1,512]{1,0:T(1,128)}, u32[]{:S(2)}) copy-start(s32[1,512]{1,0:T(1,128)} %cell_ref.1) | copy-start | bytes 6148
  25.7 19.0 %copy-start.13 = (f32[7]{0:T(128)S(1)}, f32[7]{0:T(128)}, u32[]{:S(2)}) copy-start(f32[7]{0:T(128)} %rk_ref.1) | copy-start | bytes 88
  48.1 21.7 %copy-start.5 = (bf16[256,256]{1,0:T(8,128)(2,1)S(1)}, bf16[256,256]{1,0:T(8,128)(2,1)}, u32[]{:S(2)}) copy-start(bf16[256,256]{1,0:T(8,128)(2,1)} %constant.23.clone.tab_ref) | copy-start | bytes 393220

commit v3 on v2

--- a/solution.py
+++ b/solution.py
@@ -128,8 +128,8 @@
 
 
 def k1_body(
-    offs_ref, order_ref, ck_ref, facet_ref, sky_ref, before_ref, after_ref, win_ref, tab_ref,
-    out_ref, ext_ref, conv_ref, tw_ref, lhs_ref, u_ref, nat_ref,
+    offs_ref, order_ref, ck_ref, facet_ref, count_ref, rk_ref, sky_ref, before_ref, after_ref,
+    win_ref, tab_ref, cell_ref, out_ref, ext_ref, conv_ref, tw_ref, lhs_ref, u_ref, nat_ref,
 ):
     tw_ref[0], tw_ref[1] = twiddles(facet_ref[0])
     for b in range(16):
@@ -189,11 +189,11 @@
 PARAMS = pltpu.CompilerParams(vmem_limit_bytes=24 * 1024 * 1024)
 
 
-def k1(offs, order, ck, facet, sky, before, after):
+def k1(offs, order, ck, facet, count, rk, sky, before, after, cell):
     return pl.pallas_call(
         k1_body,
         out_shape=jax.ShapeDtypeStruct((NF, CE, 2 * XC), BF),
-        in_specs=[SMEM, SMEM, SMEM, SMEM] + [VMEM] * 5,
+        in_specs=[SMEM] * 6 + [VMEM] * 6,
         out_specs=VMEM,
         scratch_shapes=[
             pltpu.VMEM((64, FR), F32),
@@ -205,7 +205,10 @@
         ],
         compiler_params=PARAMS,
         name="facet_to_slots",
-    )(offs, order, ck, facet, sky, before, after, window(), jnp.asarray(block_table(), BF))
+    )(
+        offs, order, ck, facet, count, rk, sky, before, after, window(),
+        jnp.asarray(block_table(), BF), cell,
+    )
 
 
 def k2_body(
@@ -391,7 +394,10 @@
         )
 
     before, after = neighbours(edge(slice(0, 8)), edge(slice(24, 32)))
-    out = k1(subgrid_offsets, owner_order, column_kernel, facet, sky_image, before, after)
+    out = k1(
+        subgrid_offsets, owner_order, column_kernel, facet, visibility_count, row_kernel,
+        sky_image, before, after, visibility_cell,
+    )
     arrived = lax.all_to_all(out, "facet", split_axis=0, concat_axis=0, tiled=True)
     res, outgoing = k2(
         subgrid_offsets, owner_order, facet, visibility_count, row_kernel, column_kernel,

time: 73.3 us -> 74.5 us (1.016); the launches traced: 72.1 us -> 74.1 us
  blocking collectives: 21.7 us -> 55.6 us
  waiting for transfers between devices: 22 us -> 1.1 us
  starting transfers between devices: 15.8 us -> 5.69 us
  Pallas kernels: 9.3 us -> 8.47 us
    all_to_all x0 -> x1, blocking collectives: none -> 32.4 us  [local(): lax.all_to_all(out, 'facet', split_axis=0, concat_axis=0, tiled=True)]
    all_to_all x1 -> x0, waiting for transfers between devices: 19 us -> none  [local(): lax.all_to_all(out, 'facet', split_axis=0, concat_axis=0, tiled=True)]
    all_to_all x1 -> x0, starting transfers between devices: 11.3 us -> none  [local(): lax.all_to_all(out, 'facet', split_axis=0, concat_axis=0, tiled=True)]
    ppermute x2, waiting for transfers between devices: 3.05 us -> 1.1 us  [neighbours(): return (lax.ppermute(last, 'uv', up), lax.ppermute(first, 'uv', down))]
    all_to_all x1, blocking collectives: 21.7 us -> 23.2 us  [local(): lax.all_to_all(outgoing, 'facet', split_axis=0, concat_axis=0, tiled=True)]
    ppermute x2, starting transfers between devices: 4.46 us -> 5.69 us  [neighbours(): return (lax.ppermute(last, 'uv', up), lax.ppermute(first, 'uv', down))]
    pallas_call x1, Pallas kernels: 3.73 us -> 2.89 us  [k1(): pl.pallas_call(k1_body, out_shape=jax.ShapeDtypeStruct((NF, CE, 2 * XC),...]
  transfers between devices with their start and end apart: 3 -> 2, of which waited for: 2 -> 1; matrix products, arithmetic and copies ran while one was open for 0% -> 0% of each run, Pallas kernels for 0% -> 0%
where the time goes in v3:
time: 74.5 us; the launch traced here: 74.1 us
  blocking collectives  55.6 us (75%)
  Pallas kernels  8.47 us (11%)
  starting transfers between devices  5.69 us (8%)
  between operations  1.49 us (2%)
  waiting for transfers between devices  1.1 us (1%)
  local copies, waits for them, and re-layouts  0.92 us (1%)
  other arithmetic  0.86 us (1%)
    all_to_all x1, blocking collectives, local(): lax.all_to_all(out, 'facet', split_axis=0, concat_axis=0, tiled=True)  32.4 us
    all_to_all x1, blocking collectives, local(): lax.all_to_all(outgoing, 'facet', split_axis=0, concat_axis=0, tiled=True)  23.2 us
    ppermute x2, starting transfers between devices, neighbours(): return (lax.ppermute(last, 'uv', up), lax.ppermute(first, 'uv', down))  5.69 us
    pallas_call x1, Pallas kernels, k2(): pl.pallas_call(k2_body, out_shape=(jax.ShapeDtypeStruct((2, CB, VM), F32)...  3.39 us
    pallas_call x1, Pallas kernels, k1(): pl.pallas_call(k1_body, out_shape=jax.ShapeDtypeStruct((NF, CE, 2 * XC),...  2.89 us
    pallas_call x1, Pallas kernels, k3(): pl.pallas_call(k3_body, out_shape=jax.ShapeDtypeStruct((CB, FR), F32), in...  2.19 us
  transfers between devices with their start and end apart: 2, of which 1 were waited for; matrix products, arithmetic and copies ran while one was open for 0% of the time, Pallas kernels for 0%

profile of v3, /device:TPU:48, one launch (start us, length us, event | category | flops | bytes accessed | tf_op | source)
XLA Modules:
  0.0 74.1 jit_solution(13335669235122614565)
XLA Ops:
  0.6 0.8 %convert.4 = bf16[1,32,512]{2,1,0:T(8,128)(2,1)S(1)} convert(f32[1,32,512]{2,1,0:T(8,128)} %param.22) | non-fusion elementwise | flops 16384 | bytes 98304 | tf_op jit(solution)/shard_map/convert.1
  1.5 0.8 %fusion = (bf16[8,2048]{1,0:T(8,128)(2,1)S(1)}, bf16[8,2048]{1,0:T(8,128)(2,1)S(1)}) fusion(bf16[32,2048]{1,0:T(8,128)(2,1)} %sky_ref.1), kind=kLoop, calls=%fused_computation.8 | loop fusion | bytes 131072 | tf_op jit(solution)/shard_map/slice | solution.py:393
  2.3 0.0 copy-done.4
  2.3 2.1 %collective-permute-start = (bf16[8,3584]{1,0:T(8,128)(2,1)S(1)}, bf16[8,3584]{1,0:T(8,128)(2,1)S(1)}, u32[]{:S(2)}, u32[]{:S(2)}) collective-permute-start(bf16[8,3584]{1,0:T(8,128)(2,1)S(1)} %pad_maximum_fusion), channel_id=1, source_target_pairs={{0,1},{1,2},{2,3},{3,4},{4,5},{5,6},{6,7},{8,9},{9,10},{10,11},{11... | collective-permute-start | bytes 172040 | tf_op jit(solution)/shard_map/ppermute | solution.py:380
  4.4 0.0 copy-start.12
  4.4 0.0 copy-start.13
  4.4 0.0 copy-start.7
  4.5 3.6 %collective-permute-start.1 = (bf16[8,3584]{1,0:T(8,128)(2,1)S(1)}, bf16[8,3584]{1,0:T(8,128)(2,1)S(1)}, u32[]{:S(2)}, u32[]{:S(2)}) collective-permute-start(bf16[8,3584]{1,0:T(8,128)(2,1)S(1)} %pad_maximum_fusion.1), channel_id=1, source_target_pairs={{1,0},{2,1},{3,2},{4,3},{5,4},{6,5},{7,6},{9,8},{10,9},{11,10},{12... | collective-permute-start | bytes 172040 | tf_op jit(solution)/shard_map/ppermute | solution.py:380
  8.1 0.0 copy-start.9
  8.8 0.0 copy-start.10
  8.8 0.0 copy-start.11
  8.8 0.0 collective-permute-done.before_ref
  8.8 1.1 %collective-permute-done.1.after_ref = bf16[8,3584]{1,0:T(8,128)(2,1)S(1)} collective-permute-done((bf16[8,3584]{1,0:T(8,128)(2,1)S(1)}, bf16[8,3584]{1,0:T(8,128)(2,1)S(1)}, u32[]{:S(2)}, u32[]{:S(2)}) %collective-permute-start.1) | collective-permute-done | bytes 57376 | tf_op jit(solution)/shard_map/ppermute | solution.py:380
  9.9 0.0 copy-done.12
  10.0 2.9 %facet_to_slots.1 = bf16[32,40,256]{2,1,0:T(8,128)(2,1)S(1)} custom-call(s32[32]{0:T(128)S(1)} %copy-done.10, s32[32]{0:T(128)S(1)} %copy-done.11, f32[7]{0:T(128)S(1)} %copy-done.13, s32[1]{0:T(128)} %bitcast.facet_ref, s32[1]{0:T(128)S(6)} %copy.18.count_ref, f32[7]{0:T(128)S(1)} %copy-done.12, bf16[32,2048]{1,0:T(8,128)(2,1)S(1)} %copy-done, ...), custom_call_target="tpu_custom_call" | custom-call | tf_op jit(solution)/shard_map/facet_to_slots/pallas_call | solution.py:193
  12.9 0.0 copy-start.1
  12.9 0.0 copy-start.2
  12.9 0.0 copy-start.3
  12.9 0.0 copy-start.8
  12.9 32.4 %all_to_all.10.arr_ref = bf16[32,40,256]{2,1,0:T(8,128)(2,1)S(1)} all-to-all(bf16[32,40,256]{2,1,0:T(8,128)(2,1)S(1)} %facet_to_slots.1), channel_id=1, replica_groups=mesh['facet'=32,'uv'=8] {'facet'}, dimensions={0} | all-to-all | bytes 1310720 | tf_op jit(solution)/shard_map/all_to_all | solution.py:401
  45.3 3.4 %slot_round_trip.1 = (f32[2,32,512]{2,1,0:T(8,128)}, bf16[32,32,256]{2,1,0:T(8,128)(2,1)S(1)}) custom-call(s32[32]{0:T(128)S(1)} %copy-done.10, s32[32]{0:T(128)S(1)} %copy-done.11, s32[1]{0:T(128)} %bitcast.facet_ref, s32[1]{0:T(128)S(6)} %copy.18.count_ref, f32[7]{0:T(128)S(1)} %copy-done.12, f32[7]{0:T(128)S(1)} %copy-done.13, ...), custom_call_target="tpu_custom_call" | custom-call | tf_op jit(solution)/shard_map/slot_round_trip/pallas_call | solution.py:293
  48.7 0.0 copy-start.6
  48.8 23.2 %all_to_all.11.bp_ref = bf16[32,32,256]{2,1,0:T(8,128)(2,1)S(1)} all-to-all(bf16[32,32,256]{2,1,0:T(8,128)(2,1)S(1)} %get-tuple-element.5), channel_id=1, replica_groups=mesh['facet'=32,'uv'=8] {'facet'}, dimensions={0} | all-to-all | bytes 1048576 | tf_op jit(solution)/shard_map/all_to_all | solution.py:406
  72.0 2.2 %slots_to_facet.1 = f32[32,2048]{1,0:T(8,128)} custom-call(s32[32]{0:T(128)S(1)} %copy-done.10, s32[32]{0:T(128)S(1)} %copy-done.11, s32[1]{0:T(128)} %bitcast.facet_ref, bf16[32,32,256]{2,1,0:T(8,128)(2,1)S(1)} %all_to_all.11.bp_ref, f32[1,2048]{1,0:T(1,128)S(1)} %copy-done.7, bf16[256,256]{1,0:T(8,128)(2,1)S(1)} %copy-done.6), custom_call_target="tpu_custom_call" | custom-call | tf_op jit(solution)/shard_map/slots_to_facet/pallas_call | solution.py:360
  (18 shorter events, 0.0 us)
Async XLA Ops:
  1.5 0.8 %copy-start.4 = (bf16[1,2,32,512]{3,2,1,0:T(8,128)(2,1)S(1)}, bf16[1,2,32,512]{3,2,1,0:T(8,128)(2,1)}, u32[]{:S(2)}) copy-start(bf16[1,2,32,512]{3,2,1,0:T(8,128)(2,1)} %param.21) | copy-start | bytes 196612
  2.3 7.6 %copy-start.5 = (bf16[256,256]{1,0:T(8,128)(2,1)S(1)}, bf16[256,256]{1,0:T(8,128)(2,1)}, u32[]{:S(2)}) copy-start(bf16[256,256]{1,0:T(8,128)(2,1)} %constant.18.clone.tab_ref) | copy-start | bytes 393220
  2.3 7.6 %copy-start = (bf16[32,2048]{1,0:T(8,128)(2,1)S(1)}, bf16[32,2048]{1,0:T(8,128)(2,1)}, u32[]{:S(2)}) copy-start(bf16[32,2048]{1,0:T(8,128)(2,1)} %sky_ref.1) | copy-start | bytes 393220
  2.3 6.5 %collective-permute-start = (bf16[8,3584]{1,0:T(8,128)(2,1)S(1)}, bf16[8,3584]{1,0:T(8,128)(2,1)S(1)}, u32[]{:S(2)}, u32[]{:S(2)}) collective-permute-start(bf16[8,3584]{1,0:T(8,128)(2,1)S(1)} %pad_maximum_fusion), channel_id=1, source_target_pairs={{0,1},{1,2},{2,3},{3,4},{4,5},{5,6},{6,7},{8,9},{9,10},{10,11},{11... | collective-permute-start | bytes 172040 | tf_op jit(solution)/shard_map/ppermute | solution.py:380
  4.4 5.5 %copy-start.12 = (f32[7]{0:T(128)S(1)}, f32[7]{0:T(128)}, u32[]{:S(2)}) copy-start(f32[7]{0:T(128)} %rk_ref.3) | copy-start | bytes 88
  4.4 5.5 %copy-start.13 = (f32[7]{0:T(128)S(1)}, f32[7]{0:T(128)}, u32[]{:S(2)}) copy-start(f32[7]{0:T(128)} %ck_ref.3) | copy-start | bytes 88
  4.4 5.5 %copy-start.7 = (f32[1,2048]{1,0:T(1,128)S(1)}, f32[1,2048]{1,0:T(1,128)}, u32[]{:S(2)}) copy-start(f32[1,2048]{1,0:T(1,128)} %constant.19.clone.win_ref) | copy-start | bytes 24580
  4.5 5.5 %collective-permute-start.1 = (bf16[8,3584]{1,0:T(8,128)(2,1)S(1)}, bf16[8,3584]{1,0:T(8,128)(2,1)S(1)}, u32[]{:S(2)}, u32[]{:S(2)}) collective-permute-start(bf16[8,3584]{1,0:T(8,128)(2,1)S(1)} %pad_maximum_fusion.1), channel_id=1, source_target_pairs={{1,0},{2,1},{3,2},{4,3},{5,4},{6,5},{7,6},{9,8},{10,9},{11,10},{12... | collective-permute-start | bytes 172040 | tf_op jit(solution)/shard_map/ppermute | solution.py:380
  8.1 1.8 %copy-start.9 = (s32[1,512]{1,0:T(1,128)S(1)}, s32[1,512]{1,0:T(1,128)}, u32[]{:S(2)}) copy-start(s32[1,512]{1,0:T(1,128)} %cell_ref.3) | copy-start | bytes 6148
  8.8 1.2 %copy-start.10 = (s32[32]{0:T(128)S(1)}, s32[32]{0:T(128)}, u32[]{:S(2)}) copy-start(s32[32]{0:T(128)} %offs_ref.5) | copy-start | bytes 388
  8.8 1.2 %copy-start.11 = (s32[32]{0:T(128)S(1)}, s32[32]{0:T(128)}, u32[]{:S(2)}) copy-start(s32[32]{0:T(128)} %order_ref.5) | copy-start | bytes 388
  12.9 32.5 %copy-start.1 = (bf16[512,256]{1,0:T(8,128)(2,1)S(1)}, bf16[512,256]{1,0:T(8,128)(2,1)}, u32[]{:S(2)}) copy-start(bf16[512,256]{1,0:T(8,128)(2,1)} %constant.21.clone.wt_tab_ref) | copy-start | bytes 786436
  12.9 32.4 %copy-start.2 = (bf16[256,512]{1,0:T(8,128)(2,1)S(1)}, bf16[256,512]{1,0:T(8,128)(2,1)}, u32[]{:S(2)}) copy-start(bf16[256,512]{1,0:T(8,128)(2,1)} %constant.20.clone.w_ref) | copy-start | bytes 786436
  12.9 32.4 %copy-start.3 = (f32[1,32,512]{2,1,0:T(8,128)S(1)}, f32[1,32,512]{2,1,0:T(8,128)}, u32[]{:S(2)}) copy-start(f32[1,32,512]{2,1,0:T(8,128)} %param.22) | copy-start | bytes 196612
  12.9 32.4 %copy-start.8 = (f32[2,32,128]{2,1,0:T(8,128)S(1)}, f32[2,32,128]{2,1,0:T(8,128)}, u32[]{:S(2)}) copy-start(f32[2,32,128]{2,1,0:T(8,128)} %constant.22.clone.ph_ref) | copy-start | bytes 98308
  48.7 23.2 %copy-start.6 = (bf16[256,256]{1,0:T(8,128)(2,1)S(1)}, bf16[256,256]{1,0:T(8,128)(2,1)}, u32[]{:S(2)}) copy-start(bf16[256,256]{1,0:T(8,128)(2,1)} %constant.23.clone.tab_ref) | copy-start | bytes 393220

commit v4 on v3

--- a/solution.py
+++ b/solution.py
@@ -128,51 +128,36 @@
 
 
 def k1_body(
-    offs_ref, order_ref, ck_ref, facet_ref, count_ref, rk_ref, sky_ref, before_ref, after_ref,
-    win_ref, tab_ref, cell_ref, out_ref, ext_ref, conv_ref, tw_ref, lhs_ref, u_ref, nat_ref,
+    offs_ref, order_ref, facet_ref, count_ref, rk_ref, ck_ref, sky_ref, win_ref, tab_ref, cell_ref,
+    out_ref, tw_ref, lhs_ref, u_ref, nat_ref,
 ):
     tw_ref[0], tw_ref[1] = twiddles(facet_ref[0])
-    for b in range(16):
-        lanes = slice(128 * b, 128 * (b + 1))
-        win = win_ref[:, lanes]
-        ext_ref[8:16, lanes] = before_ref[:, lanes].astype(F32) * win
-        ext_ref[16:48, lanes] = sky_ref[:, lanes].astype(F32) * win
-        ext_ref[48:56, lanes] = after_ref[:, lanes].astype(F32) * win
-    for b in range(16):
-        lanes = slice(128 * b, 128 * (b + 1))
-        own = jnp.zeros((CB, 128), F32)
-        lo = jnp.zeros((8, 128), F32)
-        hi = jnp.zeros((8, 128), F32)
-        for t in range(TAPS):
-            k = ck_ref[t]
-            own = own + k * ext_ref[13 + t : 45 + t, lanes]
-            lo = lo + k * ext_ref[5 + t : 13 + t, lanes]
-            hi = hi + k * ext_ref[45 + t : 53 + t, lanes]
-        conv_ref[0:CB, lanes] = own
-        conv_ref[CB:CE, lanes] = halo_rows(hi, lo, 0)
-        conv_ref[CE : CE + 8, lanes] = jnp.zeros((8, 128), F32)
-
-    for g in range(3):
+    for g in range(2):
         rows = slice(16 * g, 16 * (g + 1))
-        a = real_transform([conv_ref[rows, 128 * b : 128 * (b + 1)] for b in range(16)])
+        x = []
+        for b in range(16):
+            lanes = slice(128 * b, 128 * (b + 1))
+            x.append(sky_ref[rows, lanes].astype(F32) * win_ref[:, lanes])
+        a = real_transform(x)
         for m in range(16):
             ar, ai = a[m] if m <= 8 else (a[16 - m][0], -a[16 - m][1])
             c, s = tw_ref[0, m : m + 1, :], tw_ref[1, m : m + 1, :]
             lhs_ref[m, rows, 0:128] = (ar * c + ai * s).astype(BF)
             lhs_ref[m, rows, 128:256] = (ai * c - ar * s).astype(BF)
-    u = jnp.dot(lhs_ref[...].reshape(16 * 48, 256), tab_ref[...], preferred_element_type=F32)
-    u_ref[...] = u.reshape(16, 48, 256)
+    u = jnp.dot(lhs_ref[...].reshape(16 * CB, 256), tab_ref[...], preferred_element_type=F32)
+    u_ref[...] = u.reshape(16, CB, 256)
 
     lane = lax.broadcasted_iota(jnp.int32, (8, 128), 1)
-    for g in range(5):
+    for g in range(4):
         rows = slice(8 * g, 8 * (g + 1))
         for p in range(2):
-            x = swap_index([u_ref[m, rows, 128 * p : 128 * (p + 1)] for m in range(16)], lane)
+            cols = slice(128 * p, 128 * (p + 1))
+            x = swap_index([u_ref[m, rows, cols] for m in range(16)], lane)
             for b in range(16):
-                nat_ref[b, rows, 128 * p : 128 * (p + 1)] = x[b]
-            nat_ref[16, rows, 128 * p : 128 * (p + 1)] = x[0]
-
-    lane = lax.broadcasted_iota(jnp.int32, (CE, 128), 1)
+                nat_ref[b, rows, cols] = x[b]
+            nat_ref[16, rows, cols] = x[0]
+
+    lane = lax.broadcasted_iota(jnp.int32, (CB, 128), 1)
     for i in range(NF):
         off = offs_ref[order_ref[i]]
         b, s = off >> 7, off & 127
@@ -189,40 +174,86 @@
 PARAMS = pltpu.CompilerParams(vmem_limit_bytes=24 * 1024 * 1024)
 
 
-def k1(offs, order, ck, facet, count, rk, sky, before, after, cell):
+def k1(offs, order, facet, count, rk, ck, sky, cell):
     return pl.pallas_call(
         k1_body,
-        out_shape=jax.ShapeDtypeStruct((NF, CE, 2 * XC), BF),
-        in_specs=[SMEM] * 6 + [VMEM] * 6,
+        out_shape=jax.ShapeDtypeStruct((NF, CB, 2 * XC), BF),
+        in_specs=[SMEM] * 6 + [VMEM] * 4,
         out_specs=VMEM,
         scratch_shapes=[
-            pltpu.VMEM((64, FR), F32),
-            pltpu.VMEM((48, FR), F32),
             pltpu.VMEM((2, 16, 128), F32),
-            pltpu.VMEM((16, 48, 256), BF),
-            pltpu.VMEM((16, 48, 256), F32),
-            pltpu.VMEM((17, CE, 256), F32),
+            pltpu.VMEM((16, CB, 256), BF),
+            pltpu.VMEM((16, CB, 256), F32),
+            pltpu.VMEM((17, CB, 256), F32),
         ],
         compiler_params=PARAMS,
         name="facet_to_slots",
     )(
-        offs, order, ck, facet, count, rk, sky, before, after, window(),
-        jnp.asarray(block_table(), BF), cell,
-    )
-
-
-def k2_body(
-    offs_ref, order_ref, facet_ref, count_ref, rk_ref, ck_ref, arr_ref, cell_ref, obs_ref, wt_ref,
-    before_ref, after_ref, w_ref, wt_tab_ref, ph_ref,
-    res_ref, out_ref, lhs_ref, u_ref, dt_ref, ext_ref, y_ref, pho_ref,
-):
-    for f in range(NF):
-        lhs_ref[f, 0:CE, :] = arr_ref[f]
+        offs, order, facet, count, rk, ck, sky, window(), jnp.asarray(block_table(), BF), cell
+    )
+
+
+def slot_phases(offs_ref, order_ref, facet_ref, ph_ref, pho_ref):
     off = offs_ref[order_ref[facet_ref[0]]]
     back = (128 - 2 * off) & 127
     pho_ref[0] = pltpu.roll(ph_ref[0], back, 1)
     pho_ref[1] = pltpu.roll(ph_ref[1], back, 1)
 
+
+def ka_body(
+    offs_ref, order_ref, facet_ref, arr_ref, obs_ref, wt_ref, w_ref, ph_ref,
+    sub_ref, first_ref, last_ref, u_ref, pho_ref,
+):
+    slot_phases(offs_ref, order_ref, facet_ref, ph_ref, pho_ref)
+    u = jnp.dot(arr_ref[...].reshape(NF * CB, 256), w_ref[...], preferred_element_type=F32)
+    u_ref[...] = u.reshape(NF, CB, 2 * SG)
+    for h in range(2):
+        re = jnp.zeros((CB, 128), F32)
+        im = jnp.zeros((CB, 128), F32)
+        for f in range(NF):
+            ur = u_ref[f, :, 128 * h : 128 * (h + 1)]
+            ui = u_ref[f, :, SG + 128 * h : SG + 128 * (h + 1)]
+            pc = pho_ref[0, f : f + 1, :]
+            ps = pho_ref[1, f : f + 1, :]
+            re = re + (ur * pc - ui * ps)
+            im = im + (ur * ps + ui * pc)
+        sub_ref[:, 128 * h : 128 * (h + 1)] = re
+        sub_ref[:, SG + 128 * h : SG + 128 * (h + 1)] = im
+    for ref, rows in ((first_ref, slice(0, 8)), (last_ref, slice(24, 32))):
+        ref[:, 0 : 2 * SG] = sub_ref[rows, :].astype(BF)
+        ref[:, 2 * SG : 2 * SG + VM] = obs_ref[0, rows, :]
+        ref[:, 2 * SG + VM : 2 * SG + 2 * VM] = obs_ref[1, rows, :]
+        ref[:, 2 * SG + 2 * VM :] = wt_ref[rows, :].astype(BF)
+
+
+EDGE = 2 * SG + 3 * VM
+
+
+def ka(offs, order, facet, arrived, obs, wt):
+    return pl.pallas_call(
+        ka_body,
+        out_shape=(
+            jax.ShapeDtypeStruct((CB, 2 * SG), F32),
+            jax.ShapeDtypeStruct((8, EDGE), BF),
+            jax.ShapeDtypeStruct((8, EDGE), BF),
+        ),
+        in_specs=[SMEM] * 3 + [VMEM] * 5,
+        out_specs=(VMEM, VMEM, VMEM),
+        scratch_shapes=[
+            pltpu.VMEM((NF, CB, 2 * SG), F32),
+            pltpu.VMEM((2, NF, 128), F32),
+        ],
+        compiler_params=PARAMS,
+        name="sum_facets",
+    )(offs, order, facet, arrived, obs, wt, jnp.asarray(subgrid_table(), BF), facet_phase())
+
+
+def kb_body(
+    offs_ref, order_ref, facet_ref, count_ref, rk_ref, ck_ref, sub_ref, cell_ref, obs_ref, wt_ref,
+    before_ref, after_ref, wt_tab_ref, ph_ref,
+    res_ref, out_ref, dt_ref, sub_ext_ref, ext_ref, y_ref, pho_ref,
+):
+    slot_phases(offs_ref, order_ref, facet_ref, ph_ref, pho_ref)
     cell = cell_ref[...]
     d = lax.broadcasted_iota(jnp.int32, (SG, VM), 0) - cell + 3
     m = jnp.zeros((SG, VM), F32)
@@ -230,36 +261,34 @@
         m = jnp.where(d == t, rk_ref[t], m)
     dt_ref[...] = m.astype(BF)
 
-    u = jnp.dot(lhs_ref[...].reshape(NF * 48, 256), w_ref[...], preferred_element_type=F32)
-    u_ref[...] = u.reshape(NF, 48, 2 * SG)
-    res = []
-    ims = []
-    for h in range(2):
-        re = jnp.zeros((CE, 128), F32)
-        im = jnp.zeros((CE, 128), F32)
-        for f in range(NF):
-            ur = u_ref[f, 0:CE, 128 * h : 128 * (h + 1)]
-            ui = u_ref[f, 0:CE, SG + 128 * h : SG + 128 * (h + 1)]
-            pc = pho_ref[0, f : f + 1, :]
-            ps = pho_ref[1, f : f + 1, :]
-            re = re + (ur * pc - ui * ps)
-            im = im + (ur * ps + ui * pc)
-        res.append(re)
-        ims.append(im)
-    grid = jnp.concatenate(
-        [jnp.concatenate(res, axis=1), jnp.concatenate(ims, axis=1)], axis=0
-    ).astype(BF)
+    sub_ext_ref[8:16, :] = before_ref[:, 0 : 2 * SG].astype(F32)
+    sub_ext_ref[16:48, :] = sub_ref[...]
+    sub_ext_ref[48:56, :] = after_ref[:, 0 : 2 * SG].astype(F32)
+    parts = []
+    for p in range(2):
+        lanes = slice(SG * p, SG * (p + 1))
+        own = jnp.zeros((CB, SG), F32)
+        lo = jnp.zeros((8, SG), F32)
+        hi = jnp.zeros((8, SG), F32)
+        for t in range(TAPS):
+            k = ck_ref[t]
+            own = own + k * sub_ext_ref[13 + t : 45 + t, lanes]
+            lo = lo + k * sub_ext_ref[5 + t : 13 + t, lanes]
+            hi = hi + k * sub_ext_ref[45 + t : 53 + t, lanes]
+        parts += [own, halo_rows(hi, lo, 0)]
+    grid = jnp.concatenate(parts, axis=0).astype(BF)
     model = jnp.dot(grid, dt_ref[...], preferred_element_type=F32)
 
     live = (lax.broadcasted_iota(jnp.int32, (1, VM), 1) < count_ref[0]).astype(F32)
     wt = wt_ref[...] * live
-    wt_h = halo_rows(after_ref[:, FR + 2 * VM :], before_ref[:, FR + 2 * VM :], 0).astype(F32) * live
+    cols = slice(2 * SG + 2 * VM, EDGE)
+    wt_h = halo_rows(after_ref[:, cols].astype(F32), before_ref[:, cols].astype(F32), 0) * live
     parts = []
     for p in range(2):
         own = wt * (obs_ref[p].astype(F32) - model[p * CE : p * CE + CB])
         res_ref[p] = own
-        cols = slice(FR + p * VM, FR + (p + 1) * VM)
-        obs_h = halo_rows(after_ref[:, cols], before_ref[:, cols], 0).astype(F32)
+        cols = slice(2 * SG + p * VM, 2 * SG + (p + 1) * VM)
+        obs_h = halo_rows(after_ref[:, cols].astype(F32), before_ref[:, cols].astype(F32), 0)
         parts += [own, wt_h * (obs_h - model[p * CE + CB : (p + 1) * CE])]
     rr = jnp.concatenate(parts, axis=0).astype(BF)
     gridded = lax.dot_general(
@@ -288,20 +317,18 @@
     out_ref[...] = z.astype(BF).reshape(NF, CB, 2 * XC)
 
 
-def k2(offs, order, facet, count, rk, ck, arrived, cell, obs, wt, before, after):
-    tab = subgrid_table()
+def kb(offs, order, facet, count, rk, ck, sub, cell, obs, wt, before, after):
     return pl.pallas_call(
-        k2_body,
+        kb_body,
         out_shape=(
             jax.ShapeDtypeStruct((2, CB, VM), F32),
             jax.ShapeDtypeStruct((NF, CB, 2 * XC), BF),
         ),
-        in_specs=[SMEM] * 6 + [VMEM] * 9,
+        in_specs=[SMEM] * 6 + [VMEM] * 8,
         out_specs=(VMEM, VMEM),
         scratch_shapes=[
-            pltpu.VMEM((NF, 48, 256), BF),
-            pltpu.VMEM((NF, 48, 2 * SG), F32),
             pltpu.VMEM((SG, VM), BF),
+            pltpu.VMEM((64, 2 * SG), F32),
             pltpu.VMEM((2, 48, SG), F32),
             pltpu.VMEM((NF, CB, 2 * SG), BF),
             pltpu.VMEM((2, NF, 128), F32),
@@ -309,8 +336,8 @@
         compiler_params=PARAMS,
         name="slot_round_trip",
     )(
-        offs, order, facet, count, rk, ck, arrived, cell, obs, wt, before, after,
-        jnp.asarray(tab, BF), jnp.asarray(tab.T, BF), facet_phase(),
+        offs, order, facet, count, rk, ck, sub, cell, obs, wt, before, after,
+        jnp.asarray(subgrid_table().T, BF), facet_phase(),
     )
 
 
@@ -388,20 +415,16 @@
     obs = observed[0]
     wt = visibility_weight[0]
 
-    def edge(rows):
-        return jnp.concatenate(
-            [sky_image[rows], obs[0, rows], obs[1, rows], wt[rows].astype(BF)], axis=1
-        )
-
-    before, after = neighbours(edge(slice(0, 8)), edge(slice(24, 32)))
     out = k1(
-        subgrid_offsets, owner_order, column_kernel, facet, visibility_count, row_kernel,
-        sky_image, before, after, visibility_cell,
+        subgrid_offsets, owner_order, facet, visibility_count, row_kernel, column_kernel,
+        sky_image, visibility_cell,
     )
     arrived = lax.all_to_all(out, "facet", split_axis=0, concat_axis=0, tiled=True)
-    res, outgoing = k2(
+    sub, first, last = ka(subgrid_offsets, owner_order, facet, arrived, obs, wt)
+    before, after = neighbours(first, last)
+    res, outgoing = kb(
         subgrid_offsets, owner_order, facet, visibility_count, row_kernel, column_kernel,
-        arrived, visibility_cell, obs, wt, before, after,
+        sub, visibility_cell, obs, wt, before, after,
     )
     back = lax.all_to_all(outgoing, "facet", split_axis=0, concat_axis=0, tiled=True)
     dirty = k3(subgrid_offsets, owner_order, facet, back)

time: 74.5 us -> 71.6 us (0.961)
  blocking collectives: 55.6 us -> 52.1 us
  local copies, waits for them, and re-layouts: 0.92 us -> 2.5 us
  other arithmetic: 0.86 us -> 0 us
    all_to_all x1, blocking collectives: 32.4 us -> 28.7 us  [local(): lax.all_to_all(out, 'facet', split_axis=0, concat_axis=0, tiled=True)]
    unnamed x28, local copies, waits for them, and re-layouts: 0.11 us -> 2.5 us
    another operation x1 -> x0, other arithmetic: 0.85 us -> none
    slice x1 -> x0, local copies, waits for them, and re-layouts: 0.81 us -> none  [edge(): sky_image[rows]]
    pallas_call x2 -> x3, Pallas kernels: 6.28 us -> 5.57 us  [the longest x1 2.63 us: kb(): pl.pallas_call(kb_body, out_shape=(jax.ShapeDtypeStruct((2, CB, VM), F32)...]
where the time goes in v4:
time: 71.6 us; the launch traced here: 71 us
  blocking collectives  52.1 us (73%)
  Pallas kernels  7.76 us (11%)
  starting transfers between devices  5.56 us (8%)
  local copies, waits for them, and re-layouts  2.5 us (3%)
  waiting for transfers between devices  1.57 us (2%)
  between operations  1.49 us (2%)
    all_to_all x1, blocking collectives, local(): lax.all_to_all(out, 'facet', split_axis=0, concat_axis=0, tiled=True)  28.7 us
    all_to_all x1, blocking collectives, local(): lax.all_to_all(outgoing, 'facet', split_axis=0, concat_axis=0, tiled=True)  23.4 us
    ppermute x2, starting transfers between devices, neighbours(): return (lax.ppermute(last, 'uv', up), lax.ppermute(first, 'uv', down))  5.56 us
    pallas_call x1, Pallas kernels, kb(): pl.pallas_call(kb_body, out_shape=(jax.ShapeDtypeStruct((2, CB, VM), F32)...  2.63 us
    unnamed x28, local copies, waits for them, and re-layouts  2.5 us
    pallas_call x1, Pallas kernels, k3(): pl.pallas_call(k3_body, out_shape=jax.ShapeDtypeStruct((CB, FR), F32), in...  2.19 us
    pallas_call x1, Pallas kernels, k1(): pl.pallas_call(k1_body, out_shape=jax.ShapeDtypeStruct((NF, CB, 2 * XC),...  1.95 us
    ppermute x2, waiting for transfers between devices, neighbours(): return (lax.ppermute(last, 'uv', up), lax.ppermute(first, 'uv', down))  1.57 us
  transfers between devices with their start and end apart: 2, of which 1 were waited for; matrix products, arithmetic and copies ran while one was open for 0% of the time, Pallas kernels for 0%

profile of v4, /device:TPU:48, one launch (start us, length us, event | category | flops | bytes accessed | tf_op | source)
XLA Modules:
  0.0 71.0 jit_solution(2994537289435789191)
XLA Ops:
  0.6 0.0 copy-start.8
  0.6 0.0 copy-start.13
  0.7 0.0 copy-start.9
  1.4 0.6 copy-done.10
  2.0 0.0 copy-done.11
  2.0 0.0 copy-done.12
  2.0 0.9 %copy-done.4 = bf16[32,2048]{1,0:T(8,128)(2,1)S(1)} copy-done((bf16[32,2048]{1,0:T(8,128)(2,1)S(1)}, bf16[32,2048]{1,0:T(8,128)(2,1)}, u32[]{:S(2)}) %copy-start.4) | copy-done | bytes 131096
  2.9 0.9 %copy-done.5 = bf16[256,256]{1,0:T(8,128)(2,1)S(1)} copy-done((bf16[256,256]{1,0:T(8,128)(2,1)S(1)}, bf16[256,256]{1,0:T(8,128)(2,1)}, u32[]{:S(2)}) %copy-start.5) | copy-done | bytes 131096
  3.8 1.9 %facet_to_slots.1 = bf16[32,32,256]{2,1,0:T(8,128)(2,1)S(1)} custom-call(s32[32]{0:T(128)S(1)} %copy-done.10, s32[32]{0:T(128)S(1)} %copy-done.11, s32[1]{0:T(128)} %bitcast.facet_ref, s32[1]{0:T(128)S(6)} %copy.19.count_ref, f32[7]{0:T(128)S(1)} %copy-done.12, f32[7]{0:T(128)S(1)} %copy-done.13, bf16[32,2048]{1,0:T(8,128)(2,1)S(1)} %copy-done.4, ...), custom_call_target="tpu_custom_call" | custom-call | tf_op jit(solution)/shard_map/facet_to_slots/pallas_call | solution.py:178
  5.8 0.0 copy-start
  5.8 0.0 copy-start.1
  5.8 0.0 copy-start.3
  5.8 0.0 copy-start.6
  5.8 28.7 %all_to_all.10.arr_ref = bf16[32,32,256]{2,1,0:T(8,128)(2,1)S(1)} all-to-all(bf16[32,32,256]{2,1,0:T(8,128)(2,1)S(1)} %facet_to_slots.1), channel_id=1, replica_groups=mesh['facet'=32,'uv'=8] {'facet'}, dimensions={0} | all-to-all | bytes 1048576 | tf_op jit(solution)/shard_map/all_to_all | solution.py:422
  34.6 0.0 copy-start.2
  34.6 1.0 %sum_facets.1 = (f32[32,512]{1,0:T(8,128)S(1)}, bf16[8,2048]{1,0:T(8,128)(2,1)S(1)}, bf16[8,2048]{1,0:T(8,128)(2,1)S(1)}) custom-call(s32[32]{0:T(128)S(1)} %copy-done.10, s32[32]{0:T(128)S(1)} %copy-done.11, s32[1]{0:T(128)} %bitcast.facet_ref, bf16[32,32,256]{2,1,0:T(8,128)(2,1)S(1)} %all_to_all.10.arr_ref, bf16[2,32,512]{2,1,0:T(8,128)(2,1)S(1)} %bitcast.4, ...), custom_call_target="tpu_custom_call" | custom-call | tf_op jit(solution)/shard_map/sum_facets/pallas_call | solution.py:233
  35.6 1.9 %collective-permute-start = (bf16[8,2048]{1,0:T(8,128)(2,1)S(1)}, bf16[8,2048]{1,0:T(8,128)(2,1)S(1)}, u32[]{:S(2)}, u32[]{:S(2)}) collective-permute-start(bf16[8,2048]{1,0:T(8,128)(2,1)S(1)} %get-tuple-element.8), channel_id=1, source_target_pairs={{0,1},{1,2},{2,3},{3,4},{4,5},{5,6},{6,7},{8,9},{9,10},{10,11},{11... | collective-permute-start | bytes 98312 | tf_op jit(solution)/shard_map/ppermute | solution.py:407
  37.5 3.6 %collective-permute-start.1 = (bf16[8,2048]{1,0:T(8,128)(2,1)S(1)}, bf16[8,2048]{1,0:T(8,128)(2,1)S(1)}, u32[]{:S(2)}, u32[]{:S(2)}) collective-permute-start(bf16[8,2048]{1,0:T(8,128)(2,1)S(1)} %get-tuple-element.9), channel_id=1, source_target_pairs={{1,0},{2,1},{3,2},{4,3},{5,4},{6,5},{7,6},{9,8},{10,9},{11,10},{12... | collective-permute-start | bytes 98312 | tf_op jit(solution)/shard_map/ppermute | solution.py:407
  41.2 0.0 collective-permute-done.before_ref
  41.2 1.6 %collective-permute-done.1.after_ref = bf16[8,2048]{1,0:T(8,128)(2,1)S(1)} collective-permute-done((bf16[8,2048]{1,0:T(8,128)(2,1)S(1)}, bf16[8,2048]{1,0:T(8,128)(2,1)S(1)}, u32[]{:S(2)}, u32[]{:S(2)}) %collective-permute-start.1) | collective-permute-done | bytes 32800 | tf_op jit(solution)/shard_map/ppermute | solution.py:407
  42.8 2.6 %slot_round_trip.1 = (f32[2,32,512]{2,1,0:T(8,128)}, bf16[32,32,256]{2,1,0:T(8,128)(2,1)S(1)}) custom-call(s32[32]{0:T(128)S(1)} %copy-done.10, s32[32]{0:T(128)S(1)} %copy-done.11, s32[1]{0:T(128)} %bitcast.facet_ref, s32[1]{0:T(128)S(6)} %copy.19.count_ref, f32[7]{0:T(128)S(1)} %copy-done.12, f32[7]{0:T(128)S(1)} %copy-done.13, ...), custom_call_target="tpu_custom_call" | custom-call | tf_op jit(solution)/shard_map/slot_round_trip/pallas_call | solution.py:321
  45.4 0.0 copy-start.7
  45.4 23.4 %all_to_all.11.bp_ref = bf16[32,32,256]{2,1,0:T(8,128)(2,1)S(1)} all-to-all(bf16[32,32,256]{2,1,0:T(8,128)(2,1)S(1)} %get-tuple-element.11), channel_id=1, replica_groups=mesh['facet'=32,'uv'=8] {'facet'}, dimensions={0} | all-to-all | bytes 1048576 | tf_op jit(solution)/shard_map/all_to_all | solution.py:429
  68.8 2.2 %slots_to_facet.1 = f32[32,2048]{1,0:T(8,128)} custom-call(s32[32]{0:T(128)S(1)} %copy-done.10, s32[32]{0:T(128)S(1)} %copy-done.11, s32[1]{0:T(128)} %bitcast.facet_ref, bf16[32,32,256]{2,1,0:T(8,128)(2,1)S(1)} %all_to_all.11.bp_ref, f32[1,2048]{1,0:T(1,128)S(1)} %copy-done.8, bf16[256,256]{1,0:T(8,128)(2,1)S(1)} %copy-done.7), custom_call_target="tpu_custom_call" | custom-call | tf_op jit(solution)/shard_map/slots_to_facet/pallas_call | solution.py:387
  (14 shorter events, 0.0 us)
Async XLA Ops:
  0.6 0.7 %copy-start.8 = (f32[1,2048]{1,0:T(1,128)S(1)}, f32[1,2048]{1,0:T(1,128)}, u32[]{:S(2)}) copy-start(f32[1,2048]{1,0:T(1,128)} %constant.19.clone.win_ref) | copy-start | bytes 24580
  0.6 0.7 %copy-start.13 = (f32[7]{0:T(128)S(1)}, f32[7]{0:T(128)}, u32[]{:S(2)}) copy-start(f32[7]{0:T(128)} %ck_ref.3) | copy-start | bytes 88
  0.7 0.7 %copy-start.9 = (s32[1,512]{1,0:T(1,128)S(1)}, s32[1,512]{1,0:T(1,128)}, u32[]{:S(2)}) copy-start(s32[1,512]{1,0:T(1,128)} %cell_ref.3) | copy-start | bytes 6148
  1.3 0.7 copy-start.10
  1.3 0.7 copy-start.11
  1.4 0.7 copy-start.12
  2.0 0.9 %copy-start.4 = (bf16[32,2048]{1,0:T(8,128)(2,1)S(1)}, bf16[32,2048]{1,0:T(8,128)(2,1)}, u32[]{:S(2)}) copy-start(bf16[32,2048]{1,0:T(8,128)(2,1)} %sky_ref.1) | copy-start | bytes 393220
  2.9 0.9 %copy-start.5 = (bf16[256,256]{1,0:T(8,128)(2,1)S(1)}, bf16[256,256]{1,0:T(8,128)(2,1)}, u32[]{:S(2)}) copy-start(bf16[256,256]{1,0:T(8,128)(2,1)} %constant.18.clone.tab_ref) | copy-start | bytes 393220
  5.8 28.8 %copy-start = (bf16[1,2,32,512]{3,2,1,0:T(8,128)(2,1)S(1)}, bf16[1,2,32,512]{3,2,1,0:T(8,128)(2,1)}, u32[]{:S(2)}) copy-start(bf16[1,2,32,512]{3,2,1,0:T(8,128)(2,1)} %param.22) | copy-start | bytes 196612
  5.8 28.8 %copy-start.1 = (f32[1,32,512]{2,1,0:T(8,128)S(1)}, f32[1,32,512]{2,1,0:T(8,128)}, u32[]{:S(2)}) copy-start(f32[1,32,512]{2,1,0:T(8,128)} %param.23) | copy-start | bytes 196612
  5.8 28.8 %copy-start.3 = (bf16[256,512]{1,0:T(8,128)(2,1)S(1)}, bf16[256,512]{1,0:T(8,128)(2,1)}, u32[]{:S(2)}) copy-start(bf16[256,512]{1,0:T(8,128)(2,1)} %constant.20.clone.w_ref) | copy-start | bytes 786436
  5.8 28.8 %copy-start.6 = (f32[2,32,128]{2,1,0:T(8,128)S(1)}, f32[2,32,128]{2,1,0:T(8,128)}, u32[]{:S(2)}) copy-start(f32[2,32,128]{2,1,0:T(8,128)} %constant.21.clone.ph_ref) | copy-start | bytes 98308
  34.6 8.2 %copy-start.2 = (bf16[512,256]{1,0:T(8,128)(2,1)S(1)}, bf16[512,256]{1,0:T(8,128)(2,1)}, u32[]{:S(2)}) copy-start(bf16[512,256]{1,0:T(8,128)(2,1)} %constant.22.clone.wt_tab_ref) | copy-start | bytes 786436
  35.6 5.6 %collective-permute-start = (bf16[8,2048]{1,0:T(8,128)(2,1)S(1)}, bf16[8,2048]{1,0:T(8,128)(2,1)S(1)}, u32[]{:S(2)}, u32[]{:S(2)}) collective-permute-start(bf16[8,2048]{1,0:T(8,128)(2,1)S(1)} %get-tuple-element.8), channel_id=1, source_target_pairs={{0,1},{1,2},{2,3},{3,4},{4,5},{5,6},{6,7},{8,9},{9,10},{10,11},{11... | collective-permute-start | bytes 98312 | tf_op jit(solution)/shard_map/ppermute | solution.py:407
  37.5 5.2 %collective-permute-start.1 = (bf16[8,2048]{1,0:T(8,128)(2,1)S(1)}, bf16[8,2048]{1,0:T(8,128)(2,1)S(1)}, u32[]{:S(2)}, u32[]{:S(2)}) collective-permute-start(bf16[8,2048]{1,0:T(8,128)(2,1)S(1)} %get-tuple-element.9), channel_id=1, source_target_pairs={{1,0},{2,1},{3,2},{4,3},{5,4},{6,5},{7,6},{9,8},{10,9},{11,10},{12... | collective-permute-start | bytes 98312 | tf_op jit(solution)/shard_map/ppermute | solution.py:407
  45.4 23.4 %copy-start.7 = (bf16[256,256]{1,0:T(8,128)(2,1)S(1)}, bf16[256,256]{1,0:T(8,128)(2,1)}, u32[]{:S(2)}) copy-start(bf16[256,256]{1,0:T(8,128)(2,1)} %constant.23.clone.tab_ref) | copy-start | bytes 393220

commit v5 on v4

--- a/solution.py
+++ b/solution.py
@@ -67,6 +67,29 @@
     m = lax.broadcasted_iota(jnp.int32, (16, 128), 0)
     lane = lax.broadcasted_iota(jnp.int32, (16, 128), 1)
     return turn((m * (lane + 64 + 128 * facet)) & (FR - 1))
+
+
+def make_window(win_ref):
+    for b in range(16):
+        r = lax.broadcasted_iota(jnp.int32, (8, 128), 1) + (128 * b)
+        x = (r.astype(F32) - 1023.5) * (math.pi / FR)
+        y = x * x
+        c = 1.0 / 24 + y * (-1.0 / 720 + y * (1.0 / 40320 + y * (-1.0 / 3628800 + y / 479001600)))
+        win_ref[:, 128 * b : 128 * (b + 1)] = (1.0 + y * (-0.5 + y * c)) * (1.0 / math.sqrt(FR))
+
+
+def make_block_table(tab_ref, transposed=False):
+    lane = lax.broadcasted_iota(jnp.int32, (128, 128), 0 if transposed else 1)
+    row = lax.broadcasted_iota(jnp.int32, (128, 128), 1 if transposed else 0) + 64
+    g = 8 * (lane & 15) + (lane >> 4)
+    c, s = turn((16 * g * row) & (FR - 1))
+    c, s, t = c.astype(BF), s.astype(BF), (-s).astype(BF)
+    if transposed:
+        s, t = t, s
+    tab_ref[0:128, 0:128] = c
+    tab_ref[0:128, 128:256] = t
+    tab_ref[128:256, 0:128] = s
+    tab_ref[128:256, 128:256] = c
 
 
 def cmul(a, w):
@@ -128,16 +151,21 @@
 
 
 def k1_body(
-    offs_ref, order_ref, facet_ref, count_ref, rk_ref, ck_ref, sky_ref, win_ref, tab_ref, cell_ref,
-    out_ref, tw_ref, lhs_ref, u_ref, nat_ref,
+    offs_ref, order_ref, sky_hbm,
+    out_ref, tw_ref, lhs_ref, u_ref, nat_ref, sky_ref, win_ref, tab_ref, sem,
 ):
-    tw_ref[0], tw_ref[1] = twiddles(facet_ref[0])
+    copy = pltpu.make_async_copy(sky_hbm, sky_ref, sem)
+    copy.start()
+    tw_ref[0], tw_ref[1] = twiddles(lax.axis_index("facet"))
+    make_window(win_ref)
+    make_block_table(tab_ref)
+    copy.wait()
     for g in range(2):
         rows = slice(16 * g, 16 * (g + 1))
         x = []
         for b in range(16):
             lanes = slice(128 * b, 128 * (b + 1))
-            x.append(sky_ref[rows, lanes].astype(F32) * win_ref[:, lanes])
+            x.append(sky_ref[rows, lanes].astype(F32) * win_ref[0:1, lanes])
         a = real_transform(x)
         for m in range(16):
             ar, ai = a[m] if m <= 8 else (a[16 - m][0], -a[16 - m][1])
@@ -174,37 +202,38 @@
 PARAMS = pltpu.CompilerParams(vmem_limit_bytes=24 * 1024 * 1024)
 
 
-def k1(offs, order, facet, count, rk, ck, sky, cell):
+def k1(offs, order, sky):
     return pl.pallas_call(
         k1_body,
         out_shape=jax.ShapeDtypeStruct((NF, CB, 2 * XC), BF),
-        in_specs=[SMEM] * 6 + [VMEM] * 4,
+        in_specs=[SMEM] * 2 + [pl.BlockSpec(memory_space=pl.ANY)],
         out_specs=VMEM,
         scratch_shapes=[
             pltpu.VMEM((2, 16, 128), F32),
             pltpu.VMEM((16, CB, 256), BF),
             pltpu.VMEM((16, CB, 256), F32),
             pltpu.VMEM((17, CB, 256), F32),
+            pltpu.VMEM((CB, FR), BF),
+            pltpu.VMEM((8, FR), F32),
+            pltpu.VMEM((256, 256), BF),
+            pltpu.SemaphoreType.DMA,
         ],
-        compiler_params=PARAMS,
         name="facet_to_slots",
-    )(
-        offs, order, facet, count, rk, ck, sky, window(), jnp.asarray(block_table(), BF), cell
-    )
-
-
-def slot_phases(offs_ref, order_ref, facet_ref, ph_ref, pho_ref):
-    off = offs_ref[order_ref[facet_ref[0]]]
+    )(offs, order, sky)
+
+
+def slot_phases(offs_ref, order_ref, ph_ref, pho_ref):
+    off = offs_ref[order_ref[lax.axis_index("facet")]]
     back = (128 - 2 * off) & 127
     pho_ref[0] = pltpu.roll(ph_ref[0], back, 1)
     pho_ref[1] = pltpu.roll(ph_ref[1], back, 1)
 
 
 def ka_body(
-    offs_ref, order_ref, facet_ref, arr_ref, obs_ref, wt_ref, w_ref, ph_ref,
-    sub_ref, first_ref, last_ref, u_ref, pho_ref,
+    offs_ref, order_ref, arr_ref, obs_ref, wt_ref, w_ref, ph_ref,
+    sub_ref, sibling_ref, neighbour_ref, u_ref, pho_ref,
 ):
-    slot_phases(offs_ref, order_ref, facet_ref, ph_ref, pho_ref)
+    slot_phases(offs_ref, order_ref, ph_ref, pho_ref)
     u = jnp.dot(arr_ref[...].reshape(NF * CB, 256), w_ref[...], preferred_element_type=F32)
     u_ref[...] = u.reshape(NF, CB, 2 * SG)
     for h in range(2):
@@ -219,17 +248,27 @@
             im = im + (ur * ps + ui * pc)
         sub_ref[:, 128 * h : 128 * (h + 1)] = re
         sub_ref[:, SG + 128 * h : SG + 128 * (h + 1)] = im
-    for ref, rows in ((first_ref, slice(0, 8)), (last_ref, slice(24, 32))):
-        ref[:, 0 : 2 * SG] = sub_ref[rows, :].astype(BF)
-        ref[:, 2 * SG : 2 * SG + VM] = obs_ref[0, rows, :]
-        ref[:, 2 * SG + VM : 2 * SG + 2 * VM] = obs_ref[1, rows, :]
-        ref[:, 2 * SG + 2 * VM :] = wt_ref[rows, :].astype(BF)
+    even = lax.rem(lax.axis_index("uv"), 2) == 0
+    wide = 2 * SG
+
+    def put(cols, first, last):
+        sibling_ref[:, cols] = jnp.where(even, last, first).astype(BF)
+        neighbour_ref[:, cols] = jnp.where(even, first, last).astype(BF)
+
+    put(slice(0, wide), sub_ref[0:8, :], sub_ref[24:32, :])
+    for p in range(2):
+        put(
+            slice(wide + p * VM, wide + (p + 1) * VM),
+            obs_ref[p, 0:8, :].astype(F32),
+            obs_ref[p, 24:32, :].astype(F32),
+        )
+    put(slice(wide + 2 * VM, EDGE), wt_ref[0:8, :], wt_ref[24:32, :])
 
 
 EDGE = 2 * SG + 3 * VM
 
 
-def ka(offs, order, facet, arrived, obs, wt):
+def ka(offs, order, arrived, obs, wt):
     return pl.pallas_call(
         ka_body,
         out_shape=(
@@ -237,7 +276,7 @@
             jax.ShapeDtypeStruct((8, EDGE), BF),
             jax.ShapeDtypeStruct((8, EDGE), BF),
         ),
-        in_specs=[SMEM] * 3 + [VMEM] * 5,
+        in_specs=[SMEM] * 2 + [VMEM] * 5,
         out_specs=(VMEM, VMEM, VMEM),
         scratch_shapes=[
             pltpu.VMEM((NF, CB, 2 * SG), F32),
@@ -245,15 +284,15 @@
         ],
         compiler_params=PARAMS,
         name="sum_facets",
-    )(offs, order, facet, arrived, obs, wt, jnp.asarray(subgrid_table(), BF), facet_phase())
+    )(offs, order, arrived, obs, wt, jnp.asarray(subgrid_table(), BF), facet_phase())
 
 
 def kb_body(
-    offs_ref, order_ref, facet_ref, count_ref, rk_ref, ck_ref, sub_ref, cell_ref, obs_ref, wt_ref,
-    before_ref, after_ref, wt_tab_ref, ph_ref,
+    offs_ref, order_ref, count_ref, rk_ref, ck_ref, sub_ref, cell_ref, obs_ref, wt_ref,
+    sibling_ref, neighbour_ref, wt_tab_ref, ph_ref,
     res_ref, out_ref, dt_ref, sub_ext_ref, ext_ref, y_ref, pho_ref,
 ):
-    slot_phases(offs_ref, order_ref, facet_ref, ph_ref, pho_ref)
+    slot_phases(offs_ref, order_ref, ph_ref, pho_ref)
     cell = cell_ref[...]
     d = lax.broadcasted_iota(jnp.int32, (SG, VM), 0) - cell + 3
     m = jnp.zeros((SG, VM), F32)
@@ -261,9 +300,20 @@
         m = jnp.where(d == t, rk_ref[t], m)
     dt_ref[...] = m.astype(BF)
 
-    sub_ext_ref[8:16, :] = before_ref[:, 0 : 2 * SG].astype(F32)
+    uv = lax.axis_index("uv")
+    even = lax.rem(uv, 2) == 0
+    in_before, in_after = uv > 0, uv < 7
+
+    def sides(cols):
+        s, n = sibling_ref[:, cols].astype(F32), neighbour_ref[:, cols].astype(F32)
+        before = jnp.where(in_before, jnp.where(even, n, s), 0.0)
+        after = jnp.where(in_after, jnp.where(even, s, n), 0.0)
+        return before, after
+
+    before, after = sides(slice(0, 2 * SG))
+    sub_ext_ref[8:16, :] = before
     sub_ext_ref[16:48, :] = sub_ref[...]
-    sub_ext_ref[48:56, :] = after_ref[:, 0 : 2 * SG].astype(F32)
+    sub_ext_ref[48:56, :] = after
     parts = []
     for p in range(2):
         lanes = slice(SG * p, SG * (p + 1))
@@ -281,14 +331,14 @@
 
     live = (lax.broadcasted_iota(jnp.int32, (1, VM), 1) < count_ref[0]).astype(F32)
     wt = wt_ref[...] * live
-    cols = slice(2 * SG + 2 * VM, EDGE)
-    wt_h = halo_rows(after_ref[:, cols].astype(F32), before_ref[:, cols].astype(F32), 0) * live
+    before, after = sides(slice(2 * SG + 2 * VM, EDGE))
+    wt_h = halo_rows(after, before, 0) * live
     parts = []
     for p in range(2):
         own = wt * (obs_ref[p].astype(F32) - model[p * CE : p * CE + CB])
         res_ref[p] = own
-        cols = slice(2 * SG + p * VM, 2 * SG + (p + 1) * VM)
-        obs_h = halo_rows(after_ref[:, cols].astype(F32), before_ref[:, cols].astype(F32), 0)
+        before, after = sides(slice(2 * SG + p * VM, 2 * SG + (p + 1) * VM))
+        obs_h = halo_rows(after, before, 0)
         parts += [own, wt_h * (obs_h - model[p * CE + CB : (p + 1) * CE])]
     rr = jnp.concatenate(parts, axis=0).astype(BF)
     gridded = lax.dot_general(
@@ -317,14 +367,14 @@
     out_ref[...] = z.astype(BF).reshape(NF, CB, 2 * XC)
 
 
-def kb(offs, order, facet, count, rk, ck, sub, cell, obs, wt, before, after):
+def kb(offs, order, count, rk, ck, sub, cell, obs, wt, sibling, neighbour):
     return pl.pallas_call(
         kb_body,
         out_shape=(
             jax.ShapeDtypeStruct((2, CB, VM), F32),
             jax.ShapeDtypeStruct((NF, CB, 2 * XC), BF),
         ),
-        in_specs=[SMEM] * 6 + [VMEM] * 8,
+        in_specs=[SMEM] * 5 + [VMEM] * 8,
         out_specs=(VMEM, VMEM),
         scratch_shapes=[
             pltpu.VMEM((SG, VM), BF),
@@ -336,16 +386,16 @@
         compiler_params=PARAMS,
         name="slot_round_trip",
     )(
-        offs, order, facet, count, rk, ck, sub, cell, obs, wt, before, after,
+        offs, order, count, rk, ck, sub, cell, obs, wt, sibling, neighbour,
         jnp.asarray(subgrid_table().T, BF), facet_phase(),
     )
 
 
 def k3_body(
-    offs_ref, order_ref, facet_ref, bp_ref, win_ref, tab_ref,
+    offs_ref, order_ref, bp_ref, win_ref, tab_ref,
     out_ref, nat_ref, tw_ref, lhs_ref, v_ref,
 ):
-    tw_ref[0], tw_ref[1] = twiddles(facet_ref[0])
+    tw_ref[0], tw_ref[1] = twiddles(lax.axis_index("facet"))
     nat_ref[...] = jnp.zeros_like(nat_ref)
     lane = lax.broadcasted_iota(jnp.int32, (CB, 128), 1)
     for i in range(NF):
@@ -383,11 +433,11 @@
             out_ref[rows, lanes] = x[b] * (0.5 * win_ref[:, lanes])
 
 
-def k3(offs, order, facet, bp):
+def k3(offs, order, bp):
     return pl.pallas_call(
         k3_body,
         out_shape=jax.ShapeDtypeStruct((CB, FR), F32),
-        in_specs=[SMEM, SMEM, SMEM, VMEM, VMEM, VMEM],
+        in_specs=[SMEM, SMEM, VMEM, VMEM, VMEM],
         out_specs=VMEM,
         scratch_shapes=[
             pltpu.VMEM((17, CB, 256), F32),
@@ -397,37 +447,33 @@
         ],
         compiler_params=PARAMS,
         name="slots_to_facet",
-    )(offs, order, facet, bp, window(), jnp.asarray(block_table().T, BF))
-
-
-def neighbours(first, last):
+    )(offs, order, bp, window(), jnp.asarray(block_table().T, BF))
+
+
+def swapped(sibling, neighbour):
     n = lax.axis_size("uv")
-    up = [(i, i + 1) for i in range(n - 1)]
-    down = [(i + 1, i) for i in range(n - 1)]
-    return lax.ppermute(last, "uv", up), lax.ppermute(first, "uv", down)
+    near = [(i, i ^ 1) for i in range(n)]
+    far = [(i, (i - 1 if i % 2 == 0 else i + 1) % n) for i in range(n)]
+    return lax.ppermute(sibling, "uv", near), lax.ppermute(neighbour, "uv", far)
 
 
 def local(
     sky_image, subgrid_offsets, owner_order, visibility_count, visibility_cell, observed,
     visibility_weight, row_kernel, column_kernel,
 ):
-    facet = lax.axis_index("facet").astype(jnp.int32).reshape(1)
     obs = observed[0]
     wt = visibility_weight[0]
 
-    out = k1(
-        subgrid_offsets, owner_order, facet, visibility_count, row_kernel, column_kernel,
-        sky_image, visibility_cell,
-    )
+    out = k1(subgrid_offsets, owner_order, sky_image)
     arrived = lax.all_to_all(out, "facet", split_axis=0, concat_axis=0, tiled=True)
-    sub, first, last = ka(subgrid_offsets, owner_order, facet, arrived, obs, wt)
-    before, after = neighbours(first, last)
+    sub, sibling, neighbour = ka(subgrid_offsets, owner_order, arrived, obs, wt)
+    sibling, neighbour = swapped(sibling, neighbour)
     res, outgoing = kb(
-        subgrid_offsets, owner_order, facet, visibility_count, row_kernel, column_kernel,
-        sub, visibility_cell, obs, wt, before, after,
+        subgrid_offsets, owner_order, visibility_count, row_kernel, column_kernel,
+        sub, visibility_cell, obs, wt, sibling, neighbour,
     )
     back = lax.all_to_all(outgoing, "facet", split_axis=0, concat_axis=0, tiled=True)
-    dirty = k3(subgrid_offsets, owner_order, facet, back)
+    dirty = k3(subgrid_offsets, owner_order, back)
     return (res[None], dirty)
 
 

time: 71.6 us -> 67.4 us (0.941)
  starting transfers between devices: 5.56 us -> 0.64 us
  Pallas kernels: 7.76 us -> 9.57 us
  local copies, waits for them, and re-layouts: 2.5 us -> 0.7 us
    ppermute x2, starting transfers between devices: 5.56 us -> 0.64 us  [the longest x1 0.54 us: swapped(): lax.ppermute(neighbour, 'uv', far)]
    pallas_call x1, Pallas kernels: 1.95 us -> 3.76 us  [k1(): pl.pallas_call(k1_body, out_shape=jax.ShapeDtypeStruct((NF, CB, 2 * XC),...]
    unnamed x28 -> x24, local copies, waits for them, and re-layouts: 2.5 us -> 0.7 us
where the time goes in v5:
time: 67.4 us; the launch traced here: 66.5 us
  blocking collectives  51.9 us (77%)
  Pallas kernels  9.57 us (14%)
  waiting for transfers between devices  2.2 us (3%)
  between operations  1.43 us (2%)
  local copies, waits for them, and re-layouts  0.7 us (1%)
    all_to_all x1, blocking collectives, local(): lax.all_to_all(out, 'facet', split_axis=0, concat_axis=0, tiled=True)  28.9 us
    all_to_all x1, blocking collectives, local(): lax.all_to_all(outgoing, 'facet', split_axis=0, concat_axis=0, tiled=True)  23 us
    pallas_call x1, Pallas kernels, k1(): pl.pallas_call(k1_body, out_shape=jax.ShapeDtypeStruct((NF, CB, 2 * XC),...  3.76 us
    pallas_call x1, Pallas kernels, kb(): pl.pallas_call(kb_body, out_shape=(jax.ShapeDtypeStruct((2, CB, VM), F32)...  2.64 us
    ppermute x1, waiting for transfers between devices, swapped(): lax.ppermute(neighbour, 'uv', far)  2.2 us
    pallas_call x1, Pallas kernels, k3(): pl.pallas_call(k3_body, out_shape=jax.ShapeDtypeStruct((CB, FR), F32), in...  2.18 us
  transfers between devices with their start and end apart: 2, of which 1 were waited for; matrix products, arithmetic and copies ran while one was open for 0% of the time, Pallas kernels for 0%

profile of v5, /device:TPU:48, one launch (start us, length us, event | category | flops | bytes accessed | tf_op | source)
XLA Modules:
  0.0 66.5 jit_solution(2058973748148133576)
XLA Ops:
  0.6 3.8 %facet_to_slots.1 = bf16[32,32,256]{2,1,0:T(8,128)(2,1)} custom-call(s32[32]{0:T(128)} %offs_ref.7, s32[32]{0:T(128)} %order_ref.7, bf16[32,2048]{1,0:T(8,128)(2,1)} %sky_hbm.1), custom_call_target="tpu_custom_call" | custom-call | tf_op jit(solution)/shard_map/facet_to_slots/pallas_call | solution.py:206
  4.4 0.0 copy-start
  4.4 0.0 copy-start.1
  4.4 0.0 copy-start.2
  4.4 0.0 copy-start.4
  4.5 28.9 %all_to_all.10.arr_ref = bf16[32,32,256]{2,1,0:T(8,128)(2,1)S(1)} all-to-all(bf16[32,32,256]{2,1,0:T(8,128)(2,1)} %facet_to_slots.1), channel_id=1, replica_groups=mesh['facet'=32,'uv'=8] {'facet'}, dimensions={0} | all-to-all | bytes 1048576 | tf_op jit(solution)/shard_map/all_to_all | solution.py:468
  33.4 0.0 copy-done
  33.4 0.0 copy-done.1
  33.4 0.6 copy-done.7
  34.1 0.0 copy-done.8
  34.1 1.0 %sum_facets.1 = (f32[32,512]{1,0:T(8,128)S(1)}, bf16[8,2048]{1,0:T(8,128)(2,1)S(1)}, bf16[8,2048]{1,0:T(8,128)(2,1)S(1)}) custom-call(s32[32]{0:T(128)S(1)} %copy-done.7, s32[32]{0:T(128)S(1)} %copy-done.8, bf16[32,32,256]{2,1,0:T(8,128)(2,1)S(1)} %all_to_all.10.arr_ref, bf16[2,32,512]{2,1,0:T(8,128)(2,1)S(1)} %bitcast.3, f32[32,512]{1,0:T(8,128)S(1)} %bitcast.5, ...), custom_call_target="tpu_custom_call" | custom-call | tf_op jit(solution)/shard_map/sum_facets/pallas_call | solution.py:272
  35.1 0.1 collective-permute-start
  35.2 0.0 copy-start.9
  35.2 0.5 collective-permute-start.1
  36.4 0.0 copy-start.10
  36.4 0.0 copy-start.11
  36.4 0.0 collective-permute-done.sibling_ref
  36.4 2.2 %collective-permute-done.1.neighbour_ref = bf16[8,2048]{1,0:T(8,128)(2,1)S(1)} collective-permute-done((bf16[8,2048]{1,0:T(8,128)(2,1)S(1)}, bf16[8,2048]{1,0:T(8,128)(2,1)S(1)}, u32[]{:S(2)}, u32[]{:S(2)}) %collective-permute-start.1) | collective-permute-done | bytes 32800 | tf_op jit(solution)/shard_map/ppermute | solution.py:457
  38.6 0.0 copy-done.11
  38.6 2.6 %slot_round_trip.1 = (f32[2,32,512]{2,1,0:T(8,128)}, bf16[32,32,256]{2,1,0:T(8,128)(2,1)S(1)}) custom-call(s32[32]{0:T(128)S(1)} %copy-done.7, s32[32]{0:T(128)S(1)} %copy-done.8, s32[1]{0:T(128)S(6)} %copy.17.count_ref, f32[7]{0:T(128)S(1)} %copy-done.10, f32[7]{0:T(128)S(1)} %copy-done.11, f32[32,512]{1,0:T(8,128)S(1)} %get-tuple-element.7.sub_ref, ...), custom_call_target="tpu_custom_call" | custom-call | tf_op jit(solution)/shard_map/slot_round_trip/pallas_call | solution.py:371
  41.3 0.0 copy-start.5
  41.3 0.0 copy-start.6
  41.3 23.0 %all_to_all.11.bp_ref = bf16[32,32,256]{2,1,0:T(8,128)(2,1)S(1)} all-to-all(bf16[32,32,256]{2,1,0:T(8,128)(2,1)S(1)} %get-tuple-element.11), channel_id=1, replica_groups=mesh['facet'=32,'uv'=8] {'facet'}, dimensions={0} | all-to-all | bytes 1048576 | tf_op jit(solution)/shard_map/all_to_all | solution.py:475
  64.3 2.2 %slots_to_facet.1 = f32[32,2048]{1,0:T(8,128)} custom-call(s32[32]{0:T(128)S(1)} %copy-done.7, s32[32]{0:T(128)S(1)} %copy-done.8, bf16[32,32,256]{2,1,0:T(8,128)(2,1)S(1)} %all_to_all.11.bp_ref, f32[1,2048]{1,0:T(1,128)S(1)} %copy-done.6, bf16[256,256]{1,0:T(8,128)(2,1)S(1)} %copy-done.5), custom_call_target="tpu_custom_call" | custom-call | tf_op jit(solution)/shard_map/slots_to_facet/pallas_call | solution.py:437
  (10 shorter events, 0.0 us)
Async XLA Ops:
  4.4 29.0 %copy-start = (bf16[256,512]{1,0:T(8,128)(2,1)S(1)}, bf16[256,512]{1,0:T(8,128)(2,1)}, u32[]{:S(2)}) copy-start(bf16[256,512]{1,0:T(8,128)(2,1)} %constant.10.clone.w_ref) | copy-start | bytes 786436
  4.4 29.0 %copy-start.1 = (bf16[1,2,32,512]{3,2,1,0:T(8,128)(2,1)S(1)}, bf16[1,2,32,512]{3,2,1,0:T(8,128)(2,1)}, u32[]{:S(2)}) copy-start(bf16[1,2,32,512]{3,2,1,0:T(8,128)(2,1)} %param.20) | copy-start | bytes 196612
  4.4 29.0 %copy-start.2 = (f32[1,32,512]{2,1,0:T(8,128)S(1)}, f32[1,32,512]{2,1,0:T(8,128)}, u32[]{:S(2)}) copy-start(f32[1,32,512]{2,1,0:T(8,128)} %param.21) | copy-start | bytes 196612
  4.4 29.0 %copy-start.4 = (f32[2,32,128]{2,1,0:T(8,128)S(1)}, f32[2,32,128]{2,1,0:T(8,128)}, u32[]{:S(2)}) copy-start(f32[2,32,128]{2,1,0:T(8,128)} %constant.11.clone.ph_ref) | copy-start | bytes 98308
  33.4 0.7 copy-start.7
  33.4 0.7 %copy-start.8 = (s32[32]{0:T(128)S(1)}, s32[32]{0:T(128)}, u32[]{:S(2)}) copy-start(s32[32]{0:T(128)} %order_ref.7) | copy-start | bytes 388
  34.1 4.5 %copy-start.3 = (bf16[512,256]{1,0:T(8,128)(2,1)S(1)}, bf16[512,256]{1,0:T(8,128)(2,1)}, u32[]{:S(2)}) copy-start(bf16[512,256]{1,0:T(8,128)(2,1)} %constant.12.clone.wt_tab_ref) | copy-start | bytes 786436
  35.1 1.3 %collective-permute-start = (bf16[8,2048]{1,0:T(8,128)(2,1)S(1)}, bf16[8,2048]{1,0:T(8,128)(2,1)S(1)}, u32[]{:S(2)}, u32[]{:S(2)}) collective-permute-start(bf16[8,2048]{1,0:T(8,128)(2,1)S(1)} %get-tuple-element.8), channel_id=1, source_target_pairs={{0,1},{1,0},{2,3},{3,2},{4,5},{5,4},{6,7},{7,6},{8,9},{9,8},{10,11... | collective-permute-start | bytes 98312 | tf_op jit(solution)/shard_map/ppermute | solution.py:457
  35.2 3.4 %copy-start.9 = (s32[1,512]{1,0:T(1,128)S(1)}, s32[1,512]{1,0:T(1,128)}, u32[]{:S(2)}) copy-start(s32[1,512]{1,0:T(1,128)} %cell_ref.1) | copy-start | bytes 6148
  35.2 3.4 %collective-permute-start.1 = (bf16[8,2048]{1,0:T(8,128)(2,1)S(1)}, bf16[8,2048]{1,0:T(8,128)(2,1)S(1)}, u32[]{:S(2)}, u32[]{:S(2)}) collective-permute-start(bf16[8,2048]{1,0:T(8,128)(2,1)S(1)} %get-tuple-element.9), channel_id=1, source_target_pairs={{0,7},{1,2},{2,1},{3,4},{4,3},{5,6},{6,5},{7,0},{8,15},{9,10},{10,... | collective-permute-start | bytes 98312 | tf_op jit(solution)/shard_map/ppermute | solution.py:457
  36.4 2.2 %copy-start.10 = (f32[7]{0:T(128)S(1)}, f32[7]{0:T(128)}, u32[]{:S(2)}) copy-start(f32[7]{0:T(128)} %rk_ref.1) | copy-start | bytes 88
  36.4 2.2 %copy-start.11 = (f32[7]{0:T(128)S(1)}, f32[7]{0:T(128)}, u32[]{:S(2)}) copy-start(f32[7]{0:T(128)} %ck_ref.1) | copy-start | bytes 88
  41.3 23.0 %copy-start.5 = (bf16[256,256]{1,0:T(8,128)(2,1)S(1)}, bf16[256,256]{1,0:T(8,128)(2,1)}, u32[]{:S(2)}) copy-start(bf16[256,256]{1,0:T(8,128)(2,1)} %constant.13.clone.tab_ref) | copy-start | bytes 393220
  41.3 23.0 %copy-start.6 = (f32[1,2048]{1,0:T(1,128)S(1)}, f32[1,2048]{1,0:T(1,128)}, u32[]{:S(2)}) copy-start(f32[1,2048]{1,0:T(1,128)} %constant.14.clone.win_ref) | copy-start | bytes 24580

commit v6 on v5

--- a/solution.py
+++ b/solution.py
@@ -132,9 +132,14 @@
     return [v for pair in zip(even, odd) for v in pair]
 
 
-def swap_index(x, lane):
+def lanes_of(shape):
+    return lax.broadcasted_iota(jnp.int32, shape, 1).astype(F32).astype(BF)
+
+
+def swap_index(x):
+    lane = lax.broadcasted_iota(jnp.int32, x[0].shape, 1)
     for bit in (1, 2, 4, 8):
-        high = (lane & bit) != 0
+        high = (lane & bit).astype(F32).astype(BF) > 0
         y = list(x)
         for i in range(16):
             if i & bit:
@@ -151,16 +156,27 @@
 
 
 def k1_body(
-    offs_ref, order_ref, sky_hbm,
-    out_ref, tw_ref, lhs_ref, u_ref, nat_ref, sky_ref, win_ref, tab_ref, sem,
+    offs_hbm, order_hbm, sky_hbm,
+    out_hbm, offs_ref, order_ref, tw_ref, lhs_ref, u_ref, nat_ref, sky_ref, win_ref, tab_ref,
+    out_ref, sky_sem, small_sem, out_sem,
 ):
-    copy = pltpu.make_async_copy(sky_hbm, sky_ref, sem)
-    copy.start()
+    halves = [
+        pltpu.make_async_copy(
+            sky_hbm.at[pl.ds(16 * g, 16), :], sky_ref.at[pl.ds(16 * g, 16), :], sky_sem.at[g]
+        )
+        for g in range(2)
+    ]
+    small = [
+        pltpu.make_async_copy(offs_hbm, offs_ref, small_sem.at[0]),
+        pltpu.make_async_copy(order_hbm, order_ref, small_sem.at[1]),
+    ]
+    for copy in halves + small:
+        copy.start()
     tw_ref[0], tw_ref[1] = twiddles(lax.axis_index("facet"))
     make_window(win_ref)
     make_block_table(tab_ref)
-    copy.wait()
     for g in range(2):
+        halves[g].wait()
         rows = slice(16 * g, 16 * (g + 1))
         x = []
         for b in range(16):
@@ -173,32 +189,42 @@
             lhs_ref[m, rows, 0:128] = (ar * c + ai * s).astype(BF)
             lhs_ref[m, rows, 128:256] = (ai * c - ar * s).astype(BF)
     u = jnp.dot(lhs_ref[...].reshape(16 * CB, 256), tab_ref[...], preferred_element_type=F32)
-    u_ref[...] = u.reshape(16, CB, 256)
-
-    lane = lax.broadcasted_iota(jnp.int32, (8, 128), 1)
-    for g in range(4):
-        rows = slice(8 * g, 8 * (g + 1))
+    u_ref[...] = u.astype(BF).reshape(16, CB, 256)
+
+    for g in range(2):
+        rows = slice(16 * g, 16 * (g + 1))
         for p in range(2):
             cols = slice(128 * p, 128 * (p + 1))
-            x = swap_index([u_ref[m, rows, cols] for m in range(16)], lane)
+            x = swap_index([u_ref[m, rows, cols] for m in range(16)])
             for b in range(16):
                 nat_ref[b, rows, cols] = x[b]
             nat_ref[16, rows, cols] = x[0]
 
-    lane = lax.broadcasted_iota(jnp.int32, (CB, 128), 1)
+    for copy in small:
+        copy.wait()
+    lane = lanes_of((CB, 128))
+    done = []
     for i in range(NF):
         off = offs_ref[order_ref[i]]
         b, s = off >> 7, off & 127
         back = (128 - s) & 127
-        keep = lane >= s
+        keep = lane >= s.astype(F32).astype(BF)
         for p in range(2):
             cols = slice(128 * p, 128 * (p + 1))
             x = jnp.where(keep, nat_ref[b, :, cols], nat_ref[b + 1, :, cols])
-            out_ref[i, :, cols] = pltpu.roll(x, back, 1).astype(BF)
+            out_ref[i, :, cols] = pltpu.roll(x, back, 1)
+        if i % 8 == 7:
+            part = pl.ds(i - 7, 8)
+            copy = pltpu.make_async_copy(out_ref.at[part], out_hbm.at[part], out_sem.at[i // 8])
+            copy.start()
+            done.append(copy)
+    for copy in done:
+        copy.wait()
 
 
 SMEM = pl.BlockSpec(memory_space=pltpu.SMEM)
 VMEM = pl.BlockSpec(memory_space=pltpu.VMEM)
+ANY = pl.BlockSpec(memory_space=pl.ANY)
 PARAMS = pltpu.CompilerParams(vmem_limit_bytes=24 * 1024 * 1024)
 
 
@@ -206,34 +232,63 @@
     return pl.pallas_call(
         k1_body,
         out_shape=jax.ShapeDtypeStruct((NF, CB, 2 * XC), BF),
-        in_specs=[SMEM] * 2 + [pl.BlockSpec(memory_space=pl.ANY)],
-        out_specs=VMEM,
+        in_specs=[ANY] * 3,
+        out_specs=ANY,
         scratch_shapes=[
+            pltpu.SMEM((NF,), jnp.int32),
+            pltpu.SMEM((NF,), jnp.int32),
             pltpu.VMEM((2, 16, 128), F32),
             pltpu.VMEM((16, CB, 256), BF),
-            pltpu.VMEM((16, CB, 256), F32),
-            pltpu.VMEM((17, CB, 256), F32),
+            pltpu.VMEM((16, CB, 256), BF),
+            pltpu.VMEM((17, CB, 256), BF),
             pltpu.VMEM((CB, FR), BF),
             pltpu.VMEM((8, FR), F32),
             pltpu.VMEM((256, 256), BF),
-            pltpu.SemaphoreType.DMA,
+            pltpu.VMEM((NF, CB, 256), BF),
+            pltpu.SemaphoreType.DMA((2,)),
+            pltpu.SemaphoreType.DMA((2,)),
+            pltpu.SemaphoreType.DMA((4,)),
         ],
         name="facet_to_slots",
     )(offs, order, sky)
 
 
-def slot_phases(offs_ref, order_ref, ph_ref, pho_ref):
+def kt_body(
+    offs_ref, order_ref, rk_ref, ck_ref, count_ref, cell_ref, ph_ref,
+    dt_ref, pho_ref, live_ref,
+):
     off = offs_ref[order_ref[lax.axis_index("facet")]]
     back = (128 - 2 * off) & 127
     pho_ref[0] = pltpu.roll(ph_ref[0], back, 1)
     pho_ref[1] = pltpu.roll(ph_ref[1], back, 1)
+    d = lax.broadcasted_iota(jnp.int32, (SG, VM), 0) - cell_ref[...] + 3
+    m = jnp.zeros((SG, VM), F32)
+    for t in range(TAPS):
+        m = jnp.where(d == t, rk_ref[t], m)
+    dt_ref[...] = m.astype(BF)
+    live_ref[...] = (lax.broadcasted_iota(jnp.int32, (1, VM), 1) < count_ref[0]).astype(F32)
+
+
+def kt(offs, order, rk, ck, count, cell):
+    return pl.pallas_call(
+        kt_body,
+        out_shape=(
+            jax.ShapeDtypeStruct((SG, VM), BF),
+            jax.ShapeDtypeStruct((2, NF, 128), F32),
+            jax.ShapeDtypeStruct((1, VM), F32),
+        ),
+        in_specs=[SMEM] * 5 + [VMEM] * 2,
+        out_specs=(VMEM, VMEM, VMEM),
+        compiler_params=PARAMS,
+        cost_estimate=pl.CostEstimate(flops=2000000, bytes_accessed=400000, transcendentals=0),
+        name="slot_tables",
+    )(offs, order, rk, ck, count, cell, facet_phase())
 
 
 def ka_body(
-    offs_ref, order_ref, arr_ref, obs_ref, wt_ref, w_ref, ph_ref,
-    sub_ref, sibling_ref, neighbour_ref, u_ref, pho_ref,
+    arr_ref, obs_ref, wt_ref, w_ref, pho_ref,
+    sub_ref, sibling_ref, neighbour_ref, u_ref,
 ):
-    slot_phases(offs_ref, order_ref, ph_ref, pho_ref)
     u = jnp.dot(arr_ref[...].reshape(NF * CB, 256), w_ref[...], preferred_element_type=F32)
     u_ref[...] = u.reshape(NF, CB, 2 * SG)
     for h in range(2):
@@ -268,7 +323,7 @@
 EDGE = 2 * SG + 3 * VM
 
 
-def ka(offs, order, arrived, obs, wt):
+def ka(arrived, obs, wt, phases):
     return pl.pallas_call(
         ka_body,
         out_shape=(
@@ -276,30 +331,19 @@
             jax.ShapeDtypeStruct((8, EDGE), BF),
             jax.ShapeDtypeStruct((8, EDGE), BF),
         ),
-        in_specs=[SMEM] * 2 + [VMEM] * 5,
+        in_specs=[VMEM] * 5,
         out_specs=(VMEM, VMEM, VMEM),
-        scratch_shapes=[
-            pltpu.VMEM((NF, CB, 2 * SG), F32),
-            pltpu.VMEM((2, NF, 128), F32),
-        ],
+        scratch_shapes=[pltpu.VMEM((NF, CB, 2 * SG), F32)],
         compiler_params=PARAMS,
         name="sum_facets",
-    )(offs, order, arrived, obs, wt, jnp.asarray(subgrid_table(), BF), facet_phase())
+    )(arrived, obs, wt, jnp.asarray(subgrid_table(), BF), phases)
 
 
 def kb_body(
-    offs_ref, order_ref, count_ref, rk_ref, ck_ref, sub_ref, cell_ref, obs_ref, wt_ref,
-    sibling_ref, neighbour_ref, wt_tab_ref, ph_ref,
-    res_ref, out_ref, dt_ref, sub_ext_ref, ext_ref, y_ref, pho_ref,
+    ck_ref, sub_ref, obs_ref, wt_ref, sibling_ref, neighbour_ref, wt_tab_ref, dt_ref, pho_ref,
+    live_ref,
+    res_hbm, out_ref, sub_ext_ref, conv_ref, res_ref, ext_ref, back_ref, y_ref, sem,
 ):
-    slot_phases(offs_ref, order_ref, ph_ref, pho_ref)
-    cell = cell_ref[...]
-    d = lax.broadcasted_iota(jnp.int32, (SG, VM), 0) - cell + 3
-    m = jnp.zeros((SG, VM), F32)
-    for t in range(TAPS):
-        m = jnp.where(d == t, rk_ref[t], m)
-    dt_ref[...] = m.astype(BF)
-
     uv = lax.axis_index("uv")
     even = lax.rem(uv, 2) == 0
     in_before, in_after = uv > 0, uv < 7
@@ -314,7 +358,6 @@
     sub_ext_ref[8:16, :] = before
     sub_ext_ref[16:48, :] = sub_ref[...]
     sub_ext_ref[48:56, :] = after
-    parts = []
     for p in range(2):
         lanes = slice(SG * p, SG * (p + 1))
         own = jnp.zeros((CB, SG), F32)
@@ -325,11 +368,11 @@
             own = own + k * sub_ext_ref[13 + t : 45 + t, lanes]
             lo = lo + k * sub_ext_ref[5 + t : 13 + t, lanes]
             hi = hi + k * sub_ext_ref[45 + t : 53 + t, lanes]
-        parts += [own, halo_rows(hi, lo, 0)]
-    grid = jnp.concatenate(parts, axis=0).astype(BF)
-    model = jnp.dot(grid, dt_ref[...], preferred_element_type=F32)
-
-    live = (lax.broadcasted_iota(jnp.int32, (1, VM), 1) < count_ref[0]).astype(F32)
+        conv_ref[p * CE : p * CE + CB, :] = own
+        conv_ref[p * CE + CB : (p + 1) * CE, :] = halo_rows(hi, lo, 0)
+    model = jnp.dot(conv_ref[...].astype(BF), dt_ref[...], preferred_element_type=F32)
+
+    live = live_ref[...]
     wt = wt_ref[...] * live
     before, after = sides(slice(2 * SG + 2 * VM, EDGE))
     wt_h = halo_rows(after, before, 0) * live
@@ -340,11 +383,12 @@
         before, after = sides(slice(2 * SG + p * VM, 2 * SG + (p + 1) * VM))
         obs_h = halo_rows(after, before, 0)
         parts += [own, wt_h * (obs_h - model[p * CE + CB : (p + 1) * CE])]
+    copy = pltpu.make_async_copy(res_ref, res_hbm, sem)
+    copy.start()
     rr = jnp.concatenate(parts, axis=0).astype(BF)
     gridded = lax.dot_general(
         rr, dt_ref[...], (((1,), (1,)), ((), ())), preferred_element_type=F32
     )
-    backs = []
     for p in range(2):
         halo = gridded[p * CE + CB : (p + 1) * CE]
         ext_ref[p, 0:8, :] = halo
@@ -353,11 +397,10 @@
         b = jnp.zeros((CB, SG), F32)
         for t in range(TAPS):
             b = b + ck_ref[t] * ext_ref[p, 11 - t : 43 - t, :]
-        backs.append(b)
-    br, bi = backs
+        back_ref[p] = b
     for h in range(2):
         lanes = slice(128 * h, 128 * (h + 1))
-        xr, xi = br[:, lanes], bi[:, lanes]
+        xr, xi = back_ref[0, :, lanes], back_ref[1, :, lanes]
         for f in range(NF):
             pc = pho_ref[0, f : f + 1, :]
             ps = pho_ref[1, f : f + 1, :]
@@ -365,35 +408,38 @@
             y_ref[f, :, SG + 128 * h : SG + 128 * (h + 1)] = (xi * pc - xr * ps).astype(BF)
     z = jnp.dot(y_ref[...].reshape(NF * CB, 2 * SG), wt_tab_ref[...], preferred_element_type=F32)
     out_ref[...] = z.astype(BF).reshape(NF, CB, 2 * XC)
-
-
-def kb(offs, order, count, rk, ck, sub, cell, obs, wt, sibling, neighbour):
+    copy.wait()
+
+
+def kb(ck, sub, obs, wt, sibling, neighbour, table, phases, live):
     return pl.pallas_call(
         kb_body,
         out_shape=(
             jax.ShapeDtypeStruct((2, CB, VM), F32),
             jax.ShapeDtypeStruct((NF, CB, 2 * XC), BF),
         ),
-        in_specs=[SMEM] * 5 + [VMEM] * 8,
-        out_specs=(VMEM, VMEM),
+        in_specs=[SMEM] + [VMEM] * 9,
+        out_specs=(ANY, VMEM),
         scratch_shapes=[
-            pltpu.VMEM((SG, VM), BF),
             pltpu.VMEM((64, 2 * SG), F32),
+            pltpu.VMEM((2 * CE, SG), F32),
+            pltpu.VMEM((2, CB, VM), F32),
             pltpu.VMEM((2, 48, SG), F32),
+            pltpu.VMEM((2, CB, SG), F32),
             pltpu.VMEM((NF, CB, 2 * SG), BF),
-            pltpu.VMEM((2, NF, 128), F32),
+            pltpu.SemaphoreType.DMA,
         ],
         compiler_params=PARAMS,
         name="slot_round_trip",
     )(
-        offs, order, count, rk, ck, sub, cell, obs, wt, sibling, neighbour,
-        jnp.asarray(subgrid_table().T, BF), facet_phase(),
+        ck, sub, obs, wt, sibling, neighbour, jnp.asarray(subgrid_table().T, BF), table, phases,
+        live,
     )
 
 
 def k3_body(
     offs_ref, order_ref, bp_ref, win_ref, tab_ref,
-    out_ref, nat_ref, tw_ref, lhs_ref, v_ref,
+    out_hbm, nat_ref, tw_ref, lhs_ref, v_ref, out_ref, sem,
 ):
     tw_ref[0], tw_ref[1] = twiddles(lax.axis_index("facet"))
     nat_ref[...] = jnp.zeros_like(nat_ref)
@@ -404,21 +450,21 @@
         keep = lane >= s
         for p in range(2):
             cols = slice(128 * p, 128 * (p + 1))
-            x = pltpu.roll(bp_ref[i, :, cols].astype(F32), s, 1)
+            x = pltpu.roll(bp_ref[i, :, cols], s, 1).astype(F32)
             nat_ref[b, :, cols] += jnp.where(keep, x, 0.0)
             nat_ref[b + 1, :, cols] += jnp.where(keep, 0.0, x)
     nat_ref[0] += nat_ref[16]
 
-    lane = lax.broadcasted_iota(jnp.int32, (16, 128), 1)
     for g in range(2):
         rows = slice(16 * g, 16 * (g + 1))
         for p in range(2):
             cols = slice(128 * p, 128 * (p + 1))
-            x = swap_index([nat_ref[b, rows, cols] for b in range(16)], lane)
+            x = swap_index([nat_ref[b, rows, cols].astype(BF) for b in range(16)])
             for m in range(16):
-                lhs_ref[m, rows, cols] = x[m].astype(BF)
+                lhs_ref[m, rows, cols] = x[m]
     v = jnp.dot(lhs_ref[...].reshape(16 * CB, 256), tab_ref[...], preferred_element_type=F32)
     v_ref[...] = v.reshape(16, CB, 256)
+    done = []
     for g in range(4):
         rows = slice(8 * g, 8 * (g + 1))
         t = []
@@ -431,6 +477,12 @@
         for b in range(16):
             lanes = slice(128 * b, 128 * (b + 1))
             out_ref[rows, lanes] = x[b] * (0.5 * win_ref[:, lanes])
+        part = pl.ds(8 * g, 8)
+        copy = pltpu.make_async_copy(out_ref.at[part, :], out_hbm.at[part, :], sem.at[g])
+        copy.start()
+        done.append(copy)
+    for copy in done:
+        copy.wait()
 
 
 def k3(offs, order, bp):
@@ -438,12 +490,14 @@
         k3_body,
         out_shape=jax.ShapeDtypeStruct((CB, FR), F32),
         in_specs=[SMEM, SMEM, VMEM, VMEM, VMEM],
-        out_specs=VMEM,
+        out_specs=ANY,
         scratch_shapes=[
             pltpu.VMEM((17, CB, 256), F32),
             pltpu.VMEM((2, 16, 128), F32),
             pltpu.VMEM((16, CB, 256), BF),
             pltpu.VMEM((16, CB, 256), F32),
+            pltpu.VMEM((CB, FR), F32),
+            pltpu.SemaphoreType.DMA((4,)),
         ],
         compiler_params=PARAMS,
         name="slots_to_facet",
@@ -466,11 +520,13 @@
 
     out = k1(subgrid_offsets, owner_order, sky_image)
     arrived = lax.all_to_all(out, "facet", split_axis=0, concat_axis=0, tiled=True)
-    sub, sibling, neighbour = ka(subgrid_offsets, owner_order, arrived, obs, wt)
+    table, phases, live = kt(
+        subgrid_offsets, owner_order, row_kernel, column_kernel, visibility_count, visibility_cell
+    )
+    sub, sibling, neighbour = ka(arrived, obs, wt, phases)
     sibling, neighbour = swapped(sibling, neighbour)
     res, outgoing = kb(
-        subgrid_offsets, owner_order, visibility_count, row_kernel, column_kernel,
-        sub, visibility_cell, obs, wt, sibling, neighbour,
+        column_kernel, sub, obs, wt, sibling, neighbour, table, phases, live
     )
     back = lax.all_to_all(outgoing, "facet", split_axis=0, concat_axis=0, tiled=True)
     dirty = k3(subgrid_offsets, owner_order, back)

time: 67.4 us -> 64 us (0.950)
  blocking collectives: 51.9 us -> 23 us
  waiting for transfers between devices: 2.2 us -> 18.4 us
  starting transfers between devices: 0.64 us -> 12 us
  Pallas kernels: 9.57 us -> 8.21 us
    all_to_all x1 -> x0, blocking collectives: 28.9 us -> none  [local(): lax.all_to_all(out, 'facet', split_axis=0, concat_axis=0, tiled=True)]
    all_to_all x0 -> x1, waiting for transfers between devices: none -> 15.5 us  [local(): lax.all_to_all(out, 'facet', split_axis=0, concat_axis=0, tiled=True)]
    all_to_all x0 -> x1, starting transfers between devices: none -> 11.3 us  [local(): lax.all_to_all(out, 'facet', split_axis=0, concat_axis=0, tiled=True)]
    pallas_call x0 -> x1, Pallas kernels: none -> 1.37 us  [kt(): pl.pallas_call(kt_body, out_shape=(jax.ShapeDtypeStruct((SG, VM), BF), ja...]
    pallas_call x1, Pallas kernels: 3.76 us -> 2.5 us  [k1(): pl.pallas_call(k1_body, out_shape=jax.ShapeDtypeStruct((NF, CB, 2 * XC),...]
    pallas_call x1, Pallas kernels: 2.64 us -> 1.76 us  [kb(): pl.pallas_call(kb_body, out_shape=(jax.ShapeDtypeStruct((2, CB, VM), F32)...]
  transfers between devices with their start and end apart: 2 -> 3, of which waited for: 1 -> 3; matrix products, arithmetic and copies ran while one was open for 0% -> 0% of each run, Pallas kernels for 0% -> 2%
where the time goes in v6:
time: 64 us; the launch traced here: 63.1 us
  blocking collectives  23 us (36%)
  waiting for transfers between devices  18.4 us (29%)
  starting transfers between devices  12 us (19%)
  Pallas kernels  8.21 us (13%)
  between operations  1.49 us (2%)
    all_to_all x1, blocking collectives, local(): lax.all_to_all(outgoing, 'facet', split_axis=0, concat_axis=0, tiled=True)  23 us
    all_to_all x1, waiting for transfers between devices, local(): lax.all_to_all(out, 'facet', split_axis=0, concat_axis=0, tiled=True)  15.5 us
    all_to_all x1, starting transfers between devices, local(): lax.all_to_all(out, 'facet', split_axis=0, concat_axis=0, tiled=True)  11.3 us
    pallas_call x1, Pallas kernels, k1(): pl.pallas_call(k1_body, out_shape=jax.ShapeDtypeStruct((NF, CB, 2 * XC),...  2.5 us
    ppermute x1, waiting for transfers between devices, swapped(): lax.ppermute(neighbour, 'uv', far)  2.23 us
    pallas_call x1, Pallas kernels, k3(): pl.pallas_call(k3_body, out_shape=jax.ShapeDtypeStruct((CB, FR), F32), in...  2.14 us
    pallas_call x1, Pallas kernels, kb(): pl.pallas_call(kb_body, out_shape=(jax.ShapeDtypeStruct((2, CB, VM), F32)...  1.76 us
    pallas_call x1, Pallas kernels, kt(): pl.pallas_call(kt_body, out_shape=(jax.ShapeDtypeStruct((SG, VM), BF), ja...  1.37 us
  transfers between devices with their start and end apart: 3, of which 3 were waited for; matrix products, arithmetic and copies ran while one was open for 0% of the time, Pallas kernels for 2%

profile of v6, /device:TPU:48, one launch (start us, length us, event | category | flops | bytes accessed | tf_op | source)
XLA Modules:
  0.0 63.1 jit_solution(15031050367215259514)
XLA Ops:
  0.6 2.5 %facet_to_slots.1 = bf16[32,32,256]{2,1,0:T(8,128)(2,1)} custom-call(s32[32]{0:T(128)} %offs_ref.3, s32[32]{0:T(128)} %order_ref.3, bf16[32,2048]{1,0:T(8,128)(2,1)} %sky_hbm.1), custom_call_target="tpu_custom_call" | custom-call | tf_op jit(solution)/shard_map/facet_to_slots/pallas_call | solution.py:232
  3.1 0.0 copy-start.5
  3.1 0.0 copy-start.9
  3.2 0.0 copy-start.11
  3.2 0.0 copy-start.1
  3.2 0.0 copy-start.2
  3.2 0.0 copy-start.3
  3.2 11.3 %all-to-all-start = ((bf16[32,32,256]{2,1,0:T(8,128)(2,1)}), bf16[32,32,256]{2,1,0:T(8,128)(2,1)S(1)}, u32[]{:S(2)}, u32[]{:S(2)}) async-start(bf16[32,32,256]{2,1,0:T(8,128)(2,1)} %facet_to_slots.1), calls=%async_computation | async-start | bytes 1048576 | tf_op jit(solution)/shard_map/all_to_all | solution.py:522
  14.6 0.0 copy-start.7
  14.6 0.0 copy-start.8
  14.6 0.0 copy-start.10
  15.3 1.4 %slot_tables.1 = (bf16[256,512]{1,0:T(8,128)(2,1)S(1)}, f32[2,32,128]{2,1,0:T(8,128)S(1)}, f32[1,512]{1,0:T(1,128)S(1)}) custom-call(s32[32]{0:T(128)S(1)} %copy-done.7, s32[32]{0:T(128)S(1)} %copy-done.8, f32[7]{0:T(128)S(1)} %copy-done.11, f32[7]{0:T(128)S(1)} %copy-done.10, s32[1]{0:T(128)S(6)} %copy.16.count_ref, s32[1,512]{1,0:T(1,128)S(1)} %copy-done.9, ...), custom_call_target="tpu_custom_call" | custom-call | flops 2000000 | bytes 400000 | tf_op jit(solution)/shard_map/slot_tables/pallas_call | solution.py:273
  16.7 15.5 %all-to-all-done.arr_ref = bf16[32,32,256]{2,1,0:T(8,128)(2,1)S(1)} async-done(((bf16[32,32,256]{2,1,0:T(8,128)(2,1)}), bf16[32,32,256]{2,1,0:T(8,128)(2,1)S(1)}, u32[]{:S(2)}, u32[]{:S(2)}) %all-to-all-start) | async-done | bytes 524320 | tf_op jit(solution)/shard_map/all_to_all | solution.py:522
  32.2 0.0 copy-start
  32.2 0.4 sum_facets.1
  32.6 0.1 collective-permute-start
  32.7 0.6 collective-permute-start.1
  33.3 0.6 %collective-permute-done.sibling_ref = bf16[8,2048]{1,0:T(8,128)(2,1)S(1)} collective-permute-done((bf16[8,2048]{1,0:T(8,128)(2,1)S(1)}, bf16[8,2048]{1,0:T(8,128)(2,1)S(1)}, u32[]{:S(2)}, u32[]{:S(2)}) %collective-permute-start) | collective-permute-done | bytes 32800 | tf_op jit(solution)/shard_map/ppermute | solution.py:511
  33.9 2.2 %collective-permute-done.1.neighbour_ref = bf16[8,2048]{1,0:T(8,128)(2,1)S(1)} collective-permute-done((bf16[8,2048]{1,0:T(8,128)(2,1)S(1)}, bf16[8,2048]{1,0:T(8,128)(2,1)S(1)}, u32[]{:S(2)}, u32[]{:S(2)}) %collective-permute-start.1) | collective-permute-done | bytes 32800 | tf_op jit(solution)/shard_map/ppermute | solution.py:511
  36.2 1.8 %slot_round_trip.1 = (f32[2,32,512]{2,1,0:T(8,128)}, bf16[32,32,256]{2,1,0:T(8,128)(2,1)S(1)}) custom-call(f32[7]{0:T(128)S(1)} %copy-done.10, f32[32,512]{1,0:T(8,128)S(1)} %get-tuple-element.11.sub_ref, bf16[2,32,512]{2,1,0:T(8,128)(2,1)S(1)} %bitcast.4, f32[32,512]{1,0:T(8,128)S(1)} %bitcast.6, bf16[8,2048]{1,0:T(8,128)(2,1)S(1)} %collective-permute-done.sibling_ref, ...), custom_call_target="tpu_custom_call" | custom-call | tf_op jit(solution)/shard_map/slot_round_trip/pallas_call | solution.py:415
  37.9 0.0 copy-start.4
  37.9 0.0 copy-start.6
  38.0 23.0 %all_to_all.10.bp_ref = bf16[32,32,256]{2,1,0:T(8,128)(2,1)S(1)} all-to-all(bf16[32,32,256]{2,1,0:T(8,128)(2,1)S(1)} %get-tuple-element.17), channel_id=1, replica_groups=mesh['facet'=32,'uv'=8] {'facet'}, dimensions={0} | all-to-all | bytes 1048576 | tf_op jit(solution)/shard_map/all_to_all | solution.py:531
  61.0 2.1 %slots_to_facet.1 = f32[32,2048]{1,0:T(8,128)} custom-call(s32[32]{0:T(128)S(1)} %copy-done.7, s32[32]{0:T(128)S(1)} %copy-done.8, bf16[32,32,256]{2,1,0:T(8,128)(2,1)S(1)} %all_to_all.10.bp_ref, f32[1,2048]{1,0:T(1,128)S(1)} %copy-done.6, bf16[256,256]{1,0:T(8,128)(2,1)S(1)} %copy-done.4), custom_call_target="tpu_custom_call" | custom-call | tf_op jit(solution)/shard_map/slots_to_facet/pallas_call | solution.py:489
  (12 shorter events, 0.0 us)
Async XLA Ops:
  3.1 12.1 %copy-start.5 = (f32[2,32,128]{2,1,0:T(8,128)S(1)}, f32[2,32,128]{2,1,0:T(8,128)}, u32[]{:S(2)}) copy-start(f32[2,32,128]{2,1,0:T(8,128)} %constant.10.clone.ph_ref) | copy-start | bytes 98308
  3.1 12.1 %copy-start.9 = (s32[1,512]{1,0:T(1,128)S(1)}, s32[1,512]{1,0:T(1,128)}, u32[]{:S(2)}) copy-start(s32[1,512]{1,0:T(1,128)} %cell_ref.1) | copy-start | bytes 6148
  3.2 12.1 %copy-start.11 = (f32[7]{0:T(128)S(1)}, f32[7]{0:T(128)}, u32[]{:S(2)}) copy-start(f32[7]{0:T(128)} %rk_ref.1) | copy-start | bytes 88
  3.2 29.0 %copy-start.1 = (bf16[256,512]{1,0:T(8,128)(2,1)S(1)}, bf16[256,512]{1,0:T(8,128)(2,1)}, u32[]{:S(2)}) copy-start(bf16[256,512]{1,0:T(8,128)(2,1)} %constant.11.clone.w_ref) | copy-start | bytes 786436
  3.2 29.0 %copy-start.2 = (bf16[1,2,32,512]{3,2,1,0:T(8,128)(2,1)S(1)}, bf16[1,2,32,512]{3,2,1,0:T(8,128)(2,1)}, u32[]{:S(2)}) copy-start(bf16[1,2,32,512]{3,2,1,0:T(8,128)(2,1)} %param.19) | copy-start | bytes 196612
  3.2 29.0 %copy-start.3 = (f32[1,32,512]{2,1,0:T(8,128)S(1)}, f32[1,32,512]{2,1,0:T(8,128)}, u32[]{:S(2)}) copy-start(f32[1,32,512]{2,1,0:T(8,128)} %param.20) | copy-start | bytes 196612
  3.2 29.0 %all-to-all-start = ((bf16[32,32,256]{2,1,0:T(8,128)(2,1)}), bf16[32,32,256]{2,1,0:T(8,128)(2,1)S(1)}, u32[]{:S(2)}, u32[]{:S(2)}) async-start(bf16[32,32,256]{2,1,0:T(8,128)(2,1)} %facet_to_slots.1), calls=%async_computation | async-start | bytes 1048576 | tf_op jit(solution)/shard_map/all_to_all | solution.py:522
  14.6 0.7 %copy-start.7 = (s32[32]{0:T(128)S(1)}, s32[32]{0:T(128)}, u32[]{:S(2)}) copy-start(s32[32]{0:T(128)} %offs_ref.3) | copy-start | bytes 388
  14.6 0.7 %copy-start.8 = (s32[32]{0:T(128)S(1)}, s32[32]{0:T(128)}, u32[]{:S(2)}) copy-start(s32[32]{0:T(128)} %order_ref.3) | copy-start | bytes 388
  14.6 0.7 %copy-start.10 = (f32[7]{0:T(128)S(1)}, f32[7]{0:T(128)}, u32[]{:S(2)}) copy-start(f32[7]{0:T(128)} %ck_ref.3) | copy-start | bytes 88
  32.2 4.0 %copy-start = (bf16[512,256]{1,0:T(8,128)(2,1)S(1)}, bf16[512,256]{1,0:T(8,128)(2,1)}, u32[]{:S(2)}) copy-start(bf16[512,256]{1,0:T(8,128)(2,1)} %constant.12.clone.wt_tab_ref) | copy-start | bytes 786436
  32.6 1.3 %collective-permute-start = (bf16[8,2048]{1,0:T(8,128)(2,1)S(1)}, bf16[8,2048]{1,0:T(8,128)(2,1)S(1)}, u32[]{:S(2)}, u32[]{:S(2)}) collective-permute-start(bf16[8,2048]{1,0:T(8,128)(2,1)S(1)} %get-tuple-element.12), channel_id=1, source_target_pairs={{0,1},{1,0},{2,3},{3,2},{4,5},{5,4},{6,7},{7,6},{8,9},{9,8},{10,11... | collective-permute-start | bytes 98312 | tf_op jit(solution)/shard_map/ppermute | solution.py:511
  32.7 3.4 %collective-permute-start.1 = (bf16[8,2048]{1,0:T(8,128)(2,1)S(1)}, bf16[8,2048]{1,0:T(8,128)(2,1)S(1)}, u32[]{:S(2)}, u32[]{:S(2)}) collective-permute-start(bf16[8,2048]{1,0:T(8,128)(2,1)S(1)} %get-tuple-element.13), channel_id=1, source_target_pairs={{0,7},{1,2},{2,1},{3,4},{4,3},{5,6},{6,5},{7,0},{8,15},{9,10},{10,... | collective-permute-start | bytes 98312 | tf_op jit(solution)/shard_map/ppermute | solution.py:511
  37.9 23.0 %copy-start.4 = (bf16[256,256]{1,0:T(8,128)(2,1)S(1)}, bf16[256,256]{1,0:T(8,128)(2,1)}, u32[]{:S(2)}) copy-start(bf16[256,256]{1,0:T(8,128)(2,1)} %constant.13.clone.tab_ref) | copy-start | bytes 393220
  37.9 23.0 %copy-start.6 = (f32[1,2048]{1,0:T(1,128)S(1)}, f32[1,2048]{1,0:T(1,128)}, u32[]{:S(2)}) copy-start(f32[1,2048]{1,0:T(1,128)} %constant.14.clone.win_ref) | copy-start | bytes 24580

commit v7 on v6

--- a/solution.py
+++ b/solution.py
@@ -27,14 +27,6 @@
     a = 2.0 * np.pi * ((g * row) % 128) / 128
     c, s = np.cos(a), np.sin(a)
     return np.block([[c, -s], [s, c]]).astype(np.float32)
-
-
-def subgrid_table():
-    j = np.arange(SG)[None, :]
-    k = np.arange(XC)[:, None]
-    a = 2.0 * np.pi * ((j * k) % SG) / SG
-    c, s = np.cos(a) / 64.0, np.sin(a) / 64.0
-    return np.block([[c, s], [-s, c]]).astype(np.float32)
 
 
 def facet_phase():
@@ -207,12 +199,10 @@
     for i in range(NF):
         off = offs_ref[order_ref[i]]
         b, s = off >> 7, off & 127
-        back = (128 - s) & 127
         keep = lane >= s.astype(F32).astype(BF)
         for p in range(2):
             cols = slice(128 * p, 128 * (p + 1))
-            x = jnp.where(keep, nat_ref[b, :, cols], nat_ref[b + 1, :, cols])
-            out_ref[i, :, cols] = pltpu.roll(x, back, 1)
+            out_ref[i, :, cols] = jnp.where(keep, nat_ref[b, :, cols], nat_ref[b + 1, :, cols])
         if i % 8 == 7:
             part = pl.ds(i - 7, 8)
             copy = pltpu.make_async_copy(out_ref.at[part], out_hbm.at[part], out_sem.at[i // 8])
@@ -255,7 +245,7 @@
 
 def kt_body(
     offs_ref, order_ref, rk_ref, ck_ref, count_ref, cell_ref, ph_ref,
-    dt_ref, pho_ref, live_ref,
+    dt_ref, pho_ref, live_ref, w_ref, back_ref, taps_ref,
 ):
     off = offs_ref[order_ref[lax.axis_index("facet")]]
     back = (128 - 2 * off) & 127
@@ -265,8 +255,20 @@
     m = jnp.zeros((SG, VM), F32)
     for t in range(TAPS):
         m = jnp.where(d == t, rk_ref[t], m)
+        taps_ref[t : t + 1, :] = jnp.full((1, SG), ck_ref[t], F32)
+    taps_ref[TAPS : TAPS + 1, :] = jnp.zeros((1, SG), F32)
     dt_ref[...] = m.astype(BF)
     live_ref[...] = (lax.broadcasted_iota(jnp.int32, (1, VM), 1) < count_ref[0]).astype(F32)
+    for ref, shape, axis in ((w_ref, (XC, SG), 0), (back_ref, (SG, XC), 1)):
+        k = (lax.broadcasted_iota(jnp.int32, shape, axis) - off) & (XC - 1)
+        j = lax.broadcasted_iota(jnp.int32, shape, 1 - axis)
+        c, s = turn((8 * j * k) & (FR - 1))
+        c, s, t = (x.astype(BF) for x in (c * (1 / 64), s * (1 / 64), s * (-1 / 64)))
+        rows, cols = shape
+        ref[0:rows, 0:cols] = c
+        ref[rows:, cols:] = c
+        ref[0:rows, cols:] = s if axis == 0 else t
+        ref[rows:, 0:cols] = t if axis == 0 else s
 
 
 def kt(offs, order, rk, ck, count, cell):
@@ -276,11 +278,14 @@
             jax.ShapeDtypeStruct((SG, VM), BF),
             jax.ShapeDtypeStruct((2, NF, 128), F32),
             jax.ShapeDtypeStruct((1, VM), F32),
+            jax.ShapeDtypeStruct((2 * XC, 2 * SG), BF),
+            jax.ShapeDtypeStruct((2 * SG, 2 * XC), BF),
+            jax.ShapeDtypeStruct((8, SG), F32),
         ),
         in_specs=[SMEM] * 5 + [VMEM] * 2,
-        out_specs=(VMEM, VMEM, VMEM),
+        out_specs=(VMEM,) * 6,
         compiler_params=PARAMS,
-        cost_estimate=pl.CostEstimate(flops=2000000, bytes_accessed=400000, transcendentals=0),
+        cost_estimate=pl.CostEstimate(flops=4000000, bytes_accessed=1000000, transcendentals=0),
         name="slot_tables",
     )(offs, order, rk, ck, count, cell, facet_phase())
 
@@ -323,7 +328,7 @@
 EDGE = 2 * SG + 3 * VM
 
 
-def ka(arrived, obs, wt, phases):
+def ka(arrived, obs, wt, table, phases):
     return pl.pallas_call(
         ka_body,
         out_shape=(
@@ -336,11 +341,11 @@
         scratch_shapes=[pltpu.VMEM((NF, CB, 2 * SG), F32)],
         compiler_params=PARAMS,
         name="sum_facets",
-    )(arrived, obs, wt, jnp.asarray(subgrid_table(), BF), phases)
+    )(arrived, obs, wt, table, phases)
 
 
 def kb_body(
-    ck_ref, sub_ref, obs_ref, wt_ref, sibling_ref, neighbour_ref, wt_tab_ref, dt_ref, pho_ref,
+    taps_ref, sub_ref, obs_ref, wt_ref, sibling_ref, neighbour_ref, wt_tab_ref, dt_ref, pho_ref,
     live_ref,
     res_hbm, out_ref, sub_ext_ref, conv_ref, res_ref, ext_ref, back_ref, y_ref, sem,
 ):
@@ -364,7 +369,7 @@
         lo = jnp.zeros((8, SG), F32)
         hi = jnp.zeros((8, SG), F32)
         for t in range(TAPS):
-            k = ck_ref[t]
+            k = taps_ref[t : t + 1, :]
             own = own + k * sub_ext_ref[13 + t : 45 + t, lanes]
             lo = lo + k * sub_ext_ref[5 + t : 13 + t, lanes]
             hi = hi + k * sub_ext_ref[45 + t : 53 + t, lanes]
@@ -396,7 +401,7 @@
         ext_ref[p, 40:48, :] = halo
         b = jnp.zeros((CB, SG), F32)
         for t in range(TAPS):
-            b = b + ck_ref[t] * ext_ref[p, 11 - t : 43 - t, :]
+            b = b + taps_ref[t : t + 1, :] * ext_ref[p, 11 - t : 43 - t, :]
         back_ref[p] = b
     for h in range(2):
         lanes = slice(128 * h, 128 * (h + 1))
@@ -411,14 +416,14 @@
     copy.wait()
 
 
-def kb(ck, sub, obs, wt, sibling, neighbour, table, phases, live):
+def kb(taps, sub, obs, wt, sibling, neighbour, back, table, phases, live):
     return pl.pallas_call(
         kb_body,
         out_shape=(
             jax.ShapeDtypeStruct((2, CB, VM), F32),
             jax.ShapeDtypeStruct((NF, CB, 2 * XC), BF),
         ),
-        in_specs=[SMEM] + [VMEM] * 9,
+        in_specs=[VMEM] * 10,
         out_specs=(ANY, VMEM),
         scratch_shapes=[
             pltpu.VMEM((64, 2 * SG), F32),
@@ -432,17 +437,24 @@
         compiler_params=PARAMS,
         name="slot_round_trip",
     )(
-        ck, sub, obs, wt, sibling, neighbour, jnp.asarray(subgrid_table().T, BF), table, phases,
-        live,
+        taps, sub, obs, wt, sibling, neighbour, back, table, phases, live
     )
 
 
 def k3_body(
-    offs_ref, order_ref, bp_ref, win_ref, tab_ref,
-    out_hbm, nat_ref, tw_ref, lhs_ref, v_ref, out_ref, sem,
+    offs_hbm, order_hbm, bp_ref, win_ref, tab_ref,
+    out_hbm, offs_ref, order_ref, nat_ref, tw_ref, lhs_ref, v_ref, out_ref, small_sem, sem,
 ):
+    small = [
+        pltpu.make_async_copy(offs_hbm, offs_ref, small_sem.at[0]),
+        pltpu.make_async_copy(order_hbm, order_ref, small_sem.at[1]),
+    ]
+    for copy in small:
+        copy.start()
     tw_ref[0], tw_ref[1] = twiddles(lax.axis_index("facet"))
     nat_ref[...] = jnp.zeros_like(nat_ref)
+    for copy in small:
+        copy.wait()
     lane = lax.broadcasted_iota(jnp.int32, (CB, 128), 1)
     for i in range(NF):
         off = offs_ref[order_ref[i]]
@@ -450,7 +462,7 @@
         keep = lane >= s
         for p in range(2):
             cols = slice(128 * p, 128 * (p + 1))
-            x = pltpu.roll(bp_ref[i, :, cols], s, 1).astype(F32)
+            x = bp_ref[i, :, cols].astype(F32)
             nat_ref[b, :, cols] += jnp.where(keep, x, 0.0)
             nat_ref[b + 1, :, cols] += jnp.where(keep, 0.0, x)
     nat_ref[0] += nat_ref[16]
@@ -489,14 +501,17 @@
     return pl.pallas_call(
         k3_body,
         out_shape=jax.ShapeDtypeStruct((CB, FR), F32),
-        in_specs=[SMEM, SMEM, VMEM, VMEM, VMEM],
+        in_specs=[ANY, ANY, VMEM, VMEM, VMEM],
         out_specs=ANY,
         scratch_shapes=[
+            pltpu.SMEM((NF,), jnp.int32),
+            pltpu.SMEM((NF,), jnp.int32),
             pltpu.VMEM((17, CB, 256), F32),
             pltpu.VMEM((2, 16, 128), F32),
             pltpu.VMEM((16, CB, 256), BF),
             pltpu.VMEM((16, CB, 256), F32),
             pltpu.VMEM((CB, FR), F32),
+            pltpu.SemaphoreType.DMA((2,)),
             pltpu.SemaphoreType.DMA((4,)),
         ],
         compiler_params=PARAMS,
@@ -520,16 +535,16 @@
 
     out = k1(subgrid_offsets, owner_order, sky_image)
     arrived = lax.all_to_all(out, "facet", split_axis=0, concat_axis=0, tiled=True)
-    table, phases, live = kt(
+    table, phases, live, there, back, taps = kt(
         subgrid_offsets, owner_order, row_kernel, column_kernel, visibility_count, visibility_cell
     )
-    sub, sibling, neighbour = ka(arrived, obs, wt, phases)
+    sub, sibling, neighbour = ka(arrived, obs, wt, there, phases)
     sibling, neighbour = swapped(sibling, neighbour)
     res, outgoing = kb(
-        column_kernel, sub, obs, wt, sibling, neighbour, table, phases, live
+        taps, sub, obs, wt, sibling, neighbour, back, table, phases, live
     )
-    back = lax.all_to_all(outgoing, "facet", split_axis=0, concat_axis=0, tiled=True)
-    dirty = k3(subgrid_offsets, owner_order, back)
+    returned = lax.all_to_all(outgoing, "facet", split_axis=0, concat_axis=0, tiled=True)
+    dirty = k3(subgrid_offsets, owner_order, returned)
     return (res[None], dirty)
 
 

time: 64 us -> 63.2 us (0.988)
    pallas_call x1, Pallas kernels: 1.76 us -> 1.07 us  [kb(): pl.pallas_call(kb_body, out_shape=(jax.ShapeDtypeStruct((2, CB, VM), F32)...]
  transfers between devices with their start and end apart: 3 -> 3, of which waited for: 3 -> 3; matrix products, arithmetic and copies ran while one was open for 0% -> 0% of each run, Pallas kernels for 2% -> 3%
where the time goes in v7:
time: 63.2 us; the launch traced here: 62.3 us
  blocking collectives  23 us (36%)
  waiting for transfers between devices  17.9 us (28%)
  starting transfers between devices  12 us (19%)
  Pallas kernels  7.88 us (12%)
  between operations  1.47 us (2%)
    all_to_all x1, blocking collectives, local(): lax.all_to_all(outgoing, 'facet', split_axis=0, concat_axis=0, tiled=True)  23 us
    all_to_all x1, waiting for transfers between devices, local(): lax.all_to_all(out, 'facet', split_axis=0, concat_axis=0, tiled=True)  15 us
    all_to_all x1, starting transfers between devices, local(): lax.all_to_all(out, 'facet', split_axis=0, concat_axis=0, tiled=True)  11.3 us
    pallas_call x1, Pallas kernels, k1(): pl.pallas_call(k1_body, out_shape=jax.ShapeDtypeStruct((NF, CB, 2 * XC),...  2.41 us
    ppermute x1, waiting for transfers between devices, swapped(): lax.ppermute(neighbour, 'uv', far)  2.23 us
    pallas_call x1, Pallas kernels, k3(): pl.pallas_call(k3_body, out_shape=jax.ShapeDtypeStruct((CB, FR), F32), in...  2.11 us
    pallas_call x1, Pallas kernels, kt(): pl.pallas_call(kt_body, out_shape=(jax.ShapeDtypeStruct((SG, VM), BF), ja...  1.85 us
  transfers between devices with their start and end apart: 3, of which 3 were waited for; matrix products, arithmetic and copies ran while one was open for 0% of the time, Pallas kernels for 3%

profile of v7, /device:TPU:48, one launch (start us, length us, event | category | flops | bytes accessed | tf_op | source)
XLA Modules:
  0.0 62.3 jit_solution(362660769243312016)
XLA Ops:
  0.6 2.4 %facet_to_slots.1 = bf16[32,32,256]{2,1,0:T(8,128)(2,1)} custom-call(s32[32]{0:T(128)} %offs_hbm.3, s32[32]{0:T(128)} %order_hbm.3, bf16[32,2048]{1,0:T(8,128)(2,1)} %sky_hbm.1), custom_call_target="tpu_custom_call" | custom-call | tf_op jit(solution)/shard_map/facet_to_slots/pallas_call | solution.py:222
  3.0 0.0 copy-start.3
  3.1 0.0 copy-start.7
  3.1 0.0 copy-start.9
  3.1 0.0 copy-start
  3.1 0.0 copy-start.1
  3.1 11.3 %all-to-all-start = ((bf16[32,32,256]{2,1,0:T(8,128)(2,1)}), bf16[32,32,256]{2,1,0:T(8,128)(2,1)S(1)}, u32[]{:S(2)}, u32[]{:S(2)}) async-start(bf16[32,32,256]{2,1,0:T(8,128)(2,1)} %facet_to_slots.1), calls=%async_computation | async-start | bytes 1048576 | tf_op jit(solution)/shard_map/all_to_all | solution.py:537
  14.4 0.0 copy-start.5
  14.5 0.0 copy-start.6
  14.5 0.0 copy-start.8
  15.1 0.0 copy-done.3
  15.2 0.0 copy-done.7
  15.2 1.8 %slot_tables.1 = (bf16[256,512]{1,0:T(8,128)(2,1)S(1)}, f32[2,32,128]{2,1,0:T(8,128)S(1)}, f32[1,512]{1,0:T(1,128)S(1)}, bf16[256,512]{1,0:T(8,128)(2,1)S(1)}, b...) custom-call(s32[32]{0:T(128)S(1)} %copy-done.5, s32[32]{0:T(128)S(1)} %copy-done.6, f32[7]{0:T(128)S(1)} %copy-done.8, ...), custom_call_target="tpu_custom_call" | custom-call | flops 4000000 | bytes 1000000 | tf_op jit(solution)/shard_map/slot_tables/pallas_call | solution.py:275
  17.1 15.0 %all-to-all-done.arr_ref = bf16[32,32,256]{2,1,0:T(8,128)(2,1)S(1)} async-done(((bf16[32,32,256]{2,1,0:T(8,128)(2,1)}), bf16[32,32,256]{2,1,0:T(8,128)(2,1)S(1)}, u32[]{:S(2)}, u32[]{:S(2)}) %all-to-all-start) | async-done | bytes 524320 | tf_op jit(solution)/shard_map/all_to_all | solution.py:537
  32.1 0.4 sum_facets.1
  32.5 0.1 collective-permute-start
  32.6 0.6 collective-permute-start.1
  33.2 0.6 %collective-permute-done.sibling_ref = bf16[8,2048]{1,0:T(8,128)(2,1)S(1)} collective-permute-done((bf16[8,2048]{1,0:T(8,128)(2,1)S(1)}, bf16[8,2048]{1,0:T(8,128)(2,1)S(1)}, u32[]{:S(2)}, u32[]{:S(2)}) %collective-permute-start) | collective-permute-done | bytes 32800 | tf_op jit(solution)/shard_map/ppermute | solution.py:526
  33.8 2.2 %collective-permute-done.1.neighbour_ref = bf16[8,2048]{1,0:T(8,128)(2,1)S(1)} collective-permute-done((bf16[8,2048]{1,0:T(8,128)(2,1)S(1)}, bf16[8,2048]{1,0:T(8,128)(2,1)S(1)}, u32[]{:S(2)}, u32[]{:S(2)}) %collective-permute-start.1) | collective-permute-done | bytes 32800 | tf_op jit(solution)/shard_map/ppermute | solution.py:526
  36.0 1.1 %slot_round_trip.1 = (f32[2,32,512]{2,1,0:T(8,128)}, bf16[32,32,256]{2,1,0:T(8,128)(2,1)S(1)}) custom-call(f32[8,256]{1,0:T(8,128)S(1)} %get-tuple-element.13.taps_ref, f32[32,512]{1,0:T(8,128)S(1)} %get-tuple-element.16.sub_ref, bf16[2,32,512]{2,1,0:T(8,128)(2,1)S(1)} %bitcast.4, f32[32,512]{1,0:T(8,128)S(1)} %bitcast.6, ...), custom_call_target="tpu_custom_call" | custom-call | tf_op jit(solution)/shard_map/slot_round_trip/pallas_call | solution.py:420
  37.1 0.0 copy-start.2
  37.1 0.0 copy-start.4
  37.1 23.0 %all_to_all.10.bp_ref = bf16[32,32,256]{2,1,0:T(8,128)(2,1)S(1)} all-to-all(bf16[32,32,256]{2,1,0:T(8,128)(2,1)S(1)} %get-tuple-element.23), channel_id=1, replica_groups=mesh['facet'=32,'uv'=8] {'facet'}, dimensions={0} | all-to-all | bytes 1048576 | tf_op jit(solution)/shard_map/all_to_all | solution.py:546
  60.2 2.1 %slots_to_facet.1 = f32[32,2048]{1,0:T(8,128)} custom-call(s32[32]{0:T(128)S(1)} %copy-done.5, s32[32]{0:T(128)S(1)} %copy-done.6, bf16[32,32,256]{2,1,0:T(8,128)(2,1)S(1)} %all_to_all.10.bp_ref, f32[1,2048]{1,0:T(1,128)S(1)} %copy-done.4, bf16[256,256]{1,0:T(8,128)(2,1)S(1)} %copy-done.2), custom_call_target="tpu_custom_call" | custom-call | tf_op jit(solution)/shard_map/slots_to_facet/pallas_call | solution.py:501
  (8 shorter events, 0.0 us)
Async XLA Ops:
  3.0 12.1 %copy-start.3 = (f32[2,32,128]{2,1,0:T(8,128)S(1)}, f32[2,32,128]{2,1,0:T(8,128)}, u32[]{:S(2)}) copy-start(f32[2,32,128]{2,1,0:T(8,128)} %constant.6.clone.ph_ref) | copy-start | bytes 98308
  3.1 12.1 %copy-start.7 = (s32[1,512]{1,0:T(1,128)S(1)}, s32[1,512]{1,0:T(1,128)}, u32[]{:S(2)}) copy-start(s32[1,512]{1,0:T(1,128)} %cell_ref.1) | copy-start | bytes 6148
  3.1 12.1 %copy-start.9 = (f32[7]{0:T(128)S(1)}, f32[7]{0:T(128)}, u32[]{:S(2)}) copy-start(f32[7]{0:T(128)} %ck_ref.1) | copy-start | bytes 88
  3.1 29.0 %copy-start = (bf16[1,2,32,512]{3,2,1,0:T(8,128)(2,1)S(1)}, bf16[1,2,32,512]{3,2,1,0:T(8,128)(2,1)}, u32[]{:S(2)}) copy-start(bf16[1,2,32,512]{3,2,1,0:T(8,128)(2,1)} %param.17) | copy-start | bytes 196612
  3.1 29.0 %copy-start.1 = (f32[1,32,512]{2,1,0:T(8,128)S(1)}, f32[1,32,512]{2,1,0:T(8,128)}, u32[]{:S(2)}) copy-start(f32[1,32,512]{2,1,0:T(8,128)} %param.18) | copy-start | bytes 196612
  3.1 29.0 %all-to-all-start = ((bf16[32,32,256]{2,1,0:T(8,128)(2,1)}), bf16[32,32,256]{2,1,0:T(8,128)(2,1)S(1)}, u32[]{:S(2)}, u32[]{:S(2)}) async-start(bf16[32,32,256]{2,1,0:T(8,128)(2,1)} %facet_to_slots.1), calls=%async_computation | async-start | bytes 1048576 | tf_op jit(solution)/shard_map/all_to_all | solution.py:537
  14.4 0.7 %copy-start.5 = (s32[32]{0:T(128)S(1)}, s32[32]{0:T(128)}, u32[]{:S(2)}) copy-start(s32[32]{0:T(128)} %offs_hbm.3) | copy-start | bytes 388
  14.5 0.7 %copy-start.6 = (s32[32]{0:T(128)S(1)}, s32[32]{0:T(128)}, u32[]{:S(2)}) copy-start(s32[32]{0:T(128)} %order_hbm.3) | copy-start | bytes 388
  14.5 0.7 %copy-start.8 = (f32[7]{0:T(128)S(1)}, f32[7]{0:T(128)}, u32[]{:S(2)}) copy-start(f32[7]{0:T(128)} %rk_ref.1) | copy-start | bytes 88
  32.5 1.3 %collective-permute-start = (bf16[8,2048]{1,0:T(8,128)(2,1)S(1)}, bf16[8,2048]{1,0:T(8,128)(2,1)S(1)}, u32[]{:S(2)}, u32[]{:S(2)}) collective-permute-start(bf16[8,2048]{1,0:T(8,128)(2,1)S(1)} %get-tuple-element.17), channel_id=1, source_target_pairs={{0,1},{1,0},{2,3},{3,2},{4,5},{5,4},{6,7},{7,6},{8,9},{9,8},{10,11... | collective-permute-start | bytes 98312 | tf_op jit(solution)/shard_map/ppermute | solution.py:526
  32.6 3.4 %collective-permute-start.1 = (bf16[8,2048]{1,0:T(8,128)(2,1)S(1)}, bf16[8,2048]{1,0:T(8,128)(2,1)S(1)}, u32[]{:S(2)}, u32[]{:S(2)}) collective-permute-start(bf16[8,2048]{1,0:T(8,128)(2,1)S(1)} %get-tuple-element.18), channel_id=1, source_target_pairs={{0,7},{1,2},{2,1},{3,4},{4,3},{5,6},{6,5},{7,0},{8,15},{9,10},{10,... | collective-permute-start | bytes 98312 | tf_op jit(solution)/shard_map/ppermute | solution.py:526
  37.1 23.0 %copy-start.2 = (bf16[256,256]{1,0:T(8,128)(2,1)S(1)}, bf16[256,256]{1,0:T(8,128)(2,1)}, u32[]{:S(2)}) copy-start(bf16[256,256]{1,0:T(8,128)(2,1)} %constant.7.clone.tab_ref) | copy-start | bytes 393220
  37.1 23.0 %copy-start.4 = (f32[1,2048]{1,0:T(1,128)S(1)}, f32[1,2048]{1,0:T(1,128)}, u32[]{:S(2)}) copy-start(f32[1,2048]{1,0:T(1,128)} %constant.8.clone.win_ref) | copy-start | bytes 24580

commit v8 on v7

--- a/solution.py
+++ b/solution.py
@@ -244,13 +244,25 @@
 
 
 def kt_body(
-    offs_ref, order_ref, rk_ref, ck_ref, count_ref, cell_ref, ph_ref,
-    dt_ref, pho_ref, live_ref, w_ref, back_ref, taps_ref,
+    offs_ref, order_ref, rk_ref, ck_ref, count_ref, cell_ref, ph_ref, obs_ref, wt_ref,
+    dt_ref, pho_ref, live_ref, w_ref, back_ref, taps_ref, offset_ref,
+    sibling_ref, neighbour_ref,
 ):
     off = offs_ref[order_ref[lax.axis_index("facet")]]
     back = (128 - 2 * off) & 127
     pho_ref[0] = pltpu.roll(ph_ref[0], back, 1)
     pho_ref[1] = pltpu.roll(ph_ref[1], back, 1)
+    even = lax.rem(lax.axis_index("uv"), 2) == 0
+    for p in range(3):
+        edges = obs_ref[p].astype(F32) if p < 2 else wt_ref[...]
+        first, last = edges[0:8], edges[24:32]
+        sibling_ref[:, p * VM : (p + 1) * VM] = jnp.where(even, last, first).astype(BF)
+        neighbour_ref[:, p * VM : (p + 1) * VM] = jnp.where(even, first, last).astype(BF)
+    lane = lax.broadcasted_iota(jnp.int32, (8, 128), 1)
+    offsets = jnp.zeros((8, 128), jnp.int32)
+    for i in range(NF):
+        offsets = jnp.where(lane == i, offs_ref[order_ref[i]], offsets)
+    offset_ref[...] = offsets
     d = lax.broadcasted_iota(jnp.int32, (SG, VM), 0) - cell_ref[...] + 3
     m = jnp.zeros((SG, VM), F32)
     for t in range(TAPS):
@@ -271,7 +283,7 @@
         ref[rows:, 0:cols] = t if axis == 0 else s
 
 
-def kt(offs, order, rk, ck, count, cell):
+def kt(offs, order, rk, ck, count, cell, obs, wt):
     return pl.pallas_call(
         kt_body,
         out_shape=(
@@ -281,17 +293,20 @@
             jax.ShapeDtypeStruct((2 * XC, 2 * SG), BF),
             jax.ShapeDtypeStruct((2 * SG, 2 * XC), BF),
             jax.ShapeDtypeStruct((8, SG), F32),
+            jax.ShapeDtypeStruct((8, 128), jnp.int32),
+            jax.ShapeDtypeStruct((8, EDGE), BF),
+            jax.ShapeDtypeStruct((8, EDGE), BF),
         ),
-        in_specs=[SMEM] * 5 + [VMEM] * 2,
-        out_specs=(VMEM,) * 6,
+        in_specs=[SMEM] * 5 + [VMEM] * 4,
+        out_specs=(VMEM,) * 9,
         compiler_params=PARAMS,
         cost_estimate=pl.CostEstimate(flops=4000000, bytes_accessed=1000000, transcendentals=0),
         name="slot_tables",
-    )(offs, order, rk, ck, count, cell, facet_phase())
+    )(offs, order, rk, ck, count, cell, facet_phase(), obs, wt)
 
 
 def ka_body(
-    arr_ref, obs_ref, wt_ref, w_ref, pho_ref,
+    arr_ref, w_ref, pho_ref,
     sub_ref, sibling_ref, neighbour_ref, u_ref,
 ):
     u = jnp.dot(arr_ref[...].reshape(NF * CB, 256), w_ref[...], preferred_element_type=F32)
@@ -309,57 +324,46 @@
         sub_ref[:, 128 * h : 128 * (h + 1)] = re
         sub_ref[:, SG + 128 * h : SG + 128 * (h + 1)] = im
     even = lax.rem(lax.axis_index("uv"), 2) == 0
-    wide = 2 * SG
-
-    def put(cols, first, last):
-        sibling_ref[:, cols] = jnp.where(even, last, first).astype(BF)
-        neighbour_ref[:, cols] = jnp.where(even, first, last).astype(BF)
-
-    put(slice(0, wide), sub_ref[0:8, :], sub_ref[24:32, :])
-    for p in range(2):
-        put(
-            slice(wide + p * VM, wide + (p + 1) * VM),
-            obs_ref[p, 0:8, :].astype(F32),
-            obs_ref[p, 24:32, :].astype(F32),
-        )
-    put(slice(wide + 2 * VM, EDGE), wt_ref[0:8, :], wt_ref[24:32, :])
-
-
-EDGE = 2 * SG + 3 * VM
-
-
-def ka(arrived, obs, wt, table, phases):
+    first, last = sub_ref[0:8, :], sub_ref[24:32, :]
+    sibling_ref[...] = jnp.where(even, last, first).astype(BF)
+    neighbour_ref[...] = jnp.where(even, first, last).astype(BF)
+
+
+EDGE = 3 * VM
+
+
+def ka(arrived, table, phases):
     return pl.pallas_call(
         ka_body,
         out_shape=(
             jax.ShapeDtypeStruct((CB, 2 * SG), F32),
-            jax.ShapeDtypeStruct((8, EDGE), BF),
-            jax.ShapeDtypeStruct((8, EDGE), BF),
+            jax.ShapeDtypeStruct((8, 2 * SG), BF),
+            jax.ShapeDtypeStruct((8, 2 * SG), BF),
         ),
-        in_specs=[VMEM] * 5,
+        in_specs=[VMEM] * 3,
         out_specs=(VMEM, VMEM, VMEM),
         scratch_shapes=[pltpu.VMEM((NF, CB, 2 * SG), F32)],
         compiler_params=PARAMS,
         name="sum_facets",
-    )(arrived, obs, wt, table, phases)
+    )(arrived, table, phases)
 
 
 def kb_body(
     taps_ref, sub_ref, obs_ref, wt_ref, sibling_ref, neighbour_ref, wt_tab_ref, dt_ref, pho_ref,
-    live_ref,
+    live_ref, sibling_vis_ref, neighbour_vis_ref,
     res_hbm, out_ref, sub_ext_ref, conv_ref, res_ref, ext_ref, back_ref, y_ref, sem,
 ):
     uv = lax.axis_index("uv")
     even = lax.rem(uv, 2) == 0
     in_before, in_after = uv > 0, uv < 7
 
-    def sides(cols):
-        s, n = sibling_ref[:, cols].astype(F32), neighbour_ref[:, cols].astype(F32)
+    def sides(s, n):
+        s, n = s.astype(F32), n.astype(F32)
         before = jnp.where(in_before, jnp.where(even, n, s), 0.0)
         after = jnp.where(in_after, jnp.where(even, s, n), 0.0)
         return before, after
 
-    before, after = sides(slice(0, 2 * SG))
+    before, after = sides(sibling_ref[...], neighbour_ref[...])
     sub_ext_ref[8:16, :] = before
     sub_ext_ref[16:48, :] = sub_ref[...]
     sub_ext_ref[48:56, :] = after
@@ -379,13 +383,15 @@
 
     live = live_ref[...]
     wt = wt_ref[...] * live
-    before, after = sides(slice(2 * SG + 2 * VM, EDGE))
+    cols = slice(2 * VM, EDGE)
+    before, after = sides(sibling_vis_ref[:, cols], neighbour_vis_ref[:, cols])
     wt_h = halo_rows(after, before, 0) * live
     parts = []
     for p in range(2):
         own = wt * (obs_ref[p].astype(F32) - model[p * CE : p * CE + CB])
         res_ref[p] = own
-        before, after = sides(slice(2 * SG + p * VM, 2 * SG + (p + 1) * VM))
+        cols = slice(p * VM, (p + 1) * VM)
+        before, after = sides(sibling_vis_ref[:, cols], neighbour_vis_ref[:, cols])
         obs_h = halo_rows(after, before, 0)
         parts += [own, wt_h * (obs_h - model[p * CE + CB : (p + 1) * CE])]
     copy = pltpu.make_async_copy(res_ref, res_hbm, sem)
@@ -416,14 +422,14 @@
     copy.wait()
 
 
-def kb(taps, sub, obs, wt, sibling, neighbour, back, table, phases, live):
+def kb(taps, sub, obs, wt, sibling, neighbour, back, table, phases, live, *edges):
     return pl.pallas_call(
         kb_body,
         out_shape=(
             jax.ShapeDtypeStruct((2, CB, VM), F32),
             jax.ShapeDtypeStruct((NF, CB, 2 * XC), BF),
         ),
-        in_specs=[VMEM] * 10,
+        in_specs=[VMEM] * 12,
         out_specs=(ANY, VMEM),
         scratch_shapes=[
             pltpu.VMEM((64, 2 * SG), F32),
@@ -437,27 +443,20 @@
         compiler_params=PARAMS,
         name="slot_round_trip",
     )(
-        taps, sub, obs, wt, sibling, neighbour, back, table, phases, live
+        taps, sub, obs, wt, sibling, neighbour, back, table, phases, live, *edges
     )
 
 
 def k3_body(
-    offs_hbm, order_hbm, bp_ref, win_ref, tab_ref,
-    out_hbm, offs_ref, order_ref, nat_ref, tw_ref, lhs_ref, v_ref, out_ref, small_sem, sem,
+    offset_ref, bp_ref, win_ref, tab_ref,
+    out_hbm, nat_ref, tw_ref, lhs_ref, v_ref, out_ref, sem,
 ):
-    small = [
-        pltpu.make_async_copy(offs_hbm, offs_ref, small_sem.at[0]),
-        pltpu.make_async_copy(order_hbm, order_ref, small_sem.at[1]),
-    ]
-    for copy in small:
-        copy.start()
+    offsets = offset_ref[...]
     tw_ref[0], tw_ref[1] = twiddles(lax.axis_index("facet"))
     nat_ref[...] = jnp.zeros_like(nat_ref)
-    for copy in small:
-        copy.wait()
     lane = lax.broadcasted_iota(jnp.int32, (CB, 128), 1)
     for i in range(NF):
-        off = offs_ref[order_ref[i]]
+        off = offsets[0, i]
         b, s = off >> 7, off & 127
         keep = lane >= s
         for p in range(2):
@@ -497,26 +496,23 @@
         copy.wait()
 
 
-def k3(offs, order, bp):
+def k3(offsets, bp):
     return pl.pallas_call(
         k3_body,
         out_shape=jax.ShapeDtypeStruct((CB, FR), F32),
-        in_specs=[ANY, ANY, VMEM, VMEM, VMEM],
+        in_specs=[VMEM] * 4,
         out_specs=ANY,
         scratch_shapes=[
-            pltpu.SMEM((NF,), jnp.int32),
-            pltpu.SMEM((NF,), jnp.int32),
             pltpu.VMEM((17, CB, 256), F32),
             pltpu.VMEM((2, 16, 128), F32),
             pltpu.VMEM((16, CB, 256), BF),
             pltpu.VMEM((16, CB, 256), F32),
             pltpu.VMEM((CB, FR), F32),
-            pltpu.SemaphoreType.DMA((2,)),
             pltpu.SemaphoreType.DMA((4,)),
         ],
         compiler_params=PARAMS,
         name="slots_to_facet",
-    )(offs, order, bp, window(), jnp.asarray(block_table().T, BF))
+    )(offsets, bp, window(), jnp.asarray(block_table().T, BF))
 
 
 def swapped(sibling, neighbour):
@@ -535,16 +531,18 @@
 
     out = k1(subgrid_offsets, owner_order, sky_image)
     arrived = lax.all_to_all(out, "facet", split_axis=0, concat_axis=0, tiled=True)
-    table, phases, live, there, back, taps = kt(
-        subgrid_offsets, owner_order, row_kernel, column_kernel, visibility_count, visibility_cell
+    table, phases, live, there, back, taps, offsets, *edges = kt(
+        subgrid_offsets, owner_order, row_kernel, column_kernel, visibility_count,
+        visibility_cell, obs, wt,
     )
-    sub, sibling, neighbour = ka(arrived, obs, wt, there, phases)
+    edges = swapped(*edges)
+    sub, sibling, neighbour = ka(arrived, there, phases)
     sibling, neighbour = swapped(sibling, neighbour)
     res, outgoing = kb(
-        taps, sub, obs, wt, sibling, neighbour, back, table, phases, live
+        taps, sub, obs, wt, sibling, neighbour, back, table, phases, live, *edges
     )
     returned = lax.all_to_all(outgoing, "facet", split_axis=0, concat_axis=0, tiled=True)
-    dirty = k3(subgrid_offsets, owner_order, returned)
+    dirty = k3(offsets, returned)
     return (res[None], dirty)
 
 

time: 63.2 us -> 62.4 us (0.987)
  waiting for transfers between devices: 17.9 us -> 16.4 us
    all_to_all x1, waiting for transfers between devices: 15 us -> 13.8 us  [local(): lax.all_to_all(out, 'facet', split_axis=0, concat_axis=0, tiled=True)]
    ppermute x1 -> x2, waiting for transfers between devices: 2.23 us -> 2.01 us  [swapped(): lax.ppermute(neighbour, 'uv', far)]
  transfers between devices with their start and end apart: 3 -> 5, of which waited for: 3 -> 3; matrix products, arithmetic and copies ran while one was open for 0% -> 0% of each run, Pallas kernels for 3% -> 4%
where the time goes in v8:
time: 62.4 us; the launch traced here: 61.5 us
  blocking collectives  23 us (37%)
  waiting for transfers between devices  16.4 us (26%)
  starting transfers between devices  12.6 us (20%)
  Pallas kernels  7.39 us (12%)
  between operations  1.45 us (2%)
  local copies, waits for them, and re-layouts  0.67 us (1%)
    all_to_all x1, blocking collectives, local(): lax.all_to_all(outgoing, 'facet', split_axis=0, concat_axis=0, tiled=True)  23 us
    all_to_all x1, waiting for transfers between devices, local(): lax.all_to_all(out, 'facet', split_axis=0, concat_axis=0, tiled=True)  13.8 us
    all_to_all x1, starting transfers between devices, local(): lax.all_to_all(out, 'facet', split_axis=0, concat_axis=0, tiled=True)  11.3 us
    pallas_call x1, Pallas kernels, k1(): pl.pallas_call(k1_body, out_shape=jax.ShapeDtypeStruct((NF, CB, 2 * XC),...  2.42 us
    ppermute x2, waiting for transfers between devices, swapped(): lax.ppermute(neighbour, 'uv', far)  2.01 us
    pallas_call x1, Pallas kernels, kt(): pl.pallas_call(kt_body, out_shape=(jax.ShapeDtypeStruct((SG, VM), BF), ja...  1.85 us
    pallas_call x1, Pallas kernels, k3(): pl.pallas_call(k3_body, out_shape=jax.ShapeDtypeStruct((CB, FR), F32), in...  1.61 us
  transfers between devices with their start and end apart: 5, of which 3 were waited for; matrix products, arithmetic and copies ran while one was open for 0% of the time, Pallas kernels for 4%

profile of v8, /device:TPU:48, one launch (start us, length us, event | category | flops | bytes accessed | tf_op | source)
XLA Modules:
  0.0 61.5 jit_solution(9217337187600886213)
XLA Ops:
  0.6 2.4 %facet_to_slots.1 = bf16[32,32,256]{2,1,0:T(8,128)(2,1)} custom-call(s32[32]{0:T(128)} %offs_hbm.1, s32[32]{0:T(128)} %order_hbm.1, bf16[32,2048]{1,0:T(8,128)(2,1)} %sky_hbm.1), custom_call_target="tpu_custom_call" | custom-call | tf_op jit(solution)/shard_map/facet_to_slots/pallas_call | solution.py:222
  3.1 0.0 copy-start
  3.1 0.0 copy-start.1
  3.1 0.0 copy-start.3
  3.1 0.0 copy-start.9
  3.1 11.3 %all-to-all-start = ((bf16[32,32,256]{2,1,0:T(8,128)(2,1)}), bf16[32,32,256]{2,1,0:T(8,128)(2,1)S(1)}, u32[]{:S(2)}, u32[]{:S(2)}) async-start(bf16[32,32,256]{2,1,0:T(8,128)(2,1)} %facet_to_slots.1), calls=%async_computation | async-start | bytes 1048576 | tf_op jit(solution)/shard_map/all_to_all | solution.py:533
  15.1 0.0 copy-start.5
  15.1 0.0 copy-start.8
  15.2 0.6 copy-done.5
  15.8 0.0 copy-done.8
  15.8 1.9 %slot_tables.1 = (bf16[256,512]{1,0:T(8,128)(2,1)S(1)}, f32[2,32,128]{2,1,0:T(8,128)S(1)}, f32[1,512]{1,0:T(1,128)S(1)}, bf16[256,512]{1,0:T(8,128)(2,1)S(1)}, b...) custom-call(s32[32]{0:T(128)S(1)} %copy-done.6, ...), custom_call_target="tpu_custom_call" | custom-call | flops 4000000 | bytes 1000000 | tf_op jit(solution)/shard_map/slot_tables/pallas_call | solution.py:287
  17.7 0.1 collective-permute-start.2
  17.8 0.6 collective-permute-start.3
  18.3 13.8 %all-to-all-done.arr_ref = bf16[32,32,256]{2,1,0:T(8,128)(2,1)S(1)} async-done(((bf16[32,32,256]{2,1,0:T(8,128)(2,1)}), bf16[32,32,256]{2,1,0:T(8,128)(2,1)S(1)}, u32[]{:S(2)}, u32[]{:S(2)}) %all-to-all-start) | async-done | bytes 524320 | tf_op jit(solution)/shard_map/all_to_all | solution.py:533
  32.1 0.4 sum_facets.1
  32.5 0.1 collective-permute-start
  32.6 0.6 collective-permute-start.1
  33.2 0.6 collective-permute-done.sibling_ref
  33.8 2.0 %collective-permute-done.1.neighbour_ref = bf16[8,512]{1,0:T(8,128)(2,1)S(1)} collective-permute-done((bf16[8,512]{1,0:T(8,128)(2,1)S(1)}, bf16[8,512]{1,0:T(8,128)(2,1)S(1)}, u32[]{:S(2)}, u32[]{:S(2)}) %collective-permute-start.1) | collective-permute-done | bytes 8224 | tf_op jit(solution)/shard_map/ppermute | solution.py:522
  35.8 1.1 %slot_round_trip.1 = (f32[2,32,512]{2,1,0:T(8,128)}, bf16[32,32,256]{2,1,0:T(8,128)(2,1)S(1)}) custom-call(f32[8,256]{1,0:T(8,128)S(1)} %get-tuple-element.16.taps_ref, f32[32,512]{1,0:T(8,128)S(1)} %get-tuple-element.19.sub_ref, bf16[2,32,512]{2,1,0:T(8,128)(2,1)S(1)} %bitcast.4, f32[32,512]{1,0:T(8,128)S(1)} %bitcast.6, ...), custom_call_target="tpu_custom_call" | custom-call | tf_op jit(solution)/shard_map/slot_round_trip/pallas_call | solution.py:426
  36.9 0.0 copy-start.2
  36.9 0.0 copy-start.4
  36.9 23.0 %all_to_all.10.bp_ref = bf16[32,32,256]{2,1,0:T(8,128)(2,1)S(1)} all-to-all(bf16[32,32,256]{2,1,0:T(8,128)(2,1)S(1)} %get-tuple-element.29), channel_id=1, replica_groups=mesh['facet'=32,'uv'=8] {'facet'}, dimensions={0} | all-to-all | bytes 1048576 | tf_op jit(solution)/shard_map/all_to_all | solution.py:544
  59.9 1.6 %slots_to_facet.1 = f32[32,2048]{1,0:T(8,128)} custom-call(s32[8,128]{1,0:T(8,128)S(1)} %get-tuple-element.28.offset_ref, bf16[32,32,256]{2,1,0:T(8,128)(2,1)S(1)} %all_to_all.10.bp_ref, f32[1,2048]{1,0:T(1,128)S(1)} %copy-done.4, bf16[256,256]{1,0:T(8,128)(2,1)S(1)} %copy-done.2), custom_call_target="tpu_custom_call" | custom-call | tf_op jit(solution)/shard_map/slots_to_facet/pallas_call | solution.py:500
  (12 shorter events, 0.0 us)
Async XLA Ops:
  3.1 12.1 %copy-start = (bf16[1,2,32,512]{3,2,1,0:T(8,128)(2,1)S(1)}, bf16[1,2,32,512]{3,2,1,0:T(8,128)(2,1)}, u32[]{:S(2)}) copy-start(bf16[1,2,32,512]{3,2,1,0:T(8,128)(2,1)} %param.17) | copy-start | bytes 196612
  3.1 12.1 %copy-start.1 = (f32[1,32,512]{2,1,0:T(8,128)S(1)}, f32[1,32,512]{2,1,0:T(8,128)}, u32[]{:S(2)}) copy-start(f32[1,32,512]{2,1,0:T(8,128)} %param.18) | copy-start | bytes 196612
  3.1 12.1 %copy-start.3 = (f32[2,32,128]{2,1,0:T(8,128)S(1)}, f32[2,32,128]{2,1,0:T(8,128)}, u32[]{:S(2)}) copy-start(f32[2,32,128]{2,1,0:T(8,128)} %constant.6.clone.ph_ref) | copy-start | bytes 98308
  3.1 12.1 %copy-start.9 = (f32[7]{0:T(128)S(1)}, f32[7]{0:T(128)}, u32[]{:S(2)}) copy-start(f32[7]{0:T(128)} %ck_ref.1) | copy-start | bytes 88
  3.1 29.0 %all-to-all-start = ((bf16[32,32,256]{2,1,0:T(8,128)(2,1)}), bf16[32,32,256]{2,1,0:T(8,128)(2,1)S(1)}, u32[]{:S(2)}, u32[]{:S(2)}) async-start(bf16[32,32,256]{2,1,0:T(8,128)(2,1)} %facet_to_slots.1), calls=%async_computation | async-start | bytes 1048576 | tf_op jit(solution)/shard_map/all_to_all | solution.py:533
  15.1 0.7 %copy-start.5 = (s32[1,512]{1,0:T(1,128)S(1)}, s32[1,512]{1,0:T(1,128)}, u32[]{:S(2)}) copy-start(s32[1,512]{1,0:T(1,128)} %cell_ref.1) | copy-start | bytes 6148
  15.1 0.7 %copy-start.6 = (s32[32]{0:T(128)S(1)}, s32[32]{0:T(128)}, u32[]{:S(2)}) copy-start(s32[32]{0:T(128)} %offs_hbm.1) | copy-start | bytes 388
  15.1 0.7 %copy-start.7 = (s32[32]{0:T(128)S(1)}, s32[32]{0:T(128)}, u32[]{:S(2)}) copy-start(s32[32]{0:T(128)} %order_hbm.1) | copy-start | bytes 388
  15.1 0.7 %copy-start.8 = (f32[7]{0:T(128)S(1)}, f32[7]{0:T(128)}, u32[]{:S(2)}) copy-start(f32[7]{0:T(128)} %rk_ref.1) | copy-start | bytes 88
  17.7 15.5 %collective-permute-start.2 = (bf16[8,1536]{1,0:T(8,128)(2,1)S(1)}, bf16[8,1536]{1,0:T(8,128)(2,1)S(1)}, u32[]{:S(2)}, u32[]{:S(2)}) collective-permute-start(bf16[8,1536]{1,0:T(8,128)(2,1)S(1)} %get-tuple-element.25), channel_id=1, source_target_pairs={{0,1},{1,0},{2,3},{3,2},{4,5},{5,4},{6,7},{7,6},{8,9},{9,8},{10,11... | collective-permute-start | bytes 73736 | tf_op jit(solution)/shard_map/ppermute | solution.py:522
  17.8 15.4 %collective-permute-start.3 = (bf16[8,1536]{1,0:T(8,128)(2,1)S(1)}, bf16[8,1536]{1,0:T(8,128)(2,1)S(1)}, u32[]{:S(2)}, u32[]{:S(2)}) collective-permute-start(bf16[8,1536]{1,0:T(8,128)(2,1)S(1)} %get-tuple-element.26), channel_id=1, source_target_pairs={{0,7},{1,2},{2,1},{3,4},{4,3},{5,6},{6,5},{7,0},{8,15},{9,10},{10,... | collective-permute-start | bytes 73736 | tf_op jit(solution)/shard_map/ppermute | solution.py:522
  32.5 1.3 %collective-permute-start = (bf16[8,512]{1,0:T(8,128)(2,1)S(1)}, bf16[8,512]{1,0:T(8,128)(2,1)S(1)}, u32[]{:S(2)}, u32[]{:S(2)}) collective-permute-start(bf16[8,512]{1,0:T(8,128)(2,1)S(1)} %get-tuple-element.20), channel_id=1, source_target_pairs={{0,1},{1,0},{2,3},{3,2},{4,5},{5,4},{6,7},{7,6},{8,9},{9,8},{10,11... | collective-permute-start | bytes 24584 | tf_op jit(solution)/shard_map/ppermute | solution.py:522
  32.6 3.2 %collective-permute-start.1 = (bf16[8,512]{1,0:T(8,128)(2,1)S(1)}, bf16[8,512]{1,0:T(8,128)(2,1)S(1)}, u32[]{:S(2)}, u32[]{:S(2)}) collective-permute-start(bf16[8,512]{1,0:T(8,128)(2,1)S(1)} %get-tuple-element.21), channel_id=1, source_target_pairs={{0,7},{1,2},{2,1},{3,4},{4,3},{5,6},{6,5},{7,0},{8,15},{9,10},{10,... | collective-permute-start | bytes 24584 | tf_op jit(solution)/shard_map/ppermute | solution.py:522
  36.9 23.0 %copy-start.2 = (bf16[256,256]{1,0:T(8,128)(2,1)S(1)}, bf16[256,256]{1,0:T(8,128)(2,1)}, u32[]{:S(2)}) copy-start(bf16[256,256]{1,0:T(8,128)(2,1)} %constant.7.clone.tab_ref) | copy-start | bytes 393220
  36.9 23.0 %copy-start.4 = (f32[1,2048]{1,0:T(1,128)S(1)}, f32[1,2048]{1,0:T(1,128)}, u32[]{:S(2)}) copy-start(f32[1,2048]{1,0:T(1,128)} %constant.8.clone.win_ref) | copy-start | bytes 24580

commit v9 on v8

--- a/solution.py
+++ b/solution.py
@@ -305,15 +305,12 @@
     )(offs, order, rk, ck, count, cell, facet_phase(), obs, wt)
 
 
-def ka_body(
-    arr_ref, w_ref, pho_ref,
-    sub_ref, sibling_ref, neighbour_ref, u_ref,
-):
-    u = jnp.dot(arr_ref[...].reshape(NF * CB, 256), w_ref[...], preferred_element_type=F32)
-    u_ref[...] = u.reshape(NF, CB, 2 * SG)
+def facet_sum(arr, w_ref, pho_ref, u_ref, out_ref):
+    u = jnp.dot(arr.reshape(NF * 16, 256), w_ref[...], preferred_element_type=F32)
+    u_ref[...] = u.reshape(NF, 16, 2 * SG)
     for h in range(2):
-        re = jnp.zeros((CB, 128), F32)
-        im = jnp.zeros((CB, 128), F32)
+        re = jnp.zeros((16, 128), F32)
+        im = jnp.zeros((16, 128), F32)
         for f in range(NF):
             ur = u_ref[f, :, 128 * h : 128 * (h + 1)]
             ui = u_ref[f, :, SG + 128 * h : SG + 128 * (h + 1)]
@@ -321,94 +318,11 @@
             ps = pho_ref[1, f : f + 1, :]
             re = re + (ur * pc - ui * ps)
             im = im + (ur * ps + ui * pc)
-        sub_ref[:, 128 * h : 128 * (h + 1)] = re
-        sub_ref[:, SG + 128 * h : SG + 128 * (h + 1)] = im
-    even = lax.rem(lax.axis_index("uv"), 2) == 0
-    first, last = sub_ref[0:8, :], sub_ref[24:32, :]
-    sibling_ref[...] = jnp.where(even, last, first).astype(BF)
-    neighbour_ref[...] = jnp.where(even, first, last).astype(BF)
-
-
-EDGE = 3 * VM
-
-
-def ka(arrived, table, phases):
-    return pl.pallas_call(
-        ka_body,
-        out_shape=(
-            jax.ShapeDtypeStruct((CB, 2 * SG), F32),
-            jax.ShapeDtypeStruct((8, 2 * SG), BF),
-            jax.ShapeDtypeStruct((8, 2 * SG), BF),
-        ),
-        in_specs=[VMEM] * 3,
-        out_specs=(VMEM, VMEM, VMEM),
-        scratch_shapes=[pltpu.VMEM((NF, CB, 2 * SG), F32)],
-        compiler_params=PARAMS,
-        name="sum_facets",
-    )(arrived, table, phases)
-
-
-def kb_body(
-    taps_ref, sub_ref, obs_ref, wt_ref, sibling_ref, neighbour_ref, wt_tab_ref, dt_ref, pho_ref,
-    live_ref, sibling_vis_ref, neighbour_vis_ref,
-    res_hbm, out_ref, sub_ext_ref, conv_ref, res_ref, ext_ref, back_ref, y_ref, sem,
-):
-    uv = lax.axis_index("uv")
-    even = lax.rem(uv, 2) == 0
-    in_before, in_after = uv > 0, uv < 7
-
-    def sides(s, n):
-        s, n = s.astype(F32), n.astype(F32)
-        before = jnp.where(in_before, jnp.where(even, n, s), 0.0)
-        after = jnp.where(in_after, jnp.where(even, s, n), 0.0)
-        return before, after
-
-    before, after = sides(sibling_ref[...], neighbour_ref[...])
-    sub_ext_ref[8:16, :] = before
-    sub_ext_ref[16:48, :] = sub_ref[...]
-    sub_ext_ref[48:56, :] = after
-    for p in range(2):
-        lanes = slice(SG * p, SG * (p + 1))
-        own = jnp.zeros((CB, SG), F32)
-        lo = jnp.zeros((8, SG), F32)
-        hi = jnp.zeros((8, SG), F32)
-        for t in range(TAPS):
-            k = taps_ref[t : t + 1, :]
-            own = own + k * sub_ext_ref[13 + t : 45 + t, lanes]
-            lo = lo + k * sub_ext_ref[5 + t : 13 + t, lanes]
-            hi = hi + k * sub_ext_ref[45 + t : 53 + t, lanes]
-        conv_ref[p * CE : p * CE + CB, :] = own
-        conv_ref[p * CE + CB : (p + 1) * CE, :] = halo_rows(hi, lo, 0)
-    model = jnp.dot(conv_ref[...].astype(BF), dt_ref[...], preferred_element_type=F32)
-
-    live = live_ref[...]
-    wt = wt_ref[...] * live
-    cols = slice(2 * VM, EDGE)
-    before, after = sides(sibling_vis_ref[:, cols], neighbour_vis_ref[:, cols])
-    wt_h = halo_rows(after, before, 0) * live
-    parts = []
-    for p in range(2):
-        own = wt * (obs_ref[p].astype(F32) - model[p * CE : p * CE + CB])
-        res_ref[p] = own
-        cols = slice(p * VM, (p + 1) * VM)
-        before, after = sides(sibling_vis_ref[:, cols], neighbour_vis_ref[:, cols])
-        obs_h = halo_rows(after, before, 0)
-        parts += [own, wt_h * (obs_h - model[p * CE + CB : (p + 1) * CE])]
-    copy = pltpu.make_async_copy(res_ref, res_hbm, sem)
-    copy.start()
-    rr = jnp.concatenate(parts, axis=0).astype(BF)
-    gridded = lax.dot_general(
-        rr, dt_ref[...], (((1,), (1,)), ((), ())), preferred_element_type=F32
-    )
-    for p in range(2):
-        halo = gridded[p * CE + CB : (p + 1) * CE]
-        ext_ref[p, 0:8, :] = halo
-        ext_ref[p, 8:40, :] = gridded[p * CE : p * CE + CB]
-        ext_ref[p, 40:48, :] = halo
-        b = jnp.zeros((CB, SG), F32)
-        for t in range(TAPS):
-            b = b + taps_ref[t : t + 1, :] * ext_ref[p, 11 - t : 43 - t, :]
-        back_ref[p] = b
+        out_ref[:, 128 * h : 128 * (h + 1)] = re
+        out_ref[:, SG + 128 * h : SG + 128 * (h + 1)] = im
+
+
+def project(back_ref, pho_ref, table_ref, y_ref):
     for h in range(2):
         lanes = slice(128 * h, 128 * (h + 1))
         xr, xi = back_ref[0, :, lanes], back_ref[1, :, lanes]
@@ -417,34 +331,194 @@
             ps = pho_ref[1, f : f + 1, :]
             y_ref[f, :, lanes] = (xr * pc + xi * ps).astype(BF)
             y_ref[f, :, SG + 128 * h : SG + 128 * (h + 1)] = (xi * pc - xr * ps).astype(BF)
-    z = jnp.dot(y_ref[...].reshape(NF * CB, 2 * SG), wt_tab_ref[...], preferred_element_type=F32)
-    out_ref[...] = z.astype(BF).reshape(NF, CB, 2 * XC)
-    copy.wait()
-
-
-def kb(taps, sub, obs, wt, sibling, neighbour, back, table, phases, live, *edges):
+    z = jnp.dot(y_ref[...].reshape(NF * 16, 2 * SG), table_ref[...], preferred_element_type=F32)
+    return z.astype(BF).reshape(NF, 16, 2 * XC)
+
+
+def ka_body(arr_ref, w_ref, pho_ref, edge_ref, sibling_ref, neighbour_ref, u_ref):
+    arr = jnp.concatenate([arr_ref[:, 0:8, :], arr_ref[:, 24:32, :]], axis=1)
+    facet_sum(arr, w_ref, pho_ref, u_ref, edge_ref)
+    even = lax.rem(lax.axis_index("uv"), 2) == 0
+    first, last = edge_ref[0:8, :], edge_ref[8:16, :]
+    sibling_ref[...] = jnp.where(even, last, first).astype(BF)
+    neighbour_ref[...] = jnp.where(even, first, last).astype(BF)
+
+
+EDGE = 3 * VM
+
+
+def ka(arrived, table, phases):
+    return pl.pallas_call(
+        ka_body,
+        out_shape=(
+            jax.ShapeDtypeStruct((16, 2 * SG), F32),
+            jax.ShapeDtypeStruct((8, 2 * SG), BF),
+            jax.ShapeDtypeStruct((8, 2 * SG), BF),
+        ),
+        in_specs=[VMEM] * 3,
+        out_specs=(VMEM, VMEM, VMEM),
+        scratch_shapes=[pltpu.VMEM((NF, 16, 2 * SG), F32)],
+        compiler_params=PARAMS,
+        name="sum_edges",
+    )(arrived, table, phases)
+
+
+def sides(s, n):
+    uv = lax.axis_index("uv")
+    even = lax.rem(uv, 2) == 0
+    s, n = s.astype(F32), n.astype(F32)
+    before = jnp.where(uv > 0, jnp.where(even, n, s), 0.0)
+    after = jnp.where(uv < 7, jnp.where(even, s, n), 0.0)
+    return before, after
+
+
+def km_body(
+    arr_ref, w_ref, pho_ref, edge_ref, taps_ref, dt_ref, live_ref, obs_ref, wt_ref, back_tab_ref,
+    sibling_vis_ref, neighbour_vis_ref,
+    mid_ref, vis_ref, res_ref, out_ref, u_ref, s_ref, c_ref, g_ref, back_ref, y_ref, v_ref,
+):
+    facet_sum(arr_ref[:, 8:24, :], w_ref, pho_ref, u_ref, mid_ref)
+    s_ref[0:8, :] = jnp.zeros((8, 2 * SG), F32)
+    s_ref[8:16, :] = edge_ref[0:8, :]
+    s_ref[16:32, :] = mid_ref[...]
+    s_ref[32:40, :] = edge_ref[8:16, :]
+    s_ref[40:48, :] = jnp.zeros((8, 2 * SG), F32)
+    for p in range(2):
+        c = jnp.zeros((CB, SG), F32)
+        for t in range(TAPS):
+            c = c + taps_ref[t : t + 1, :] * s_ref[5 + t : 37 + t, SG * p : SG * (p + 1)]
+        c_ref[p * CB : (p + 1) * CB, :] = c
+    model = jnp.dot(c_ref[...].astype(BF), dt_ref[...], preferred_element_type=F32)
+    wt = wt_ref[...] * live_ref[...]
+    parts = []
+    for p in range(2):
+        r = wt * (obs_ref[p].astype(F32) - model[p * CB : (p + 1) * CB])
+        res_ref[p] = r[8:24]
+        parts.append(r)
+    rr = jnp.concatenate(parts, axis=0).astype(BF)
+    g_ref[...] = lax.dot_general(
+        rr, dt_ref[...], (((1,), (1,)), ((), ())), preferred_element_type=F32
+    )
+    for p in range(2):
+        b = jnp.zeros((16, SG), F32)
+        for t in range(TAPS):
+            first = p * CB + 11 - t
+            b = b + taps_ref[t : t + 1, :] * g_ref[first : first + 16, :]
+        back_ref[p] = b
+    out_ref[...] = project(back_ref, pho_ref, back_tab_ref, y_ref)
+    for p in range(3):
+        cols = slice(p * VM, (p + 1) * VM)
+        before, after = sides(sibling_vis_ref[:, cols], neighbour_vis_ref[:, cols])
+        own = obs_ref[p].astype(F32) if p < 2 else wt
+        if p == 2:
+            before, after = before * live_ref[...], after * live_ref[...]
+        v_ref[0:8, :] = before
+        v_ref[8:40, :] = own
+        v_ref[40:48, :] = after
+        vis_ref[p, 0:16, :] = v_ref[4:20, :]
+        vis_ref[p, 16:32, :] = v_ref[28:44, :]
+
+
+def km(arrived, table, phases, edge, taps, grid, live, obs, wt, back, *vis):
+    return pl.pallas_call(
+        km_body,
+        out_shape=(
+            jax.ShapeDtypeStruct((16, 2 * SG), F32),
+            jax.ShapeDtypeStruct((3, 32, VM), F32),
+            jax.ShapeDtypeStruct((2, 16, VM), F32),
+            jax.ShapeDtypeStruct((NF, 16, 2 * XC), BF),
+        ),
+        in_specs=[VMEM] * 12,
+        out_specs=(VMEM,) * 4,
+        scratch_shapes=[
+            pltpu.VMEM((NF, 16, 2 * SG), F32),
+            pltpu.VMEM((48, 2 * SG), F32),
+            pltpu.VMEM((2 * CB, SG), F32),
+            pltpu.VMEM((2 * CB, SG), F32),
+            pltpu.VMEM((2, 16, SG), F32),
+            pltpu.VMEM((NF, 16, 2 * SG), BF),
+            pltpu.VMEM((48, VM), F32),
+        ],
+        compiler_params=PARAMS,
+        cost_estimate=pl.CostEstimate(flops=300000000, bytes_accessed=2000000, transcendentals=0),
+        name="inner_columns",
+    )(arrived, table, phases, edge, taps, grid, live, obs, wt, back, *vis)
+
+
+def kb_body(
+    taps_ref, edge_ref, mid_ref, vis_ref, sibling_ref, neighbour_ref, back_tab_ref, dt_ref,
+    pho_ref, res_mid_ref, out_mid_ref,
+    res_hbm, out_ref, s_ref, c_ref, g_ref, res_ref, back_ref, y_ref, sem,
+):
+    middle = pltpu.make_async_copy(res_mid_ref, res_hbm.at[:, pl.ds(8, 16), :], sem.at[0])
+    middle.start()
+    before, after = sides(sibling_ref[...], neighbour_ref[...])
+    s_ref[0, 0:8, :] = before
+    s_ref[0, 8:16, :] = edge_ref[0:8, :]
+    s_ref[0, 16:24, :] = mid_ref[0:8, :]
+    s_ref[1, 0:8, :] = mid_ref[8:16, :]
+    s_ref[1, 8:16, :] = edge_ref[8:16, :]
+    s_ref[1, 16:24, :] = after
+    for p in range(2):
+        for side in range(2):
+            c = jnp.zeros((16, SG), F32)
+            for t in range(TAPS):
+                c = c + taps_ref[t : t + 1, :] * s_ref[side, 1 + t : 17 + t, SG * p : SG * (p + 1)]
+            c_ref[32 * p + 16 * side : 32 * p + 16 * (side + 1), :] = c
+    model = jnp.dot(c_ref[...].astype(BF), dt_ref[...], preferred_element_type=F32)
+    parts = []
+    for p in range(2):
+        r = vis_ref[2] * (vis_ref[p] - model[32 * p : 32 * (p + 1)])
+        res_ref[0, p] = r[4:12]
+        res_ref[1, p] = r[20:28]
+        parts.append(r)
+    copies = [middle]
+    for side in range(2):
+        copy = pltpu.make_async_copy(
+            res_ref.at[side], res_hbm.at[:, pl.ds(24 * side, 8), :], sem.at[1 + side]
+        )
+        copy.start()
+        copies.append(copy)
+    rr = jnp.concatenate(parts, axis=0).astype(BF)
+    g_ref[...] = lax.dot_general(
+        rr, dt_ref[...], (((1,), (1,)), ((), ())), preferred_element_type=F32
+    )
+    for p in range(2):
+        for side in range(2):
+            b = jnp.zeros((8, SG), F32)
+            for t in range(TAPS):
+                first = 32 * p + 16 * side + 7 - t
+                b = b + taps_ref[t : t + 1, :] * g_ref[first : first + 8, :]
+            back_ref[p, 8 * side : 8 * (side + 1), :] = b
+    out_ref[:, 8:24, :] = out_mid_ref[...]
+    z = project(back_ref, pho_ref, back_tab_ref, y_ref)
+    out_ref[:, 0:8, :] = z[:, 0:8, :]
+    out_ref[:, 24:32, :] = z[:, 8:16, :]
+    for copy in copies:
+        copy.wait()
+
+
+def kb(taps, edge, mid, vis, sibling, neighbour, back, grid, phases, res_mid, out_mid):
     return pl.pallas_call(
         kb_body,
         out_shape=(
             jax.ShapeDtypeStruct((2, CB, VM), F32),
             jax.ShapeDtypeStruct((NF, CB, 2 * XC), BF),
         ),
-        in_specs=[VMEM] * 12,
+        in_specs=[VMEM] * 11,
         out_specs=(ANY, VMEM),
         scratch_shapes=[
-            pltpu.VMEM((64, 2 * SG), F32),
-            pltpu.VMEM((2 * CE, SG), F32),
-            pltpu.VMEM((2, CB, VM), F32),
-            pltpu.VMEM((2, 48, SG), F32),
-            pltpu.VMEM((2, CB, SG), F32),
-            pltpu.VMEM((NF, CB, 2 * SG), BF),
-            pltpu.SemaphoreType.DMA,
+            pltpu.VMEM((2, 24, 2 * SG), F32),
+            pltpu.VMEM((64, SG), F32),
+            pltpu.VMEM((64, SG), F32),
+            pltpu.VMEM((2, 2, 8, VM), F32),
+            pltpu.VMEM((2, 16, SG), F32),
+            pltpu.VMEM((NF, 16, 2 * SG), BF),
+            pltpu.SemaphoreType.DMA((3,)),
         ],
         compiler_params=PARAMS,
-        name="slot_round_trip",
-    )(
-        taps, sub, obs, wt, sibling, neighbour, back, table, phases, live, *edges
-    )
+        name="edge_columns",
+    )(taps, edge, mid, vis, sibling, neighbour, back, grid, phases, res_mid, out_mid)
 
 
 def k3_body(
@@ -536,10 +610,13 @@
         visibility_cell, obs, wt,
     )
     edges = swapped(*edges)
-    sub, sibling, neighbour = ka(arrived, there, phases)
+    edge, sibling, neighbour = ka(arrived, there, phases)
     sibling, neighbour = swapped(sibling, neighbour)
+    mid, vis, res_mid, out_mid = km(
+        arrived, there, phases, edge, taps, table, live, obs, wt, back, *edges
+    )
     res, outgoing = kb(
-        taps, sub, obs, wt, sibling, neighbour, back, table, phases, live, *edges
+        taps, edge, mid, vis, sibling, neighbour, back, table, phases, res_mid, out_mid
     )
     returned = lax.all_to_all(outgoing, "facet", split_axis=0, concat_axis=0, tiled=True)
     dirty = k3(offsets, returned)

time: 62.4 us -> 62.4 us (level)
  waiting for transfers between devices: 16.4 us -> 15.1 us
  Pallas kernels: 7.39 us -> 8.53 us
    pallas_call x1 -> x2, Pallas kernels: 0.43 us -> 1.52 us  [the longest x1 1.22 us: km(): pl.pallas_call(km_body, out_shape=(jax.ShapeDtypeStruct((16, 2 * SG), F32...]
    ppermute x2, waiting for transfers between devices: 2.01 us -> 1.37 us  [swapped(): lax.ppermute(neighbour, 'uv', far)]
  transfers between devices with their start and end apart: 5 -> 5, of which waited for: 3 -> 2; matrix products, arithmetic and copies ran while one was open for 0% -> 0% of each run, Pallas kernels for 4% -> 5%
where the time goes in v9:
time: 62.4 us; the launch traced here: 61.4 us
  blocking collectives  23 us (37%)
  waiting for transfers between devices  15.1 us (24%)
  starting transfers between devices  12.6 us (20%)
  Pallas kernels  8.53 us (14%)
  between operations  1.46 us (2%)
  local copies, waits for them, and re-layouts  0.67 us (1%)
    all_to_all x1, blocking collectives, local(): lax.all_to_all(outgoing, 'facet', split_axis=0, concat_axis=0, tiled=True)  23 us
    all_to_all x1, waiting for transfers between devices, local(): lax.all_to_all(out, 'facet', split_axis=0, concat_axis=0, tiled=True)  13.8 us
    all_to_all x1, starting transfers between devices, local(): lax.all_to_all(out, 'facet', split_axis=0, concat_axis=0, tiled=True)  11.3 us
    pallas_call x1, Pallas kernels, k1(): pl.pallas_call(k1_body, out_shape=jax.ShapeDtypeStruct((NF, CB, 2 * XC),...  2.41 us
    pallas_call x1, Pallas kernels, kt(): pl.pallas_call(kt_body, out_shape=(jax.ShapeDtypeStruct((SG, VM), BF), ja...  1.85 us
    pallas_call x1, Pallas kernels, k3(): pl.pallas_call(k3_body, out_shape=jax.ShapeDtypeStruct((CB, FR), F32), in...  1.61 us
    ppermute x2, waiting for transfers between devices, swapped(): lax.ppermute(neighbour, 'uv', far)  1.37 us
  transfers between devices with their start and end apart: 5, of which 2 were waited for; matrix products, arithmetic and copies ran while one was open for 0% of the time, Pallas kernels for 5%

profile of v9, /device:TPU:48, one launch (start us, length us, event | category | flops | bytes accessed | tf_op | source)
XLA Modules:
  0.0 61.4 jit_solution(1660852834794112372)
XLA Ops:
  0.6 2.4 %facet_to_slots.1 = bf16[32,32,256]{2,1,0:T(8,128)(2,1)} custom-call(s32[32]{0:T(128)} %offs_hbm.1, s32[32]{0:T(128)} %order_hbm.1, bf16[32,2048]{1,0:T(8,128)(2,1)} %sky_hbm.1), custom_call_target="tpu_custom_call" | custom-call | tf_op jit(solution)/shard_map/facet_to_slots/pallas_call | solution.py:222
  3.0 0.0 copy-start
  3.1 0.0 copy-start.1
  3.1 0.0 copy-start.3
  3.1 0.0 copy-start.9
  3.1 11.3 %all-to-all-start = ((bf16[32,32,256]{2,1,0:T(8,128)(2,1)}), bf16[32,32,256]{2,1,0:T(8,128)(2,1)S(1)}, u32[]{:S(2)}, u32[]{:S(2)}) async-start(bf16[32,32,256]{2,1,0:T(8,128)(2,1)} %facet_to_slots.1), calls=%async_computation | async-start | bytes 1048576 | tf_op jit(solution)/shard_map/all_to_all | solution.py:607
  15.1 0.0 copy-start.7
  15.1 0.0 copy-start.8
  15.2 0.6 copy-done.5
  15.8 0.0 copy-done.8
  15.8 1.9 %slot_tables.1 = (bf16[256,512]{1,0:T(8,128)(2,1)S(1)}, f32[2,32,128]{2,1,0:T(8,128)S(1)}, f32[1,512]{1,0:T(1,128)S(1)}, bf16[256,512]{1,0:T(8,128)(2,1)S(1)}, b...) custom-call(s32[32]{0:T(128)S(1)} %copy-done.6, ...), custom_call_target="tpu_custom_call" | custom-call | flops 4000000 | bytes 1000000 | tf_op jit(solution)/shard_map/slot_tables/pallas_call | solution.py:287
  17.6 0.1 collective-permute-start
  17.7 0.6 collective-permute-start.1
  18.3 13.8 %all-to-all-done.arr_ref = bf16[32,32,256]{2,1,0:T(8,128)(2,1)S(1)} async-done(((bf16[32,32,256]{2,1,0:T(8,128)(2,1)}), bf16[32,32,256]{2,1,0:T(8,128)(2,1)S(1)}, u32[]{:S(2)}, u32[]{:S(2)}) %all-to-all-start) | async-done | bytes 524320 | tf_op jit(solution)/shard_map/all_to_all | solution.py:607
  32.1 0.3 sum_edges.1
  32.4 0.1 collective-permute-start.2
  32.5 0.6 collective-permute-start.3
  33.0 1.2 %inner_columns.1 = (f32[16,512]{1,0:T(8,128)S(1)}, f32[3,32,512]{2,1,0:T(8,128)S(1)}, f32[2,16,512]{2,1,0:T(8,128)S(1)}, bf16[32,16,256]{2,1,0:T(8,128)(2,1)S(1)}) custom-call(bf16[32,32,256]{2,1,0:T(8,128)(2,1)S(1)} %all-to-all-done.arr_ref, bf16[256,512]{1,0:T(8,128)(2,1)S(1)} %get-tuple-element.21.w_ref, f32[2,32,128]{2,1,0:T(8,128)S(1)} %get-tuple-element.22.pho_ref, ...), custom_call_target="tpu_custom_call" | custom-call | flops 300000000 | bytes 2000000 | tf_op jit(solution)/shard_map/inner_columns/pallas_call | solution.py:423
  34.3 1.4 %collective-permute-done.3.neighbour_ref = bf16[8,512]{1,0:T(8,128)(2,1)S(1)} collective-permute-done((bf16[8,512]{1,0:T(8,128)(2,1)S(1)}, bf16[8,512]{1,0:T(8,128)(2,1)S(1)}, u32[]{:S(2)}, u32[]{:S(2)}) %collective-permute-start.3) | collective-permute-done | bytes 8224 | tf_op jit(solution)/shard_map/ppermute | solution.py:596
  35.6 1.1 %edge_columns.1 = (f32[2,32,512]{2,1,0:T(8,128)}, bf16[32,32,256]{2,1,0:T(8,128)(2,1)S(1)}) custom-call(f32[8,256]{1,0:T(8,128)S(1)} %get-tuple-element.20.taps_ref, f32[16,512]{1,0:T(8,128)S(1)} %get-tuple-element.23.edge_ref, f32[16,512]{1,0:T(8,128)S(1)} %get-tuple-element.29.mid_ref, f32[3,32,512]{2,1,0:T(8,128)S(1)} %get-tuple-element.30.vis_ref, ...), custom_call_target="tpu_custom_call" | custom-call | tf_op jit(solution)/shard_map/edge_columns/pallas_call | solution.py:502
  36.8 0.0 copy-start.2
  36.8 0.0 copy-start.4
  36.8 23.0 %all_to_all.10.bp_ref = bf16[32,32,256]{2,1,0:T(8,128)(2,1)S(1)} all-to-all(bf16[32,32,256]{2,1,0:T(8,128)(2,1)S(1)} %get-tuple-element.37), channel_id=1, replica_groups=mesh['facet'=32,'uv'=8] {'facet'}, dimensions={0} | all-to-all | bytes 1048576 | tf_op jit(solution)/shard_map/all_to_all | solution.py:621
  59.8 1.6 %slots_to_facet.1 = f32[32,2048]{1,0:T(8,128)} custom-call(s32[8,128]{1,0:T(8,128)S(1)} %get-tuple-element.36.offset_ref, bf16[32,32,256]{2,1,0:T(8,128)(2,1)S(1)} %all_to_all.10.bp_ref, f32[1,2048]{1,0:T(1,128)S(1)} %copy-done.4, bf16[256,256]{1,0:T(8,128)(2,1)S(1)} %copy-done.2), custom_call_target="tpu_custom_call" | custom-call | tf_op jit(solution)/shard_map/slots_to_facet/pallas_call | solution.py:574
  (13 shorter events, 0.0 us)
Async XLA Ops:
  3.0 12.1 %copy-start = (bf16[1,2,32,512]{3,2,1,0:T(8,128)(2,1)S(1)}, bf16[1,2,32,512]{3,2,1,0:T(8,128)(2,1)}, u32[]{:S(2)}) copy-start(bf16[1,2,32,512]{3,2,1,0:T(8,128)(2,1)} %param.17) | copy-start | bytes 196612
  3.1 12.1 %copy-start.1 = (f32[1,32,512]{2,1,0:T(8,128)S(1)}, f32[1,32,512]{2,1,0:T(8,128)}, u32[]{:S(2)}) copy-start(f32[1,32,512]{2,1,0:T(8,128)} %param.18) | copy-start | bytes 196612
  3.1 12.1 %copy-start.3 = (f32[2,32,128]{2,1,0:T(8,128)S(1)}, f32[2,32,128]{2,1,0:T(8,128)}, u32[]{:S(2)}) copy-start(f32[2,32,128]{2,1,0:T(8,128)} %constant.6.clone.ph_ref) | copy-start | bytes 98308
  3.1 12.1 %copy-start.9 = (f32[7]{0:T(128)S(1)}, f32[7]{0:T(128)}, u32[]{:S(2)}) copy-start(f32[7]{0:T(128)} %ck_ref.1) | copy-start | bytes 88
  3.1 29.0 %all-to-all-start = ((bf16[32,32,256]{2,1,0:T(8,128)(2,1)}), bf16[32,32,256]{2,1,0:T(8,128)(2,1)S(1)}, u32[]{:S(2)}, u32[]{:S(2)}) async-start(bf16[32,32,256]{2,1,0:T(8,128)(2,1)} %facet_to_slots.1), calls=%async_computation | async-start | bytes 1048576 | tf_op jit(solution)/shard_map/all_to_all | solution.py:607
  15.1 0.7 %copy-start.5 = (s32[1,512]{1,0:T(1,128)S(1)}, s32[1,512]{1,0:T(1,128)}, u32[]{:S(2)}) copy-start(s32[1,512]{1,0:T(1,128)} %cell_ref.1) | copy-start | bytes 6148
  15.1 0.7 %copy-start.6 = (s32[32]{0:T(128)S(1)}, s32[32]{0:T(128)}, u32[]{:S(2)}) copy-start(s32[32]{0:T(128)} %offs_hbm.1) | copy-start | bytes 388
  15.1 0.7 %copy-start.7 = (s32[32]{0:T(128)S(1)}, s32[32]{0:T(128)}, u32[]{:S(2)}) copy-start(s32[32]{0:T(128)} %order_hbm.1) | copy-start | bytes 388
  15.1 0.7 %copy-start.8 = (f32[7]{0:T(128)S(1)}, f32[7]{0:T(128)}, u32[]{:S(2)}) copy-start(f32[7]{0:T(128)} %rk_ref.1) | copy-start | bytes 88
  17.6 15.4 %collective-permute-start = (bf16[8,1536]{1,0:T(8,128)(2,1)S(1)}, bf16[8,1536]{1,0:T(8,128)(2,1)S(1)}, u32[]{:S(2)}, u32[]{:S(2)}) collective-permute-start(bf16[8,1536]{1,0:T(8,128)(2,1)S(1)} %get-tuple-element.27), channel_id=1, source_target_pairs={{0,1},{1,0},{2,3},{3,2},{4,5},{5,4},{6,7},{7,6},{8,9},{9,8},{10,11... | collective-permute-start | bytes 73736 | tf_op jit(solution)/shard_map/ppermute | solution.py:596
  17.7 15.3 %collective-permute-start.1 = (bf16[8,1536]{1,0:T(8,128)(2,1)S(1)}, bf16[8,1536]{1,0:T(8,128)(2,1)S(1)}, u32[]{:S(2)}, u32[]{:S(2)}) collective-permute-start(bf16[8,1536]{1,0:T(8,128)(2,1)S(1)} %get-tuple-element.28), channel_id=1, source_target_pairs={{0,7},{1,2},{2,1},{3,4},{4,3},{5,6},{6,5},{7,0},{8,15},{9,10},{10,... | collective-permute-start | bytes 73736 | tf_op jit(solution)/shard_map/ppermute | solution.py:596
  32.4 1.9 %collective-permute-start.2 = (bf16[8,512]{1,0:T(8,128)(2,1)S(1)}, bf16[8,512]{1,0:T(8,128)(2,1)S(1)}, u32[]{:S(2)}, u32[]{:S(2)}) collective-permute-start(bf16[8,512]{1,0:T(8,128)(2,1)S(1)} %get-tuple-element.31), channel_id=1, source_target_pairs={{0,1},{1,0},{2,3},{3,2},{4,5},{5,4},{6,7},{7,6},{8,9},{9,8},{10,11... | collective-permute-start | bytes 24584 | tf_op jit(solution)/shard_map/ppermute | solution.py:596
  32.5 3.2 %collective-permute-start.3 = (bf16[8,512]{1,0:T(8,128)(2,1)S(1)}, bf16[8,512]{1,0:T(8,128)(2,1)S(1)}, u32[]{:S(2)}, u32[]{:S(2)}) collective-permute-start(bf16[8,512]{1,0:T(8,128)(2,1)S(1)} %get-tuple-element.32), channel_id=1, source_target_pairs={{0,7},{1,2},{2,1},{3,4},{4,3},{5,6},{6,5},{7,0},{8,15},{9,10},{10,... | collective-permute-start | bytes 24584 | tf_op jit(solution)/shard_map/ppermute | solution.py:596
  36.8 23.0 %copy-start.2 = (bf16[256,256]{1,0:T(8,128)(2,1)S(1)}, bf16[256,256]{1,0:T(8,128)(2,1)}, u32[]{:S(2)}) copy-start(bf16[256,256]{1,0:T(8,128)(2,1)} %constant.7.clone.tab_ref) | copy-start | bytes 393220
  36.8 23.0 %copy-start.4 = (f32[1,2048]{1,0:T(1,128)S(1)}, f32[1,2048]{1,0:T(1,128)}, u32[]{:S(2)}) copy-start(f32[1,2048]{1,0:T(1,128)} %constant.8.clone.win_ref) | copy-start | bytes 24580

commit v10 on v9

--- a/solution.py
+++ b/solution.py
@@ -447,11 +447,9 @@
 
 def kb_body(
     taps_ref, edge_ref, mid_ref, vis_ref, sibling_ref, neighbour_ref, back_tab_ref, dt_ref,
-    pho_ref, res_mid_ref, out_mid_ref,
-    res_hbm, out_ref, s_ref, c_ref, g_ref, res_ref, back_ref, y_ref, sem,
+    pho_ref, out_mid_ref,
+    res_ref, out_ref, s_ref, c_ref, g_ref, back_ref, y_ref,
 ):
-    middle = pltpu.make_async_copy(res_mid_ref, res_hbm.at[:, pl.ds(8, 16), :], sem.at[0])
-    middle.start()
     before, after = sides(sibling_ref[...], neighbour_ref[...])
     s_ref[0, 0:8, :] = before
     s_ref[0, 8:16, :] = edge_ref[0:8, :]
@@ -472,13 +470,6 @@
         res_ref[0, p] = r[4:12]
         res_ref[1, p] = r[20:28]
         parts.append(r)
-    copies = [middle]
-    for side in range(2):
-        copy = pltpu.make_async_copy(
-            res_ref.at[side], res_hbm.at[:, pl.ds(24 * side, 8), :], sem.at[1 + side]
-        )
-        copy.start()
-        copies.append(copy)
     rr = jnp.concatenate(parts, axis=0).astype(BF)
     g_ref[...] = lax.dot_general(
         rr, dt_ref[...], (((1,), (1,)), ((), ())), preferred_element_type=F32
@@ -494,37 +485,39 @@
     z = project(back_ref, pho_ref, back_tab_ref, y_ref)
     out_ref[:, 0:8, :] = z[:, 0:8, :]
     out_ref[:, 24:32, :] = z[:, 8:16, :]
-    for copy in copies:
-        copy.wait()
-
-
-def kb(taps, edge, mid, vis, sibling, neighbour, back, grid, phases, res_mid, out_mid):
+
+
+def kb(taps, edge, mid, vis, sibling, neighbour, back, grid, phases, out_mid):
     return pl.pallas_call(
         kb_body,
         out_shape=(
-            jax.ShapeDtypeStruct((2, CB, VM), F32),
+            jax.ShapeDtypeStruct((2, 2, 8, VM), F32),
             jax.ShapeDtypeStruct((NF, CB, 2 * XC), BF),
         ),
-        in_specs=[VMEM] * 11,
-        out_specs=(ANY, VMEM),
+        in_specs=[VMEM] * 10,
+        out_specs=(VMEM, VMEM),
         scratch_shapes=[
             pltpu.VMEM((2, 24, 2 * SG), F32),
             pltpu.VMEM((64, SG), F32),
             pltpu.VMEM((64, SG), F32),
-            pltpu.VMEM((2, 2, 8, VM), F32),
             pltpu.VMEM((2, 16, SG), F32),
             pltpu.VMEM((NF, 16, 2 * SG), BF),
-            pltpu.SemaphoreType.DMA((3,)),
         ],
         compiler_params=PARAMS,
         name="edge_columns",
-    )(taps, edge, mid, vis, sibling, neighbour, back, grid, phases, res_mid, out_mid)
+    )(taps, edge, mid, vis, sibling, neighbour, back, grid, phases, out_mid)
 
 
 def k3_body(
-    offset_ref, bp_ref, win_ref, tab_ref,
-    out_hbm, nat_ref, tw_ref, lhs_ref, v_ref, out_ref, sem,
+    offset_ref, bp_ref, win_ref, tab_ref, res_edge_ref, res_mid_ref,
+    res_hbm, out_hbm, nat_ref, tw_ref, lhs_ref, v_ref, out_ref, res_sem, sem,
 ):
+    done = [pltpu.make_async_copy(res_mid_ref, res_hbm.at[:, pl.ds(8, 16), :], res_sem.at[2])]
+    for side in range(2):
+        part = res_hbm.at[:, pl.ds(24 * side, 8), :]
+        done.append(pltpu.make_async_copy(res_edge_ref.at[side], part, res_sem.at[side]))
+    for copy in done:
+        copy.start()
     offsets = offset_ref[...]
     tw_ref[0], tw_ref[1] = twiddles(lax.axis_index("facet"))
     nat_ref[...] = jnp.zeros_like(nat_ref)
@@ -549,7 +542,6 @@
                 lhs_ref[m, rows, cols] = x[m]
     v = jnp.dot(lhs_ref[...].reshape(16 * CB, 256), tab_ref[...], preferred_element_type=F32)
     v_ref[...] = v.reshape(16, CB, 256)
-    done = []
     for g in range(4):
         rows = slice(8 * g, 8 * (g + 1))
         t = []
@@ -570,23 +562,27 @@
         copy.wait()
 
 
-def k3(offsets, bp):
+def k3(offsets, bp, res_edge, res_mid):
     return pl.pallas_call(
         k3_body,
-        out_shape=jax.ShapeDtypeStruct((CB, FR), F32),
-        in_specs=[VMEM] * 4,
-        out_specs=ANY,
+        out_shape=(
+            jax.ShapeDtypeStruct((2, CB, VM), F32),
+            jax.ShapeDtypeStruct((CB, FR), F32),
+        ),
+        in_specs=[VMEM] * 6,
+        out_specs=(ANY, ANY),
         scratch_shapes=[
             pltpu.VMEM((17, CB, 256), F32),
             pltpu.VMEM((2, 16, 128), F32),
             pltpu.VMEM((16, CB, 256), BF),
             pltpu.VMEM((16, CB, 256), F32),
             pltpu.VMEM((CB, FR), F32),
+            pltpu.SemaphoreType.DMA((3,)),
             pltpu.SemaphoreType.DMA((4,)),
         ],
         compiler_params=PARAMS,
         name="slots_to_facet",
-    )(offsets, bp, window(), jnp.asarray(block_table().T, BF))
+    )(offsets, bp, window(), jnp.asarray(block_table().T, BF), res_edge, res_mid)
 
 
 def swapped(sibling, neighbour):
@@ -615,11 +611,11 @@
     mid, vis, res_mid, out_mid = km(
         arrived, there, phases, edge, taps, table, live, obs, wt, back, *edges
     )
-    res, outgoing = kb(
-        taps, edge, mid, vis, sibling, neighbour, back, table, phases, res_mid, out_mid
+    res_edge, outgoing = kb(
+        taps, edge, mid, vis, sibling, neighbour, back, table, phases, out_mid
     )
     returned = lax.all_to_all(outgoing, "facet", split_axis=0, concat_axis=0, tiled=True)
-    dirty = k3(offsets, returned)
+    res, dirty = k3(offsets, returned, res_edge, res_mid)
     return (res[None], dirty)
 
 

time: 62.4 us -> 62.1 us (level)
  transfers between devices with their start and end apart: 5 -> 5, of which waited for: 2 -> 2; matrix products, arithmetic and copies ran while one was open for 0% -> 0% of each run, Pallas kernels for 5% -> 6%
where the time goes in v10:
time: 62.1 us; the launch traced here: 61.1 us
  blocking collectives  23 us (37%)
  waiting for transfers between devices  15.1 us (24%)
  starting transfers between devices  12.6 us (20%)
  Pallas kernels  8.24 us (13%)
  between operations  1.46 us (2%)
  local copies, waits for them, and re-layouts  0.67 us (1%)
    all_to_all x1, blocking collectives, local(): lax.all_to_all(outgoing, 'facet', split_axis=0, concat_axis=0, tiled=True)  23 us
    all_to_all x1, waiting for transfers between devices, local(): lax.all_to_all(out, 'facet', split_axis=0, concat_axis=0, tiled=True)  13.8 us
    all_to_all x1, starting transfers between devices, local(): lax.all_to_all(out, 'facet', split_axis=0, concat_axis=0, tiled=True)  11.3 us
    pallas_call x1, Pallas kernels, k1(): pl.pallas_call(k1_body, out_shape=jax.ShapeDtypeStruct((NF, CB, 2 * XC),...  2.41 us
    pallas_call x1, Pallas kernels, kt(): pl.pallas_call(kt_body, out_shape=(jax.ShapeDtypeStruct((SG, VM), BF), ja...  1.85 us
    pallas_call x1, Pallas kernels, k3(): pl.pallas_call(k3_body, out_shape=(jax.ShapeDtypeStruct((2, CB, VM), F32)...  1.64 us
    ppermute x2, waiting for transfers between devices, swapped(): lax.ppermute(neighbour, 'uv', far)  1.37 us
  transfers between devices with their start and end apart: 5, of which 2 were waited for; matrix products, arithmetic and copies ran while one was open for 0% of the time, Pallas kernels for 6%

profile of v10, /device:TPU:48, one launch (start us, length us, event | category | flops | bytes accessed | tf_op | source)
XLA Modules:
  0.0 61.1 jit_solution(15801584117555569638)
XLA Ops:
  0.6 2.4 %facet_to_slots.1 = bf16[32,32,256]{2,1,0:T(8,128)(2,1)} custom-call(s32[32]{0:T(128)} %offs_hbm.1, s32[32]{0:T(128)} %order_hbm.1, bf16[32,2048]{1,0:T(8,128)(2,1)} %sky_hbm.1), custom_call_target="tpu_custom_call" | custom-call | tf_op jit(solution)/shard_map/facet_to_slots/pallas_call | solution.py:222
  3.0 0.0 copy-start
  3.1 0.0 copy-start.1
  3.1 0.0 copy-start.3
  3.1 0.0 copy-start.9
  3.1 11.3 %all-to-all-start = ((bf16[32,32,256]{2,1,0:T(8,128)(2,1)}), bf16[32,32,256]{2,1,0:T(8,128)(2,1)S(1)}, u32[]{:S(2)}, u32[]{:S(2)}) async-start(bf16[32,32,256]{2,1,0:T(8,128)(2,1)} %facet_to_slots.1), calls=%async_computation | async-start | bytes 1048576 | tf_op jit(solution)/shard_map/all_to_all | solution.py:603
  15.1 0.0 copy-start.6
  15.1 0.0 copy-start.7
  15.2 0.6 copy-done.5
  15.8 0.0 copy-done.8
  15.8 1.9 %slot_tables.1 = (bf16[256,512]{1,0:T(8,128)(2,1)S(1)}, f32[2,32,128]{2,1,0:T(8,128)S(1)}, f32[1,512]{1,0:T(1,128)S(1)}, bf16[256,512]{1,0:T(8,128)(2,1)S(1)}, b...) custom-call(s32[32]{0:T(128)S(1)} %copy-done.6, ...), custom_call_target="tpu_custom_call" | custom-call | flops 4000000 | bytes 1000000 | tf_op jit(solution)/shard_map/slot_tables/pallas_call | solution.py:287
  17.6 0.1 collective-permute-start
  17.7 0.6 collective-permute-start.1
  18.3 13.8 %all-to-all-done.arr_ref = bf16[32,32,256]{2,1,0:T(8,128)(2,1)S(1)} async-done(((bf16[32,32,256]{2,1,0:T(8,128)(2,1)}), bf16[32,32,256]{2,1,0:T(8,128)(2,1)S(1)}, u32[]{:S(2)}, u32[]{:S(2)}) %all-to-all-start) | async-done | bytes 524320 | tf_op jit(solution)/shard_map/all_to_all | solution.py:603
  32.0 0.3 sum_edges.1
  32.4 0.1 collective-permute-start.2
  32.5 0.6 collective-permute-start.3
  33.0 1.2 %inner_columns.1 = (f32[16,512]{1,0:T(8,128)S(1)}, f32[3,32,512]{2,1,0:T(8,128)S(1)}, f32[2,16,512]{2,1,0:T(8,128)S(1)}, bf16[32,16,256]{2,1,0:T(8,128)(2,1)S(1)}) custom-call(bf16[32,32,256]{2,1,0:T(8,128)(2,1)S(1)} %all-to-all-done.arr_ref, bf16[256,512]{1,0:T(8,128)(2,1)S(1)} %get-tuple-element.24.w_ref, f32[2,32,128]{2,1,0:T(8,128)S(1)} %get-tuple-element.25.pho_ref, ...), custom_call_target="tpu_custom_call" | custom-call | flops 300000000 | bytes 2000000 | tf_op jit(solution)/shard_map/inner_columns/pallas_call | solution.py:423
  34.3 1.4 %collective-permute-done.3.neighbour_ref = bf16[8,512]{1,0:T(8,128)(2,1)S(1)} collective-permute-done((bf16[8,512]{1,0:T(8,128)(2,1)S(1)}, bf16[8,512]{1,0:T(8,128)(2,1)S(1)}, u32[]{:S(2)}, u32[]{:S(2)}) %collective-permute-start.3) | collective-permute-done | bytes 8224 | tf_op jit(solution)/shard_map/ppermute | solution.py:592
  35.6 0.8 %edge_columns.1 = (f32[2,2,8,512]{3,2,1,0:T(8,128)S(1)}, bf16[32,32,256]{2,1,0:T(8,128)(2,1)S(1)}) custom-call(f32[8,256]{1,0:T(8,128)S(1)} %get-tuple-element.23.taps_ref, f32[16,512]{1,0:T(8,128)S(1)} %get-tuple-element.26.edge_ref, f32[16,512]{1,0:T(8,128)S(1)} %get-tuple-element.32.mid_ref, f32[3,32,512]{2,1,0:T(8,128)S(1)} %get-tuple-element.33.vis_ref, ...), custom_call_target="tpu_custom_call" | custom-call | tf_op jit(solution)/shard_map/edge_columns/pallas_call | solution.py:491
  36.4 0.0 copy-start.2
  36.5 0.0 copy-start.4
  36.5 23.0 %all_to_all.10.bp_ref = bf16[32,32,256]{2,1,0:T(8,128)(2,1)S(1)} all-to-all(bf16[32,32,256]{2,1,0:T(8,128)(2,1)S(1)} %get-tuple-element.37), channel_id=1, replica_groups=mesh['facet'=32,'uv'=8] {'facet'}, dimensions={0} | all-to-all | bytes 1048576 | tf_op jit(solution)/shard_map/all_to_all | solution.py:617
  59.5 1.6 %slots_to_facet.1 = (f32[2,32,512]{2,1,0:T(8,128)}, f32[32,2048]{1,0:T(8,128)}) custom-call(s32[8,128]{1,0:T(8,128)S(1)} %get-tuple-element.22.offset_ref, bf16[32,32,256]{2,1,0:T(8,128)(2,1)S(1)} %all_to_all.10.bp_ref, f32[1,2048]{1,0:T(1,128)S(1)} %copy-done.4, bf16[256,256]{1,0:T(8,128)(2,1)S(1)} %copy-done.2, ...), custom_call_target="tpu_custom_call" | custom-call | tf_op jit(solution)/shard_map/slots_to_facet/pallas_call | solution.py:566
  (13 shorter events, 0.0 us)
Async XLA Ops:
  3.0 12.1 %copy-start = (bf16[1,2,32,512]{3,2,1,0:T(8,128)(2,1)S(1)}, bf16[1,2,32,512]{3,2,1,0:T(8,128)(2,1)}, u32[]{:S(2)}) copy-start(bf16[1,2,32,512]{3,2,1,0:T(8,128)(2,1)} %param.17) | copy-start | bytes 196612
  3.1 12.1 %copy-start.1 = (f32[1,32,512]{2,1,0:T(8,128)S(1)}, f32[1,32,512]{2,1,0:T(8,128)}, u32[]{:S(2)}) copy-start(f32[1,32,512]{2,1,0:T(8,128)} %param.18) | copy-start | bytes 196612
  3.1 12.1 %copy-start.3 = (f32[2,32,128]{2,1,0:T(8,128)S(1)}, f32[2,32,128]{2,1,0:T(8,128)}, u32[]{:S(2)}) copy-start(f32[2,32,128]{2,1,0:T(8,128)} %constant.6.clone.ph_ref) | copy-start | bytes 98308
  3.1 12.1 %copy-start.9 = (f32[7]{0:T(128)S(1)}, f32[7]{0:T(128)}, u32[]{:S(2)}) copy-start(f32[7]{0:T(128)} %ck_ref.1) | copy-start | bytes 88
  3.1 29.0 %all-to-all-start = ((bf16[32,32,256]{2,1,0:T(8,128)(2,1)}), bf16[32,32,256]{2,1,0:T(8,128)(2,1)S(1)}, u32[]{:S(2)}, u32[]{:S(2)}) async-start(bf16[32,32,256]{2,1,0:T(8,128)(2,1)} %facet_to_slots.1), calls=%async_computation | async-start | bytes 1048576 | tf_op jit(solution)/shard_map/all_to_all | solution.py:603
  15.1 0.7 %copy-start.5 = (s32[1,512]{1,0:T(1,128)S(1)}, s32[1,512]{1,0:T(1,128)}, u32[]{:S(2)}) copy-start(s32[1,512]{1,0:T(1,128)} %cell_ref.1) | copy-start | bytes 6148
  15.1 0.7 %copy-start.6 = (s32[32]{0:T(128)S(1)}, s32[32]{0:T(128)}, u32[]{:S(2)}) copy-start(s32[32]{0:T(128)} %offs_hbm.1) | copy-start | bytes 388
  15.1 0.7 %copy-start.7 = (s32[32]{0:T(128)S(1)}, s32[32]{0:T(128)}, u32[]{:S(2)}) copy-start(s32[32]{0:T(128)} %order_hbm.1) | copy-start | bytes 388
  15.1 0.7 %copy-start.8 = (f32[7]{0:T(128)S(1)}, f32[7]{0:T(128)}, u32[]{:S(2)}) copy-start(f32[7]{0:T(128)} %rk_ref.1) | copy-start | bytes 88
  17.6 15.4 %collective-permute-start = (bf16[8,1536]{1,0:T(8,128)(2,1)S(1)}, bf16[8,1536]{1,0:T(8,128)(2,1)S(1)}, u32[]{:S(2)}, u32[]{:S(2)}) collective-permute-start(bf16[8,1536]{1,0:T(8,128)(2,1)S(1)} %get-tuple-element.30), channel_id=1, source_target_pairs={{0,1},{1,0},{2,3},{3,2},{4,5},{5,4},{6,7},{7,6},{8,9},{9,8},{10,11... | collective-permute-start | bytes 73736 | tf_op jit(solution)/shard_map/ppermute | solution.py:592
  17.7 15.3 %collective-permute-start.1 = (bf16[8,1536]{1,0:T(8,128)(2,1)S(1)}, bf16[8,1536]{1,0:T(8,128)(2,1)S(1)}, u32[]{:S(2)}, u32[]{:S(2)}) collective-permute-start(bf16[8,1536]{1,0:T(8,128)(2,1)S(1)} %get-tuple-element.31), channel_id=1, source_target_pairs={{0,7},{1,2},{2,1},{3,4},{4,3},{5,6},{6,5},{7,0},{8,15},{9,10},{10,... | collective-permute-start | bytes 73736 | tf_op jit(solution)/shard_map/ppermute | solution.py:592
  32.4 1.9 %collective-permute-start.2 = (bf16[8,512]{1,0:T(8,128)(2,1)S(1)}, bf16[8,512]{1,0:T(8,128)(2,1)S(1)}, u32[]{:S(2)}, u32[]{:S(2)}) collective-permute-start(bf16[8,512]{1,0:T(8,128)(2,1)S(1)} %get-tuple-element.34), channel_id=1, source_target_pairs={{0,1},{1,0},{2,3},{3,2},{4,5},{5,4},{6,7},{7,6},{8,9},{9,8},{10,11... | collective-permute-start | bytes 24584 | tf_op jit(solution)/shard_map/ppermute | solution.py:592
  32.5 3.2 %collective-permute-start.3 = (bf16[8,512]{1,0:T(8,128)(2,1)S(1)}, bf16[8,512]{1,0:T(8,128)(2,1)S(1)}, u32[]{:S(2)}, u32[]{:S(2)}) collective-permute-start(bf16[8,512]{1,0:T(8,128)(2,1)S(1)} %get-tuple-element.35), channel_id=1, source_target_pairs={{0,7},{1,2},{2,1},{3,4},{4,3},{5,6},{6,5},{7,0},{8,15},{9,10},{10,... | collective-permute-start | bytes 24584 | tf_op jit(solution)/shard_map/ppermute | solution.py:592
  36.4 23.0 %copy-start.2 = (bf16[256,256]{1,0:T(8,128)(2,1)S(1)}, bf16[256,256]{1,0:T(8,128)(2,1)}, u32[]{:S(2)}) copy-start(bf16[256,256]{1,0:T(8,128)(2,1)} %constant.7.clone.tab_ref) | copy-start | bytes 393220
  36.5 23.0 %copy-start.4 = (f32[1,2048]{1,0:T(1,128)S(1)}, f32[1,2048]{1,0:T(1,128)}, u32[]{:S(2)}) copy-start(f32[1,2048]{1,0:T(1,128)} %constant.8.clone.win_ref) | copy-start | bytes 24580

commit v11 on v10

--- a/solution.py
+++ b/solution.py
@@ -152,23 +152,29 @@
     out_hbm, offs_ref, order_ref, tw_ref, lhs_ref, u_ref, nat_ref, sky_ref, win_ref, tab_ref,
     out_ref, sky_sem, small_sem, out_sem,
 ):
-    halves = [
-        pltpu.make_async_copy(
-            sky_hbm.at[pl.ds(16 * g, 16), :], sky_ref.at[pl.ds(16 * g, 16), :], sky_sem.at[g]
-        )
+    quarters = [
+        [
+            pltpu.make_async_copy(
+                sky_hbm.at[pl.ds(16 * g, 16), pl.ds(512 * q, 512)],
+                sky_ref.at[pl.ds(16 * g, 16), pl.ds(512 * q, 512)],
+                sky_sem.at[4 * g + q],
+            )
+            for q in range(4)
+        ]
         for g in range(2)
     ]
     small = [
         pltpu.make_async_copy(offs_hbm, offs_ref, small_sem.at[0]),
         pltpu.make_async_copy(order_hbm, order_ref, small_sem.at[1]),
     ]
-    for copy in halves + small:
+    for copy in quarters[0] + quarters[1] + small:
         copy.start()
     tw_ref[0], tw_ref[1] = twiddles(lax.axis_index("facet"))
     make_window(win_ref)
     make_block_table(tab_ref)
     for g in range(2):
-        halves[g].wait()
+        for copy in quarters[g]:
+            copy.wait()
         rows = slice(16 * g, 16 * (g + 1))
         x = []
         for b in range(16):
@@ -235,7 +241,7 @@
             pltpu.VMEM((8, FR), F32),
             pltpu.VMEM((256, 256), BF),
             pltpu.VMEM((NF, CB, 256), BF),
-            pltpu.SemaphoreType.DMA((2,)),
+            pltpu.SemaphoreType.DMA((8,)),
             pltpu.SemaphoreType.DMA((2,)),
             pltpu.SemaphoreType.DMA((4,)),
         ],
@@ -529,15 +535,18 @@
         for p in range(2):
             cols = slice(128 * p, 128 * (p + 1))
             x = bp_ref[i, :, cols].astype(F32)
-            nat_ref[b, :, cols] += jnp.where(keep, x, 0.0)
-            nat_ref[b + 1, :, cols] += jnp.where(keep, 0.0, x)
-    nat_ref[0] += nat_ref[16]
+            n = i % 2
+            nat_ref[n, b, :, cols] += jnp.where(keep, x, 0.0)
+            nat_ref[n, b + 1, :, cols] += jnp.where(keep, 0.0, x)
+    nat_ref[0, 0] += nat_ref[0, 16] + nat_ref[1, 16]
 
     for g in range(2):
         rows = slice(16 * g, 16 * (g + 1))
         for p in range(2):
             cols = slice(128 * p, 128 * (p + 1))
-            x = swap_index([nat_ref[b, rows, cols].astype(BF) for b in range(16)])
+            x = swap_index(
+                [(nat_ref[0, b, rows, cols] + nat_ref[1, b, rows, cols]).astype(BF) for b in range(16)]
+            )
             for m in range(16):
                 lhs_ref[m, rows, cols] = x[m]
     v = jnp.dot(lhs_ref[...].reshape(16 * CB, 256), tab_ref[...], preferred_element_type=F32)
@@ -572,7 +581,7 @@
         in_specs=[VMEM] * 6,
         out_specs=(ANY, ANY),
         scratch_shapes=[
-            pltpu.VMEM((17, CB, 256), F32),
+            pltpu.VMEM((2, 17, CB, 256), F32),
             pltpu.VMEM((2, 16, 128), F32),
             pltpu.VMEM((16, CB, 256), BF),
             pltpu.VMEM((16, CB, 256), F32),

time: 62.1 us -> 62.1 us (level)
  no operation moved by 1% of the time
where the time goes in v11:
time: 62.1 us; the launch traced here: 61.1 us
  blocking collectives  23 us (37%)
  waiting for transfers between devices  15.1 us (24%)
  starting transfers between devices  12.6 us (20%)
  Pallas kernels  8.25 us (13%)
  between operations  1.46 us (2%)
  local copies, waits for them, and re-layouts  0.67 us (1%)
    all_to_all x1, blocking collectives, local(): lax.all_to_all(outgoing, 'facet', split_axis=0, concat_axis=0, tiled=True)  23 us
    all_to_all x1, waiting for transfers between devices, local(): lax.all_to_all(out, 'facet', split_axis=0, concat_axis=0, tiled=True)  13.8 us
    all_to_all x1, starting transfers between devices, local(): lax.all_to_all(out, 'facet', split_axis=0, concat_axis=0, tiled=True)  11.3 us
    pallas_call x1, Pallas kernels, k1(): pl.pallas_call(k1_body, out_shape=jax.ShapeDtypeStruct((NF, CB, 2 * XC),...  2.4 us
    pallas_call x1, Pallas kernels, kt(): pl.pallas_call(kt_body, out_shape=(jax.ShapeDtypeStruct((SG, VM), BF), ja...  1.85 us
    pallas_call x1, Pallas kernels, k3(): pl.pallas_call(k3_body, out_shape=(jax.ShapeDtypeStruct((2, CB, VM), F32)...  1.65 us
    ppermute x2, waiting for transfers between devices, swapped(): lax.ppermute(neighbour, 'uv', far)  1.37 us
  transfers between devices with their start and end apart: 5, of which 2 were waited for; matrix products, arithmetic and copies ran while one was open for 0% of the time, Pallas kernels for 6%

profile of v11, /device:TPU:48, one launch (start us, length us, event | category | flops | bytes accessed | tf_op | source)
XLA Modules:
  0.0 61.1 jit_solution(3786099910040645699)
XLA Ops:
  0.6 2.4 %facet_to_slots.1 = bf16[32,32,256]{2,1,0:T(8,128)(2,1)} custom-call(s32[32]{0:T(128)} %offs_hbm.1, s32[32]{0:T(128)} %order_hbm.1, bf16[32,2048]{1,0:T(8,128)(2,1)} %sky_hbm.1), custom_call_target="tpu_custom_call" | custom-call | tf_op jit(solution)/shard_map/facet_to_slots/pallas_call | solution.py:228
  3.0 0.0 copy-start
  3.0 0.0 copy-start.1
  3.1 0.0 copy-start.3
  3.1 0.0 copy-start.9
  3.1 11.3 %all-to-all-start = ((bf16[32,32,256]{2,1,0:T(8,128)(2,1)}), bf16[32,32,256]{2,1,0:T(8,128)(2,1)S(1)}, u32[]{:S(2)}, u32[]{:S(2)}) async-start(bf16[32,32,256]{2,1,0:T(8,128)(2,1)} %facet_to_slots.1), calls=%async_computation | async-start | bytes 1048576 | tf_op jit(solution)/shard_map/all_to_all | solution.py:612
  15.1 0.0 copy-start.5
  15.1 0.0 copy-start.8
  15.2 0.6 copy-done.5
  15.8 0.0 copy-done.8
  15.8 1.9 %slot_tables.1 = (bf16[256,512]{1,0:T(8,128)(2,1)S(1)}, f32[2,32,128]{2,1,0:T(8,128)S(1)}, f32[1,512]{1,0:T(1,128)S(1)}, bf16[256,512]{1,0:T(8,128)(2,1)S(1)}, b...) custom-call(s32[32]{0:T(128)S(1)} %copy-done.6, ...), custom_call_target="tpu_custom_call" | custom-call | flops 4000000 | bytes 1000000 | tf_op jit(solution)/shard_map/slot_tables/pallas_call | solution.py:293
  17.6 0.1 collective-permute-start
  17.7 0.6 collective-permute-start.1
  18.3 13.8 %all-to-all-done.arr_ref = bf16[32,32,256]{2,1,0:T(8,128)(2,1)S(1)} async-done(((bf16[32,32,256]{2,1,0:T(8,128)(2,1)}), bf16[32,32,256]{2,1,0:T(8,128)(2,1)S(1)}, u32[]{:S(2)}, u32[]{:S(2)}) %all-to-all-start) | async-done | bytes 524320 | tf_op jit(solution)/shard_map/all_to_all | solution.py:612
  32.0 0.3 sum_edges.1
  32.3 0.1 collective-permute-start.2
  32.4 0.5 collective-permute-start.3
  33.0 1.2 %inner_columns.1 = (f32[16,512]{1,0:T(8,128)S(1)}, f32[3,32,512]{2,1,0:T(8,128)S(1)}, f32[2,16,512]{2,1,0:T(8,128)S(1)}, bf16[32,16,256]{2,1,0:T(8,128)(2,1)S(1)}) custom-call(bf16[32,32,256]{2,1,0:T(8,128)(2,1)S(1)} %all-to-all-done.arr_ref, bf16[256,512]{1,0:T(8,128)(2,1)S(1)} %get-tuple-element.24.w_ref, f32[2,32,128]{2,1,0:T(8,128)S(1)} %get-tuple-element.25.pho_ref, ...), custom_call_target="tpu_custom_call" | custom-call | flops 300000000 | bytes 2000000 | tf_op jit(solution)/shard_map/inner_columns/pallas_call | solution.py:429
  34.2 1.4 %collective-permute-done.3.neighbour_ref = bf16[8,512]{1,0:T(8,128)(2,1)S(1)} collective-permute-done((bf16[8,512]{1,0:T(8,128)(2,1)S(1)}, bf16[8,512]{1,0:T(8,128)(2,1)S(1)}, u32[]{:S(2)}, u32[]{:S(2)}) %collective-permute-start.3) | collective-permute-done | bytes 8224 | tf_op jit(solution)/shard_map/ppermute | solution.py:601
  35.6 0.8 %edge_columns.1 = (f32[2,2,8,512]{3,2,1,0:T(8,128)S(1)}, bf16[32,32,256]{2,1,0:T(8,128)(2,1)S(1)}) custom-call(f32[8,256]{1,0:T(8,128)S(1)} %get-tuple-element.23.taps_ref, f32[16,512]{1,0:T(8,128)S(1)} %get-tuple-element.26.edge_ref, f32[16,512]{1,0:T(8,128)S(1)} %get-tuple-element.32.mid_ref, f32[3,32,512]{2,1,0:T(8,128)S(1)} %get-tuple-element.33.vis_ref, ...), custom_call_target="tpu_custom_call" | custom-call | tf_op jit(solution)/shard_map/edge_columns/pallas_call | solution.py:497
  36.4 0.0 copy-start.2
  36.5 0.0 copy-start.4
  36.5 23.0 %all_to_all.10.bp_ref = bf16[32,32,256]{2,1,0:T(8,128)(2,1)S(1)} all-to-all(bf16[32,32,256]{2,1,0:T(8,128)(2,1)S(1)} %get-tuple-element.37), channel_id=1, replica_groups=mesh['facet'=32,'uv'=8] {'facet'}, dimensions={0} | all-to-all | bytes 1048576 | tf_op jit(solution)/shard_map/all_to_all | solution.py:626
  59.5 1.7 %slots_to_facet.1 = (f32[2,32,512]{2,1,0:T(8,128)}, f32[32,2048]{1,0:T(8,128)}) custom-call(s32[8,128]{1,0:T(8,128)S(1)} %get-tuple-element.22.offset_ref, bf16[32,32,256]{2,1,0:T(8,128)(2,1)S(1)} %all_to_all.10.bp_ref, f32[1,2048]{1,0:T(1,128)S(1)} %copy-done.4, bf16[256,256]{1,0:T(8,128)(2,1)S(1)} %copy-done.2, ...), custom_call_target="tpu_custom_call" | custom-call | tf_op jit(solution)/shard_map/slots_to_facet/pallas_call | solution.py:575
  (13 shorter events, 0.0 us)
Async XLA Ops:
  3.0 12.1 %copy-start = (bf16[1,2,32,512]{3,2,1,0:T(8,128)(2,1)S(1)}, bf16[1,2,32,512]{3,2,1,0:T(8,128)(2,1)}, u32[]{:S(2)}) copy-start(bf16[1,2,32,512]{3,2,1,0:T(8,128)(2,1)} %param.17) | copy-start | bytes 196612
  3.0 12.1 %copy-start.1 = (f32[1,32,512]{2,1,0:T(8,128)S(1)}, f32[1,32,512]{2,1,0:T(8,128)}, u32[]{:S(2)}) copy-start(f32[1,32,512]{2,1,0:T(8,128)} %param.18) | copy-start | bytes 196612
  3.1 12.1 %copy-start.3 = (f32[2,32,128]{2,1,0:T(8,128)S(1)}, f32[2,32,128]{2,1,0:T(8,128)}, u32[]{:S(2)}) copy-start(f32[2,32,128]{2,1,0:T(8,128)} %constant.6.clone.ph_ref) | copy-start | bytes 98308
  3.1 12.1 %copy-start.9 = (f32[7]{0:T(128)S(1)}, f32[7]{0:T(128)}, u32[]{:S(2)}) copy-start(f32[7]{0:T(128)} %ck_ref.1) | copy-start | bytes 88
  3.1 29.0 %all-to-all-start = ((bf16[32,32,256]{2,1,0:T(8,128)(2,1)}), bf16[32,32,256]{2,1,0:T(8,128)(2,1)S(1)}, u32[]{:S(2)}, u32[]{:S(2)}) async-start(bf16[32,32,256]{2,1,0:T(8,128)(2,1)} %facet_to_slots.1), calls=%async_computation | async-start | bytes 1048576 | tf_op jit(solution)/shard_map/all_to_all | solution.py:612
  15.1 0.7 %copy-start.5 = (s32[1,512]{1,0:T(1,128)S(1)}, s32[1,512]{1,0:T(1,128)}, u32[]{:S(2)}) copy-start(s32[1,512]{1,0:T(1,128)} %cell_ref.1) | copy-start | bytes 6148
  15.1 0.7 %copy-start.6 = (s32[32]{0:T(128)S(1)}, s32[32]{0:T(128)}, u32[]{:S(2)}) copy-start(s32[32]{0:T(128)} %offs_hbm.1) | copy-start | bytes 388
  15.1 0.7 %copy-start.7 = (s32[32]{0:T(128)S(1)}, s32[32]{0:T(128)}, u32[]{:S(2)}) copy-start(s32[32]{0:T(128)} %order_hbm.1) | copy-start | bytes 388
  15.1 0.7 %copy-start.8 = (f32[7]{0:T(128)S(1)}, f32[7]{0:T(128)}, u32[]{:S(2)}) copy-start(f32[7]{0:T(128)} %rk_ref.1) | copy-start | bytes 88
  17.6 15.4 %collective-permute-start = (bf16[8,1536]{1,0:T(8,128)(2,1)S(1)}, bf16[8,1536]{1,0:T(8,128)(2,1)S(1)}, u32[]{:S(2)}, u32[]{:S(2)}) collective-permute-start(bf16[8,1536]{1,0:T(8,128)(2,1)S(1)} %get-tuple-element.30), channel_id=1, source_target_pairs={{0,1},{1,0},{2,3},{3,2},{4,5},{5,4},{6,7},{7,6},{8,9},{9,8},{10,11... | collective-permute-start | bytes 73736 | tf_op jit(solution)/shard_map/ppermute | solution.py:601
  17.7 15.3 %collective-permute-start.1 = (bf16[8,1536]{1,0:T(8,128)(2,1)S(1)}, bf16[8,1536]{1,0:T(8,128)(2,1)S(1)}, u32[]{:S(2)}, u32[]{:S(2)}) collective-permute-start(bf16[8,1536]{1,0:T(8,128)(2,1)S(1)} %get-tuple-element.31), channel_id=1, source_target_pairs={{0,7},{1,2},{2,1},{3,4},{4,3},{5,6},{6,5},{7,0},{8,15},{9,10},{10,... | collective-permute-start | bytes 73736 | tf_op jit(solution)/shard_map/ppermute | solution.py:601
  32.3 1.9 %collective-permute-start.2 = (bf16[8,512]{1,0:T(8,128)(2,1)S(1)}, bf16[8,512]{1,0:T(8,128)(2,1)S(1)}, u32[]{:S(2)}, u32[]{:S(2)}) collective-permute-start(bf16[8,512]{1,0:T(8,128)(2,1)S(1)} %get-tuple-element.34), channel_id=1, source_target_pairs={{0,1},{1,0},{2,3},{3,2},{4,5},{5,4},{6,7},{7,6},{8,9},{9,8},{10,11... | collective-permute-start | bytes 24584 | tf_op jit(solution)/shard_map/ppermute | solution.py:601
  32.4 3.2 %collective-permute-start.3 = (bf16[8,512]{1,0:T(8,128)(2,1)S(1)}, bf16[8,512]{1,0:T(8,128)(2,1)S(1)}, u32[]{:S(2)}, u32[]{:S(2)}) collective-permute-start(bf16[8,512]{1,0:T(8,128)(2,1)S(1)} %get-tuple-element.35), channel_id=1, source_target_pairs={{0,7},{1,2},{2,1},{3,4},{4,3},{5,6},{6,5},{7,0},{8,15},{9,10},{10,... | collective-permute-start | bytes 24584 | tf_op jit(solution)/shard_map/ppermute | solution.py:601
  36.4 23.0 %copy-start.2 = (bf16[256,256]{1,0:T(8,128)(2,1)S(1)}, bf16[256,256]{1,0:T(8,128)(2,1)}, u32[]{:S(2)}) copy-start(bf16[256,256]{1,0:T(8,128)(2,1)} %constant.7.clone.tab_ref) | copy-start | bytes 393220
  36.5 23.0 %copy-start.4 = (f32[1,2048]{1,0:T(1,128)S(1)}, f32[1,2048]{1,0:T(1,128)}, u32[]{:S(2)}) copy-start(f32[1,2048]{1,0:T(1,128)} %constant.8.clone.win_ref) | copy-start | bytes 24580
